TPU v7x, 256 devices: a whole 4x4x8 slice. The times are simulated.
256 devices in a mesh: sub: 64 (over z, y, core), grp: 4 (over x).
Axes of the slice: x: 4, y: 4, z: 8, core: 2. Of those that a mesh axis runs over, the one named last changes fastest.
Arguments:
- load_source: bfloat16 [4, 64, 32, 1536], P('grp', 'sub'), may hold values from -18 to 18
- schur_diag: float32 [4, 64, 1536], P('grp', 'sub'), may hold values from 0.3 to 3
- schur_factor: bfloat16 [4, 64, 1536, 1536], P('grp', 'sub'), may hold values from -0.15625 to 0.15625
- dir_diag: float32 [4, 64, 1536], P('grp', 'sub'), may hold values from 0.3 to 3
- dir_factor: bfloat16 [4, 64, 1536, 1536], P('grp', 'sub'), may hold values from -0.15625 to 0.15625
- corner_map: bfloat16 [4, 64, 24, 1536], P('grp', 'sub'), may hold values from -0.3125 to 0.3125
- corner_row: int32 [4, 64, 24], P('grp', 'sub'), may hold values from 0 to 2047
- coarse_factor: bfloat16 [2048, 2048], P(('sub', 'grp')), may hold values from -0.125 to 0.125
- slot_table: int32 [4, 64, 6, 256], P('grp', 'sub'), may hold values from 0 to 1536, as said below
Outputs:
- multipliers: float32 [4, 64, 32, 1536], P('grp', 'sub')
- residual: float32 [4, 64, 32, 1536], P('grp', 'sub')
Inputs may be any that keep to these rules, and one draw needn't show every extreme that they name: slot_table[g, p, b, c] is the local slot of the c-th DOF that subdomain p shares with subdomain (p + k) mod 64 of group g, k = 1, 2, 5, -1, -2, -5 for b = 0 to 5; the neighbour lists the same DOF at the same c in its block (b + 3) mod 6; each pair shares 256 // 4 to 256 DOFs, listed first, and the rest of a block holds 1536; no slot appears twice in one subdomain; in every group some pair shares exactly 256.
All inputs are finite; a program needn't handle non-finite values.
Results may differ from a plain program's by a relative error of at most 0.01.
Values may be sent and summed in bfloat16 or wider, within the bound.
No kernel may reach another device: no remote copies, remote signals or barrier semaphores. Data moves between devices by JAX's collectives and lax.ppermute only.
A program may use at most 64 MiB of HBM per device.

v0:
```python
import jax
import jax.numpy as jnp
from jax import lax
from jax.experimental import pallas as pl
from jax.experimental.pallas import tpu as pltpu
from jax.sharding import PartitionSpec as P

OFFSETS = (1, 2, 5, -1, -2, -5)
BLOCKS = len(OFFSETS)
F32 = jnp.float32
BF16 = jnp.bfloat16
LANES = 128


def dot_nn(a, b):
    return jnp.dot(a, b, preferred_element_type=F32)


def dot_nt(a, b):
    return lax.dot_general(a, b, (((1,), (1,)), ((), ())), preferred_element_type=F32)


def dot_tn(a, b):
    return lax.dot_general(a, b, (((0,), (0,)), ((), ())), preferred_element_type=F32)


def column_to_row(column):
    n = column.shape[0]
    same = lax.broadcasted_iota(jnp.int32, (n, n), 0) == lax.broadcasted_iota(jnp.int32, (n, n), 1)
    return jnp.sum(jnp.where(same, column, 0.0), axis=0, keepdims=True)


def row_to_column(row):
    n = row.shape[1]
    same = lax.broadcasted_iota(jnp.int32, (n, n), 0) == lax.broadcasted_iota(jnp.int32, (n, n), 1)
    return jnp.sum(jnp.where(same, row, 0.0), axis=1, keepdims=True)


def three_parts(value):
    first = value.astype(BF16).astype(F32)
    rest = value - first
    second = rest.astype(BF16).astype(F32)
    third = (rest - second).astype(BF16).astype(F32)
    return [first, second, third]


def fold_rows(rows):
    n = rows.shape[0] // 4
    return jnp.concatenate([rows[n * i : n * i + n] for i in range(4)], axis=1)


def unfold_rows(tile):
    n = tile.shape[1] // 4
    return jnp.concatenate([tile[:, n * i : n * i + n] for i in range(4)], axis=0)


def call(body, outs, cost, *args):
    in_vmem = pl.BlockSpec(memory_space=pltpu.VMEM)
    return pl.pallas_call(
        body,
        out_shape=[jax.ShapeDtypeStruct(shape, dtype) for shape, dtype in outs],
        in_specs=[in_vmem] * len(args),
        out_specs=[in_vmem] * len(outs),
        compiler_params=pltpu.CompilerParams(vmem_limit_bytes=40 * 1024 * 1024),
        cost_estimate=pl.CostEstimate(flops=cost, bytes_accessed=cost // 64, transcendentals=0),
    )(*args)


def store_blocks(refs, values, slots_ref):
    cap = refs[0].shape[1]
    for b in range(BLOCKS):
        refs[b][...] = dot_nn(values, slots_ref[:, b * cap : (b + 1) * cap]).astype(BF16)


def first_exchange_body(table_ref, source_ref, slots_ref, *block_refs):
    interface, total = slots_ref.shape
    cap = total // BLOCKS
    rows = lax.broadcasted_iota(jnp.int32, (interface, cap), 0)
    source = source_ref[...]
    for b in range(BLOCKS):
        named = rows == table_ref[0:1, b * cap : (b + 1) * cap]
        block = jnp.where(named, 1.0, 0.0).astype(BF16)
        slots_ref[:, b * cap : (b + 1) * cap] = block
        block_refs[b][...] = dot_nn(source, block).astype(BF16)


def dirichlet_body(*refs):
    incoming = jnp.concatenate([ref[...] for ref in refs[:BLOCKS]], axis=1)
    source_ref, diag_ref, slots_ref, factor_ref = refs[BLOCKS : BLOCKS + 4]
    residual_ref, out_ref, live_ref, rho_ref, *block_refs = refs[BLOCKS + 4 :]
    cases = incoming.shape[0]
    ones = jnp.ones((16, incoming.shape[1]), BF16)
    spread = dot_nt(jnp.concatenate([incoming, ones], axis=0), slots_ref[...])
    live = spread[cases : cases + 8]
    residual = live[0:1] * (source_ref[...].astype(F32) - spread[:cases])
    factor = factor_ref[...]
    middle = dot_nn(residual.astype(BF16), factor).astype(BF16)
    out = (0.5 * (diag_ref[...] * residual + dot_nt(middle, factor))).astype(BF16)
    store_blocks(block_refs, out, slots_ref)
    live_ref[...] = live
    residual_ref[...] = residual
    out_ref[...] = out
    rho = column_to_row(jnp.sum(residual * out.astype(F32), axis=1, keepdims=True))
    rho_ref[...] = jnp.broadcast_to(rho, rho_ref.shape)


def schur_first_body(*refs):
    incoming = jnp.concatenate([ref[...] for ref in refs[:BLOCKS]], axis=1)
    out_ref, live_ref, diag_ref, slots_ref, factor_ref, corner_ref, rho_ref = refs[
        BLOCKS : BLOCKS + 7
    ]
    direction_ref, middle_ref, send_ref = refs[BLOCKS + 7 :]
    received = dot_nt(incoming, slots_ref[...])
    direction = 0.5 * (live_ref[0:1] * (out_ref[...].astype(F32) - received))
    direction_ref[...] = direction
    operand = direction.astype(BF16)
    wide = dot_nn(operand, factor_ref[...])
    middle = wide.astype(BF16)
    middle_ref[...] = middle
    curve = jnp.sum(diag_ref[...] * direction * direction, axis=1, keepdims=True)
    curve = curve + jnp.sum(wide * middle.astype(F32), axis=1, keepdims=True)
    corner_in = dot_nt(corner_ref[...], operand)
    zero = jnp.zeros((2, corner_in.shape[1]), F32)
    scalars = three_parts(rho_ref[0:1]) + three_parts(column_to_row(curve)) + [zero]
    tile = fold_rows(jnp.concatenate([corner_in] + scalars, axis=0)).astype(BF16)
    send_ref[...] = jnp.broadcast_to(tile[None], send_ref.shape)


def schur_second_body(direction_ref, middle_ref, diag_ref, factor_ref, local_ref):
    back = dot_nt(middle_ref[...], factor_ref[...])
    local_ref[...] = diag_ref[...] * direction_ref[...] + back


def deal_columns_body(rows_ref, index_ref, send_ref):
    members, depth, lanes = rows_ref.shape
    group = lax.broadcasted_iota(jnp.int32, (depth, lanes), 1) // 32 % 4
    rows = [rows_ref[a].astype(F32) for a in range(members)]
    index = index_ref[...]
    for t in range(4):
        dealt = jnp.zeros((depth, lanes), F32)
        for a in range(members):
            shift = (32 * (a - t)) % lanes
            moved = pltpu.roll(rows[a], shift, 1) if shift else rows[a]
            dealt = jnp.where(group == a, moved, dealt)
        for quad in range(lanes // LANES):
            send_ref[4 * quad + t, :, :LANES] = dealt[:, quad * LANES : (quad + 1) * LANES].astype(
                BF16
            )
    for other in range(send_ref.shape[0]):
        send_ref[other, :, LANES:] = index


def pick_rows_body(dealt_ref, picked_ref):
    count, depth, _ = dealt_ref.shape
    dealt = dealt_ref[...].astype(F32)
    columns = dealt[:, :, :LANES].reshape(count * depth, LANES).astype(BF16)
    index = dealt[:, :, LANES:].reshape(count * depth, LANES)
    size = count * depth
    place = lax.broadcasted_iota(jnp.int32, (size, size), 1).astype(F32)
    lane_group = (lax.broadcasted_iota(jnp.int32, (size, LANES), 1) // 32).astype(F32)
    near = lax.broadcasted_iota(jnp.int32, (LANES, LANES), 0)
    far = lax.broadcasted_iota(jnp.int32, (LANES, LANES), 1)
    total = jnp.zeros((size, LANES), F32)
    for q in range(3):
        high = index[:, 3 * q : 3 * q + 1] * 8.0 + index[:, 3 * q + 1 : 3 * q + 2]
        onehot = jnp.where(place == high, 1.0, 0.0).astype(BF16)
        rows = dot_nn(onehot, columns)
        rows = jnp.where(lane_group == index[:, 3 * q + 2 : 3 * q + 3], rows, 0.0).astype(BF16)
        fold = jnp.where((near % 32 == far % 32) & (far // 32 == q), 1.0, 0.0).astype(BF16)
        total = total + dot_nn(rows, fold)
    picked_ref[...] = total.astype(BF16)


def coarse_first_body(corner_ref, picked_ref, send_ref):
    count, depth, lanes = corner_ref.shape
    corner = corner_ref[...].astype(F32)
    products = dot_tn(picked_ref[...], corner.reshape(count * depth, lanes).astype(BF16))
    middle = products[:32, :32]
    for q in range(1, 3):
        middle = middle + products[32 * q : 32 * q + 32, 32 * q : 32 * q + 32]
    tile = jnp.concatenate([fold_rows(middle), jnp.sum(corner, axis=0)], axis=0)
    send_ref[...] = jnp.broadcast_to(tile[None], send_ref.shape)


def coarse_second_body(parts_ref, picked_ref, send_ref, totals_ref):
    parts = parts_ref[...]
    total = parts[0]
    for member in range(1, parts.shape[0]):
        total = total + parts[member]
    middle = unfold_rows(total[:8])
    rounded = middle.astype(BF16)
    square = jnp.sum(middle * rounded.astype(F32), axis=0, keepdims=True)
    wide = jnp.concatenate([middle] * 4, axis=1)
    wide = jnp.concatenate([wide] * 4, axis=0)
    near = lax.broadcasted_iota(jnp.int32, wide.shape, 0) // 32
    far = lax.broadcasted_iota(jnp.int32, wide.shape, 1) // 32
    diagonal = jnp.where(near == far, wide, 0.0).astype(BF16)
    out = dot_nn(picked_ref[...], diagonal)
    zero = jnp.zeros((5, 96 // 3), F32)
    scalars = jnp.concatenate(three_parts(square) + [zero], axis=0)
    extra = jnp.concatenate([jnp.zeros((8, 96), F32), scalars], axis=1)
    send_ref[...] = (out.reshape(send_ref.shape) + extra[None]).astype(BF16)
    totals_ref[...] = total[8:16]


def schur_last_body(coarse_ref, totals_ref, local_ref, corner_ref, slots_ref, *out_refs):
    schur_ref, step_ref, *block_refs = out_refs
    summed = jnp.sum(coarse_ref[...].astype(F32), axis=0)
    rows = unfold_rows(summed)
    corners = corner_ref.shape[0]
    picked = rows[:corners].astype(BF16)
    schur = (local_ref[...] + dot_tn(picked, corner_ref[...])).astype(BF16)
    schur_ref[...] = schur
    store_blocks(block_refs, schur, slots_ref)
    square = jnp.sum(rows[corners : corners + 3], axis=0, keepdims=True)
    scalars = totals_ref[:, 96:]
    rho = jnp.sum(scalars[0:3], axis=0, keepdims=True)
    curve = 2.0 * (jnp.sum(scalars[3:6], axis=0, keepdims=True) + square)
    step = row_to_column(rho / curve)
    step_ref[...] = jnp.broadcast_to(step, step_ref.shape)


def update_body(*refs):
    incoming = jnp.concatenate([ref[...] for ref in refs[:BLOCKS]], axis=1)
    schur_ref, step_ref, live_ref, direction_ref, residual_ref, slots_ref = refs[
        BLOCKS : BLOCKS + 6
    ]
    multipliers_ref, new_residual_ref = refs[BLOCKS + 6 :]
    received = dot_nt(incoming, slots_ref[...])
    image = live_ref[0:1] * (schur_ref[...].astype(F32) - received)
    step = step_ref[:, 0:1]
    multipliers_ref[...] = step * direction_ref[...]
    new_residual_ref[...] = residual_ref[...] - step * image


def exchange(blocks):
    count = lax.axis_size("sub")
    received = [None] * BLOCKS
    for b in range(BLOCKS):
        route = [(i, (i + OFFSETS[b]) % count) for i in range(count)]
        received[(b + 3) % BLOCKS] = lax.ppermute(blocks[b], "sub", route)
    return received


def on_device(
    load_source,
    schur_diag,
    schur_factor,
    dir_diag,
    dir_factor,
    corner_map,
    corner_row,
    coarse_factor,
    slot_table,
):
    source = load_source[0, 0]
    schur_factor = schur_factor[0, 0]
    dir_factor = dir_factor[0, 0]
    corner_map = corner_map[0, 0]
    cases, interface = source.shape
    corners = corner_map.shape[0]
    subs, groups = lax.axis_size("sub"), lax.axis_size("grp")
    table = slot_table.reshape(1, -1)
    total = table.shape[1]
    cap = total // BLOCKS
    block_outs = [((cases, cap), BF16)] * BLOCKS
    field = (cases, interface)
    product = 2 * cases * interface * total

    depth, coarse_size = coarse_factor.shape
    rows = lax.all_to_all(
        jnp.broadcast_to(coarse_factor[None], (groups, depth, coarse_size)), "grp", 0, 0, tiled=True
    )
    row = corner_row.reshape(corners // 8, 8)
    index = jnp.stack([row // 32, row % 8, row // 8 % 4], axis=1).reshape(-1, 8).T
    index = jnp.pad(index, ((0, 0), (0, LANES - index.shape[1]))).astype(BF16)

    slots, *blocks = call(
        first_exchange_body, [((interface, total), BF16)] + block_outs, product, table, source
    )
    incoming = exchange(blocks)
    (dealt,) = call(
        deal_columns_body, [((subs, depth, 2 * LANES), BF16)], product // 16, rows, index
    )
    dealt = lax.all_to_all(dealt, "sub", 0, 0, tiled=True)
    residual, dir_out, live, rho, *blocks = call(
        dirichlet_body,
        [(field, F32), (field, BF16), ((8, interface), F32), ((8, cases), F32)] + block_outs,
        4 * product,
        *incoming,
        source,
        dir_diag[0],
        slots,
        dir_factor,
    )
    incoming = exchange(blocks)
    (picked,) = call(pick_rows_body, [((subs * depth, LANES), BF16)], product // 4, dealt)
    direction, schur_middle, corner_in = call(
        schur_first_body,
        [(field, F32), (field, BF16), ((subs, 8, LANES), BF16)],
        2 * product,
        *incoming,
        dir_out,
        live,
        schur_diag[0],
        slots,
        schur_factor,
        corner_map,
        rho,
    )
    corner_in = lax.all_to_all(corner_in, "sub", 0, 0, tiled=True)
    (local,) = call(
        schur_second_body,
        [(field, F32)],
        product,
        direction,
        schur_middle,
        schur_diag[0],
        schur_factor,
    )
    (parts,) = call(
        coarse_first_body, [((groups, 16, LANES), F32)], product // 64, corner_in, picked
    )
    parts = lax.all_to_all(parts, "grp", 0, 0, tiled=True)
    coarse, totals = call(
        coarse_second_body,
        [((subs, 8, LANES), BF16), ((8, LANES), F32)],
        product // 64,
        parts,
        picked,
    )
    coarse = lax.all_to_all(coarse, "sub", 0, 0, tiled=True)
    schur_out, step, *blocks = call(
        schur_last_body,
        [(field, BF16), ((cases, LANES), F32)] + block_outs,
        product,
        coarse,
        totals,
        local,
        corner_map,
        slots,
    )
    incoming = exchange(blocks)
    multipliers, residual = call(
        update_body,
        [(field, F32), (field, F32)],
        product,
        *incoming,
        schur_out,
        step,
        live,
        direction,
        residual,
        slots,
    )
    return (multipliers[None, None], residual[None, None])


def solution(mesh):
    return jax.shard_map(
        on_device,
        mesh=mesh,
        in_specs=(
            P("grp", "sub", None, None),
            P("grp", "sub", None),
            P("grp", "sub", None, None),
            P("grp", "sub", None),
            P("grp", "sub", None, None),
            P("grp", "sub", None, None),
            P("grp", "sub", None),
            P(("sub", "grp"), None),
            P("grp", "sub", None, None),
        ),
        out_specs=(P("grp", "sub", None, None), P("grp", "sub", None, None)),
        check_vma=False,
    )
```

profile of v0, /device:TPU:1, one launch (start us, length us, event | category | flops | bytes accessed | tf_op | source)
XLA Modules:
  0.0 126.2 jit_solution(4008008694936299107)
XLA Ops:
  2.1 4.8 %all-to-all-start.1 = ((bf16[4,8,2048]{2,1,0:T(8,128)(2,1)}), bf16[4,8,2048]{2,1,0:T(8,128)(2,1)S(1)}, u32[]{:S(2)}, u32[]{:S(2)}) async-start(bf16[4,8,2048]{2,1,0:T(8,128)(2,1)} %broadcast_in_dim.12), calls=%async_computation.1 | async-start | bytes 262144 | tf_op jit(solution)/shard_map/all_to_all | solution.py:271
  9.1 2.7 %all-to-all-done.1.rows_ref = bf16[4,8,2048]{2,1,0:T(8,128)(2,1)S(1)} async-done(((bf16[4,8,2048]{2,1,0:T(8,128)(2,1)}), bf16[4,8,2048]{2,1,0:T(8,128)(2,1)S(1)}, u32[]{:S(2)}, u32[]{:S(2)}) %all-to-all-start.1) | async-done | bytes 131104 | tf_op jit(solution)/shard_map/all_to_all | solution.py:271
  12.7 13.8 %all-to-all-start.2 = ((bf16[64,8,256]{2,1,0:T(8,128)(2,1)}), bf16[64,8,256]{2,1,0:T(8,128)(2,1)S(1)}, u32[]{:S(2)}, u32[]{:S(2)}) async-start(bf16[64,8,256]{2,1,0:T(8,128)(2,1)} %shard_map.107), calls=%async_computation.2 | async-start | bytes 524288 | tf_op jit(solution)/shard_map/all_to_all | solution.py:285
  29.8 4.9 %collective-permute-start.1 = (bf16[32,256]{1,0:T(8,128)(2,1)S(1)}, bf16[32,256]{1,0:T(8,128)(2,1)S(1)}, u32[]{:S(2)}, u32[]{:S(2)}) collective-permute-start(bf16[32,256]{1,0:T(8,128)(2,1)S(1)} %get-tuple-element.35), channel_id=1, source_target_pairs={{0,248},{4,252},{8,0},{12,4},{16,8},{20,12},{24,16},{28,20},{32,24... | collective-permute-start | bytes 49160 | tf_op jit(solution)/shard_map/ppermute | solution.py:241
  36.4 2.7 %collective-permute-start.5 = (bf16[32,256]{1,0:T(8,128)(2,1)S(1)}, bf16[32,256]{1,0:T(8,128)(2,1)S(1)}, u32[]{:S(2)}, u32[]{:S(2)}) collective-permute-start(bf16[32,256]{1,0:T(8,128)(2,1)S(1)} %get-tuple-element.39), channel_id=1, source_target_pairs={{0,20},{4,24},{8,28},{12,32},{16,36},{20,40},{24,44},{28,48},{32,5... | collective-permute-start | bytes 49160 | tf_op jit(solution)/shard_map/ppermute | solution.py:241
  39.4 2.9 %collective-permute-done.4.refs_4_ = bf16[32,256]{1,0:T(8,128)(2,1)S(1)} collective-permute-done((bf16[32,256]{1,0:T(8,128)(2,1)S(1)}, bf16[32,256]{1,0:T(8,128)(2,1)S(1)}, u32[]{:S(2)}, u32[]{:S(2)}) %collective-permute-start.4) | collective-permute-done | bytes 16416 | tf_op jit(solution)/shard_map/ppermute | solution.py:241
  43.2 2.3 %copy-done.3 = bf16[1,1,1536,1536]{3,2,1,0:T(8,128)(2,1)S(1)} copy-done((bf16[1,1,1536,1536]{3,2,1,0:T(8,128)(2,1)S(1)}, bf16[1,1,1536,1536]{3,2,1,0:T(8,128)(2,1)}, u32[]{:S(2)}) %copy-start.3) | copy-done | bytes 4718616
  47.1 4.4 %shard_map.105 = (f32[32,1536]{1,0:T(8,128)S(1)}, bf16[32,1536]{1,0:T(8,128)(2,1)S(1)}, f32[8,1536]{1,0:T(8,128)S(1)}, f32[8,32]{1,0:T(8,128)S(1)}, bf16[32,256]...) custom-call(bf16[32,256]{1,0:T(8,128)(2,1)S(1)} %collective-permute-, ...), custom_call_target="tpu_custom_call" | custom-call | flops 603979776 | bytes 9437184 | tf_op jit(solution)/shard_map/pallas_call | solution.py:59
  51.7 2.6 %collective-permute-start.7 = (bf16[32,256]{1,0:T(8,128)(2,1)S(1)}, bf16[32,256]{1,0:T(8,128)(2,1)S(1)}, u32[]{:S(2)}, u32[]{:S(2)}) collective-permute-start(bf16[32,256]{1,0:T(8,128)(2,1)S(1)} %get-tuple-element.42), channel_id=1, source_target_pairs={{0,248},{4,252},{8,0},{12,4},{16,8},{20,12},{24,16},{28,20},{32,24... | collective-permute-start | bytes 49160 | tf_op jit(solution)/shard_map/ppermute | solution.py:241
  54.3 1.6 %collective-permute-start.8 = (bf16[32,256]{1,0:T(8,128)(2,1)S(1)}, bf16[32,256]{1,0:T(8,128)(2,1)S(1)}, u32[]{:S(2)}, u32[]{:S(2)}) collective-permute-start(bf16[32,256]{1,0:T(8,128)(2,1)S(1)} %get-tuple-element.43), channel_id=1, source_target_pairs={{0,236},{4,240},{8,244},{12,248},{16,252},{20,0},{24,4},{28,8},{32... | collective-permute-start | bytes 49160 | tf_op jit(solution)/shard_map/ppermute | solution.py:241
  56.6 3.5 %collective-permute-start.11 = (bf16[32,256]{1,0:T(8,128)(2,1)S(1)}, bf16[32,256]{1,0:T(8,128)(2,1)S(1)}, u32[]{:S(2)}, u32[]{:S(2)}) collective-permute-start(bf16[32,256]{1,0:T(8,128)(2,1)S(1)} %get-tuple-element.46), channel_id=1, source_target_pairs={{0,20},{4,24},{8,28},{12,32},{16,36},{20,40},{24,44},{28,48},{32,5... | collective-permute-start | bytes 49160 | tf_op jit(solution)/shard_map/ppermute | solution.py:241
  60.1 2.1 %collective-permute-done.10.refs_4_ = bf16[32,256]{1,0:T(8,128)(2,1)S(1)} collective-permute-done((bf16[32,256]{1,0:T(8,128)(2,1)S(1)}, bf16[32,256]{1,0:T(8,128)(2,1)S(1)}, u32[]{:S(2)}, u32[]{:S(2)}) %collective-permute-start.10) | collective-permute-done | bytes 16416 | tf_op jit(solution)/shard_map/ppermute | solution.py:241
  63.4 3.2 %shard_map.106 = (f32[32,1536]{1,0:T(8,128)S(1)}, bf16[32,1536]{1,0:T(8,128)(2,1)S(1)}, bf16[64,8,128]{2,1,0:T(8,128)(2,1)}) custom-call(bf16[32,256]{1,0:T(8,128)(2,1)S(1)} %collective-permute-done.6.refs_0_, bf16[32,256]{1,0:T(8,128)(2,1)S(1)} %collective-permute-done.7.refs_1_, bf16[32,256]{1,0:T(8,128)(2,1)S(1)} %collective-permute-done.8.refs_2_, ...), custom_call_target="tpu_custom_call" | custom-call | flops 301989888 | bytes 4718592 | tf_op jit(solution)/shard_map/pallas_call | solution.py:59
  66.6 7.1 %all-to-all-start = ((bf16[64,8,128]{2,1,0:T(8,128)(2,1)}), bf16[64,8,128]{2,1,0:T(8,128)(2,1)S(1)}, u32[]{:S(2)}, u32[]{:S(2)}) async-start(bf16[64,8,128]{2,1,0:T(8,128)(2,1)} %get-tuple-element.50), calls=%async_computation | async-start | bytes 262144 | tf_op jit(solution)/shard_map/all_to_all | solution.py:311
  74.6 10.2 %all-to-all-done.corner_ref = bf16[64,8,128]{2,1,0:T(8,128)(2,1)S(1)} async-done(((bf16[64,8,128]{2,1,0:T(8,128)(2,1)}), bf16[64,8,128]{2,1,0:T(8,128)(2,1)S(1)}, u32[]{:S(2)}, u32[]{:S(2)}) %all-to-all-start) | async-done | bytes 131104 | tf_op jit(solution)/shard_map/all_to_all | solution.py:311
  85.2 6.6 %all_to_all.25.parts_ref = f32[4,16,128]{2,1,0:T(8,128)S(1)} all-to-all(f32[4,16,128]{2,1,0:T(8,128)S(1)} %shard_map.109), channel_id=1, replica_groups=mesh['sub'=64,'grp'=4] {'grp'}, dimensions={0} | all-to-all | bytes 65536 | tf_op jit(solution)/shard_map/all_to_all | solution.py:324
  92.8 5.6 %all-to-all-start.4 = ((bf16[64,8,128]{2,1,0:T(8,128)(2,1)}), bf16[64,8,128]{2,1,0:T(8,128)(2,1)S(1)}, u32[]{:S(2)}, u32[]{:S(2)}) async-start(bf16[64,8,128]{2,1,0:T(8,128)(2,1)} %get-tuple-element.51), calls=%async_computation.4 | async-start | bytes 262144 | tf_op jit(solution)/shard_map/all_to_all | solution.py:332
  98.4 2.3 %copy-done.2 = bf16[1,1,1536,1536]{3,2,1,0:T(8,128)(2,1)S(1)} copy-done((bf16[1,1,1536,1536]{3,2,1,0:T(8,128)(2,1)S(1)}, bf16[1,1,1536,1536]{3,2,1,0:T(8,128)(2,1)}, u32[]{:S(2)}) %copy-start.2) | copy-done | bytes 4718616
  102.2 7.6 %all-to-all-done.4.coarse_ref = bf16[64,8,128]{2,1,0:T(8,128)(2,1)S(1)} async-done(((bf16[64,8,128]{2,1,0:T(8,128)(2,1)}), bf16[64,8,128]{2,1,0:T(8,128)(2,1)S(1)}, u32[]{:S(2)}, u32[]{:S(2)}) %all-to-all-start.4) | async-done | bytes 131104 | tf_op jit(solution)/shard_map/all_to_all | solution.py:332
  109.7 2.3 %copy-done.1 = bf16[1536,1536]{1,0:T(8,128)(2,1)S(1)} copy-done((bf16[1536,1536]{1,0:T(8,128)(2,1)S(1)}, bf16[1536,1536]{1,0:T(8,128)(2,1)}, u32[]{:S(2)}) %copy-start.1) | copy-done | bytes 4718616
  114.7 2.4 %collective-permute-start.14 = (bf16[32,256]{1,0:T(8,128)(2,1)S(1)}, bf16[32,256]{1,0:T(8,128)(2,1)S(1)}, u32[]{:S(2)}, u32[]{:S(2)}) collective-permute-start(bf16[32,256]{1,0:T(8,128)(2,1)S(1)} %get-tuple-element.57), channel_id=1, source_target_pairs={{0,236},{4,240},{8,244},{12,248},{16,252},{20,0},{24,4},{28,8},{32... | collective-permute-start | bytes 49160 | tf_op jit(solution)/shard_map/ppermute | solution.py:241
  117.1 4.3 %collective-permute-start.17 = (bf16[32,256]{1,0:T(8,128)(2,1)S(1)}, bf16[32,256]{1,0:T(8,128)(2,1)S(1)}, u32[]{:S(2)}, u32[]{:S(2)}) collective-permute-start(bf16[32,256]{1,0:T(8,128)(2,1)S(1)} %get-tuple-element.60), channel_id=1, source_target_pairs={{0,20},{4,24},{8,28},{12,32},{16,36},{20,40},{24,44},{28,48},{32,5... | collective-permute-start | bytes 49160 | tf_op jit(solution)/shard_map/ppermute | solution.py:241
  121.4 1.6 %collective-permute-done.16.refs_4_ = bf16[32,256]{1,0:T(8,128)(2,1)S(1)} collective-permute-done((bf16[32,256]{1,0:T(8,128)(2,1)S(1)}, bf16[32,256]{1,0:T(8,128)(2,1)S(1)}, u32[]{:S(2)}, u32[]{:S(2)}) %collective-permute-start.16) | collective-permute-done | bytes 16416 | tf_op jit(solution)/shard_map/ppermute | solution.py:241
  124.1 2.2 %shard_map.113 = (f32[32,1536]{1,0:T(8,128)}, f32[32,1536]{1,0:T(8,128)}) custom-call(bf16[32,256]{1,0:T(8,128)(2,1)S(1)} %collective-permute-done.12.refs_0_, bf16[32,256]{1,0:T(8,128)(2,1)S(1)} %collective-permute-done.13.refs_1_, bf16[32,256]{1,0:T(8,128)(2,1)S(1)} %collective-permute-done.14.refs_2_, ...), custom_call_target="tpu_custom_call" | custom-call | flops 150994944 | bytes 2359296 | tf_op jit(solution)/shard_map/pallas_call | solution.py:59
  (65 shorter events, 21.7 us)
Async XLA Ops:
  2.1 9.7 %all-to-all-start.1 = ((bf16[4,8,2048]{2,1,0:T(8,128)(2,1)}), bf16[4,8,2048]{2,1,0:T(8,128)(2,1)S(1)}, u32[]{:S(2)}, u32[]{:S(2)}) async-start(bf16[4,8,2048]{2,1,0:T(8,128)(2,1)} %broadcast_in_dim.12), calls=%async_computation.1 | async-start | bytes 262144 | tf_op jit(solution)/shard_map/all_to_all | solution.py:271
  12.7 53.9 %all-to-all-start.2 = ((bf16[64,8,256]{2,1,0:T(8,128)(2,1)}), bf16[64,8,256]{2,1,0:T(8,128)(2,1)S(1)}, u32[]{:S(2)}, u32[]{:S(2)}) async-start(bf16[64,8,256]{2,1,0:T(8,128)(2,1)} %shard_map.107), calls=%async_computation.2 | async-start | bytes 524288 | tf_op jit(solution)/shard_map/all_to_all | solution.py:285
  28.0 35.4 %slice-start = ((s8[4718592]{0:T(1024)(128)(4,1)}), s8[4194304]{0:T(1024)(128)(4,1)S(1)}, s32[]{:S(2)}) async-start(s8[4718592]{0:T(1024)(128)(4,1)} %bitcast.12), calls=%async_computation.5 | async-start | bytes 8388608
  29.3 34.1 %copy-start = (bf16[1536,1536]{1,0:T(8,128)(2,1)}, bf16[1536,1536]{1,0:T(8,128)(2,1)S(1)}, u32[]{:S(2)}) copy-start(bf16[1536,1536]{1,0:T(8,128)(2,1)S(1)} %get-tuple-element.40.refs_8_.refs_9_.slots_ref.refs_11_) | copy-start | bytes 14155780
  29.3 7.2 %collective-permute-start = (bf16[32,256]{1,0:T(8,128)(2,1)S(1)}, bf16[32,256]{1,0:T(8,128)(2,1)S(1)}, u32[]{:S(2)}, u32[]{:S(2)}) collective-permute-start(bf16[32,256]{1,0:T(8,128)(2,1)S(1)} %get-tuple-element.34), channel_id=1, source_target_pairs={{0,252},{4,0},{8,4},{12,8},{16,12},{20,16},{24,20},{28,24},{32,28}... | collective-permute-start | bytes 49160 | tf_op jit(solution)/shard_map/ppermute | solution.py:241
  29.8 9.4 %collective-permute-start.1 = (bf16[32,256]{1,0:T(8,128)(2,1)S(1)}, bf16[32,256]{1,0:T(8,128)(2,1)S(1)}, u32[]{:S(2)}, u32[]{:S(2)}) collective-permute-start(bf16[32,256]{1,0:T(8,128)(2,1)S(1)} %get-tuple-element.35), channel_id=1, source_target_pairs={{0,248},{4,252},{8,0},{12,4},{16,8},{20,12},{24,16},{28,20},{32,24... | collective-permute-start | bytes 49160 | tf_op jit(solution)/shard_map/ppermute | solution.py:241
  34.7 4.7 %collective-permute-start.2 = (bf16[32,256]{1,0:T(8,128)(2,1)S(1)}, bf16[32,256]{1,0:T(8,128)(2,1)S(1)}, u32[]{:S(2)}, u32[]{:S(2)}) collective-permute-start(bf16[32,256]{1,0:T(8,128)(2,1)S(1)} %get-tuple-element.36), channel_id=1, source_target_pairs={{0,236},{4,240},{8,244},{12,248},{16,252},{20,0},{24,4},{28,8},{32... | collective-permute-start | bytes 49160 | tf_op jit(solution)/shard_map/ppermute | solution.py:241
  35.7 3.7 %collective-permute-start.3 = (bf16[32,256]{1,0:T(8,128)(2,1)S(1)}, bf16[32,256]{1,0:T(8,128)(2,1)S(1)}, u32[]{:S(2)}, u32[]{:S(2)}) collective-permute-start(bf16[32,256]{1,0:T(8,128)(2,1)S(1)} %get-tuple-element.37), channel_id=1, source_target_pairs={{0,4},{4,8},{8,12},{12,16},{16,20},{20,24},{24,28},{28,32},{32,36}... | collective-permute-start | bytes 49160 | tf_op jit(solution)/shard_map/ppermute | solution.py:241
  36.4 5.9 %collective-permute-start.4 = (bf16[32,256]{1,0:T(8,128)(2,1)S(1)}, bf16[32,256]{1,0:T(8,128)(2,1)S(1)}, u32[]{:S(2)}, u32[]{:S(2)}) collective-permute-start(bf16[32,256]{1,0:T(8,128)(2,1)S(1)} %get-tuple-element.38), channel_id=1, source_target_pairs={{0,8},{4,12},{8,16},{12,20},{16,24},{20,28},{24,32},{28,36},{32,40... | collective-permute-start | bytes 49160 | tf_op jit(solution)/shard_map/ppermute | solution.py:241
  36.4 6.8 %collective-permute-start.5 = (bf16[32,256]{1,0:T(8,128)(2,1)S(1)}, bf16[32,256]{1,0:T(8,128)(2,1)S(1)}, u32[]{:S(2)}, u32[]{:S(2)}) collective-permute-start(bf16[32,256]{1,0:T(8,128)(2,1)S(1)} %get-tuple-element.39), channel_id=1, source_target_pairs={{0,20},{4,24},{8,28},{12,32},{16,36},{20,40},{24,44},{28,48},{32,5... | collective-permute-start | bytes 49160 | tf_op jit(solution)/shard_map/ppermute | solution.py:241
  51.6 5.0 %collective-permute-start.6 = (bf16[32,256]{1,0:T(8,128)(2,1)S(1)}, bf16[32,256]{1,0:T(8,128)(2,1)S(1)}, u32[]{:S(2)}, u32[]{:S(2)}) collective-permute-start(bf16[32,256]{1,0:T(8,128)(2,1)S(1)} %get-tuple-element.41), channel_id=1, source_target_pairs={{0,252},{4,0},{8,4},{12,8},{16,12},{20,16},{24,20},{28,24},{32,28}... | collective-permute-start | bytes 49160 | tf_op jit(solution)/shard_map/ppermute | solution.py:241
  51.7 8.4 %collective-permute-start.7 = (bf16[32,256]{1,0:T(8,128)(2,1)S(1)}, bf16[32,256]{1,0:T(8,128)(2,1)S(1)}, u32[]{:S(2)}, u32[]{:S(2)}) collective-permute-start(bf16[32,256]{1,0:T(8,128)(2,1)S(1)} %get-tuple-element.42), channel_id=1, source_target_pairs={{0,248},{4,252},{8,0},{12,4},{16,8},{20,12},{24,16},{28,20},{32,24... | collective-permute-start | bytes 49160 | tf_op jit(solution)/shard_map/ppermute | solution.py:241
  54.3 5.8 %collective-permute-start.8 = (bf16[32,256]{1,0:T(8,128)(2,1)S(1)}, bf16[32,256]{1,0:T(8,128)(2,1)S(1)}, u32[]{:S(2)}, u32[]{:S(2)}) collective-permute-start(bf16[32,256]{1,0:T(8,128)(2,1)S(1)} %get-tuple-element.43), channel_id=1, source_target_pairs={{0,236},{4,240},{8,244},{12,248},{16,252},{20,0},{24,4},{28,8},{32... | collective-permute-start | bytes 49160 | tf_op jit(solution)/shard_map/ppermute | solution.py:241
  55.9 4.1 %collective-permute-start.9 = (bf16[32,256]{1,0:T(8,128)(2,1)S(1)}, bf16[32,256]{1,0:T(8,128)(2,1)S(1)}, u32[]{:S(2)}, u32[]{:S(2)}) collective-permute-start(bf16[32,256]{1,0:T(8,128)(2,1)S(1)} %get-tuple-element.44), channel_id=1, source_target_pairs={{0,4},{4,8},{8,12},{12,16},{16,20},{20,24},{24,28},{28,32},{32,36}... | collective-permute-start | bytes 49160 | tf_op jit(solution)/shard_map/ppermute | solution.py:241
  56.3 5.9 %collective-permute-start.10 = (bf16[32,256]{1,0:T(8,128)(2,1)S(1)}, bf16[32,256]{1,0:T(8,128)(2,1)S(1)}, u32[]{:S(2)}, u32[]{:S(2)}) collective-permute-start(bf16[32,256]{1,0:T(8,128)(2,1)S(1)} %get-tuple-element.45), channel_id=1, source_target_pairs={{0,8},{4,12},{8,16},{12,20},{16,24},{20,28},{24,32},{28,36},{32,40... | collective-permute-start | bytes 49160 | tf_op jit(solution)/shard_map/ppermute | solution.py:241
  56.6 6.8 %collective-permute-start.11 = (bf16[32,256]{1,0:T(8,128)(2,1)S(1)}, bf16[32,256]{1,0:T(8,128)(2,1)S(1)}, u32[]{:S(2)}, u32[]{:S(2)}) collective-permute-start(bf16[32,256]{1,0:T(8,128)(2,1)S(1)} %get-tuple-element.46), channel_id=1, source_target_pairs={{0,20},{4,24},{8,28},{12,32},{16,36},{20,40},{24,44},{28,48},{32,5... | collective-permute-start | bytes 49160 | tf_op jit(solution)/shard_map/ppermute | solution.py:241
  66.6 18.3 %all-to-all-start = ((bf16[64,8,128]{2,1,0:T(8,128)(2,1)}), bf16[64,8,128]{2,1,0:T(8,128)(2,1)S(1)}, u32[]{:S(2)}, u32[]{:S(2)}) async-start(bf16[64,8,128]{2,1,0:T(8,128)(2,1)} %get-tuple-element.50), calls=%async_computation | async-start | bytes 262144 | tf_op jit(solution)/shard_map/all_to_all | solution.py:311
  92.8 17.0 %all-to-all-start.4 = ((bf16[64,8,128]{2,1,0:T(8,128)(2,1)}), bf16[64,8,128]{2,1,0:T(8,128)(2,1)S(1)}, u32[]{:S(2)}, u32[]{:S(2)}) async-start(bf16[64,8,128]{2,1,0:T(8,128)(2,1)} %get-tuple-element.51), calls=%async_computation.4 | async-start | bytes 262144 | tf_op jit(solution)/shard_map/all_to_all | solution.py:332
  113.3 3.8 %collective-permute-start.12 = (bf16[32,256]{1,0:T(8,128)(2,1)S(1)}, bf16[32,256]{1,0:T(8,128)(2,1)S(1)}, u32[]{:S(2)}, u32[]{:S(2)}) collective-permute-start(bf16[32,256]{1,0:T(8,128)(2,1)S(1)} %get-tuple-element.55), channel_id=1, source_target_pairs={{0,252},{4,0},{8,4},{12,8},{16,12},{20,16},{24,20},{28,24},{32,28}... | collective-permute-start | bytes 49160 | tf_op jit(solution)/shard_map/ppermute | solution.py:241
  113.7 7.7 %collective-permute-start.13 = (bf16[32,256]{1,0:T(8,128)(2,1)S(1)}, bf16[32,256]{1,0:T(8,128)(2,1)S(1)}, u32[]{:S(2)}, u32[]{:S(2)}) collective-permute-start(bf16[32,256]{1,0:T(8,128)(2,1)S(1)} %get-tuple-element.56), channel_id=1, source_target_pairs={{0,248},{4,252},{8,0},{12,4},{16,8},{20,12},{24,16},{28,20},{32,24... | collective-permute-start | bytes 49160 | tf_op jit(solution)/shard_map/ppermute | solution.py:241
  114.7 6.7 %collective-permute-start.14 = (bf16[32,256]{1,0:T(8,128)(2,1)S(1)}, bf16[32,256]{1,0:T(8,128)(2,1)S(1)}, u32[]{:S(2)}, u32[]{:S(2)}) collective-permute-start(bf16[32,256]{1,0:T(8,128)(2,1)S(1)} %get-tuple-element.57), channel_id=1, source_target_pairs={{0,236},{4,240},{8,244},{12,248},{16,252},{20,0},{24,4},{28,8},{32... | collective-permute-start | bytes 49160 | tf_op jit(solution)/shard_map/ppermute | solution.py:241
  117.1 4.3 %collective-permute-start.15 = (bf16[32,256]{1,0:T(8,128)(2,1)S(1)}, bf16[32,256]{1,0:T(8,128)(2,1)S(1)}, u32[]{:S(2)}, u32[]{:S(2)}) collective-permute-start(bf16[32,256]{1,0:T(8,128)(2,1)S(1)} %get-tuple-element.58), channel_id=1, source_target_pairs={{0,4},{4,8},{8,12},{12,16},{16,20},{20,24},{24,28},{28,32},{32,36}... | collective-permute-start | bytes 49160 | tf_op jit(solution)/shard_map/ppermute | solution.py:241
  117.1 5.9 %collective-permute-start.16 = (bf16[32,256]{1,0:T(8,128)(2,1)S(1)}, bf16[32,256]{1,0:T(8,128)(2,1)S(1)}, u32[]{:S(2)}, u32[]{:S(2)}) collective-permute-start(bf16[32,256]{1,0:T(8,128)(2,1)S(1)} %get-tuple-element.59), channel_id=1, source_target_pairs={{0,8},{4,12},{8,16},{12,20},{16,24},{20,28},{24,32},{28,36},{32,40... | collective-permute-start | bytes 49160 | tf_op jit(solution)/shard_map/ppermute | solution.py:241
  117.1 7.0 %collective-permute-start.17 = (bf16[32,256]{1,0:T(8,128)(2,1)S(1)}, bf16[32,256]{1,0:T(8,128)(2,1)S(1)}, u32[]{:S(2)}, u32[]{:S(2)}) collective-permute-start(bf16[32,256]{1,0:T(8,128)(2,1)S(1)} %get-tuple-element.60), channel_id=1, source_target_pairs={{0,20},{4,24},{8,28},{12,32},{16,36},{20,40},{24,44},{28,48},{32,5... | collective-permute-start | bytes 49160 | tf_op jit(solution)/shard_map/ppermute | solution.py:241
  (10 other events, 58.9 us)
where the time goes:
time: 127 us; the launch traced here: 126 us
  starting transfers between devices  57.8 us (46%)
  waiting for transfers between devices  30.4 us (24%)
  Pallas kernels  16.8 us (13%)
  local copies, waits for them, and re-layouts  12.4 us (10%)
  blocking collectives  6.65 us (5%)
  other arithmetic  1.35 us (1%)
    ppermute x18, starting transfers between devices, exchange(): received[(b + 3) % BLOCKS] = lax.ppermute(blocks[b], 'sub', route)  26.5 us
    pallas_call x10, Pallas kernels, call(): pl.pallas_call(body, out_shape=[jax.ShapeDtypeStruct(shape, dtype) for sh...  16.8 us
    all_to_all x1, starting transfers between devices, on_device(): dealt = lax.all_to_all(dealt, 'sub', 0, 0, tiled=True)  13.8 us
    unnamed x25, local copies, waits for them, and re-layouts  10.7 us
    all_to_all x1, waiting for transfers between devices, on_device(): corner_in = lax.all_to_all(corner_in, 'sub', 0, 0, tiled=True)  10.2 us
    ppermute x18, waiting for transfers between devices, exchange(): received[(b + 3) % BLOCKS] = lax.ppermute(blocks[b], 'sub', route)  10 us
    all_to_all x1, waiting for transfers between devices, on_device(): coarse = lax.all_to_all(coarse, 'sub', 0, 0, tiled=True)  7.55 us
    all_to_all x1, starting transfers between devices, on_device(): corner_in = lax.all_to_all(corner_in, 'sub', 0, 0, tiled=True)  7.13 us
  transfers between devices with their start and end apart: 22, of which 10 were waited for; matrix products, arithmetic and copies ran while one was open for 2% of the time, Pallas kernels for 9%

commit v1 on v0

v1 whole, which is shorter than its diff:
```python
import jax
import jax.numpy as jnp
from jax import lax
from jax.experimental import pallas as pl
from jax.experimental.pallas import tpu as pltpu
from jax.sharding import PartitionSpec as P

OFFSETS = (1, 2, 5, -1, -2, -5)
BLOCKS = len(OFFSETS)
F32 = jnp.float32
BF16 = jnp.bfloat16
LANES = 128
PIECES = 3
TABLE, DIR_DIAG, SCHUR_DIAG, CORNER_ROW = 0, 1, 2, 3


def dot_nn(a, b):
    return jnp.dot(a, b, preferred_element_type=F32)


def dot_nt(a, b):
    return lax.dot_general(a, b, (((1,), (1,)), ((), ())), preferred_element_type=F32)


def dot_tn(a, b):
    return lax.dot_general(a, b, (((0,), (0,)), ((), ())), preferred_element_type=F32)


def column_to_row(column):
    n = column.shape[0]
    same = lax.broadcasted_iota(jnp.int32, (n, n), 0) == lax.broadcasted_iota(jnp.int32, (n, n), 1)
    return jnp.sum(jnp.where(same, column, 0.0), axis=0, keepdims=True)


def row_to_column(row):
    n = row.shape[1]
    same = lax.broadcasted_iota(jnp.int32, (n, n), 0) == lax.broadcasted_iota(jnp.int32, (n, n), 1)
    return jnp.sum(jnp.where(same, row, 0.0), axis=1, keepdims=True)


def three_parts(value):
    first = value.astype(BF16).astype(F32)
    rest = value - first
    second = rest.astype(BF16).astype(F32)
    third = (rest - second).astype(BF16).astype(F32)
    return [first, second, third]


def fold_rows(rows):
    n = rows.shape[0] // 4
    return jnp.concatenate([rows[n * i : n * i + n] for i in range(4)], axis=1)


def unfold_rows(tile):
    n = tile.shape[1] // 4
    return jnp.concatenate([tile[:, n * i : n * i + n] for i in range(4)], axis=0)


def call(body, outs, weight, *args, scratch=(), in_hbm=(), vmem=20):
    in_vmem = pl.BlockSpec(memory_space=pltpu.VMEM)
    left = pl.BlockSpec(memory_space=pltpu.HBM)
    return pl.pallas_call(
        body,
        out_shape=[jax.ShapeDtypeStruct(shape, dtype) for shape, dtype in outs],
        in_specs=[left if i in in_hbm else in_vmem for i in range(len(args))],
        out_specs=[in_vmem] * len(outs),
        scratch_shapes=list(scratch),
        compiler_params=pltpu.CompilerParams(vmem_limit_bytes=vmem * 1024 * 1024),
        cost_estimate=pl.CostEstimate(
            flops=weight << 20, bytes_accessed=weight << 20, transcendentals=0
        ),
    )(*args)


def slot_block(rows_ref, b, interface):
    cap = rows_ref.shape[1] // BLOCKS
    rows = lax.broadcasted_iota(jnp.int32, (interface, cap), 0).astype(F32)
    named = rows == rows_ref[TABLE : TABLE + 1, b * cap : (b + 1) * cap]
    return jnp.where(named, 1.0, 0.0).astype(BF16)


def from_slots(values, rows_ref, b):
    return dot_nn(values, slot_block(rows_ref, b, values.shape[1])).astype(BF16)


def to_slots(blocks, rows_ref, interface):
    total = dot_nt(blocks[0], slot_block(rows_ref, 0, interface))
    for b in range(1, BLOCKS):
        total = total + dot_nt(blocks[b], slot_block(rows_ref, b, interface))
    return total


def share_rows_body(coarse_ref, shared_ref):
    shared_ref[...] = jnp.broadcast_to(coarse_ref[...][None], shared_ref.shape)


def first_exchange_body(rows_ref, fields_ref, *block_refs):
    values = fields_ref[...]
    for b in range(BLOCKS):
        block_refs[b][...] = from_slots(values, rows_ref, b)


def load_factor(factor_ref, held_ref, semaphores):
    size = held_ref.shape[0] // PIECES
    copies = []
    for i in range(PIECES):
        piece = pl.ds(size * i, size)
        copies.append(
            pltpu.make_async_copy(factor_ref.at[piece], held_ref.at[piece], semaphores.at[i])
        )
        copies[i].start()
    return copies


def times_factor(operand, held_ref, copies):
    size = held_ref.shape[0] // PIECES
    total = None
    for i in range(PIECES):
        copies[i].wait()
        part = dot_nn(operand[:, size * i : size * i + size], held_ref[size * i : size * i + size])
        total = part if total is None else total + part
    return total


def dirichlet_body(*refs):
    rows_ref, fields_ref, factor_ref = refs[BLOCKS : BLOCKS + 3]
    residual_ref, out_ref, live_ref, rho_ref, *block_refs = refs[BLOCKS + 3 : -3]
    slots_ref, held_ref, semaphores = refs[-3:]
    copies = load_factor(factor_ref, held_ref, semaphores)
    cases, interface = residual_ref.shape
    cap = block_refs[0].shape[1]
    ones = jnp.ones((16, cap), BF16)
    spread = jnp.zeros((cases + 16, interface), F32)
    for b in range(BLOCKS):
        block = slot_block(rows_ref, b, interface)
        slots_ref[:, b * cap : (b + 1) * cap] = block
        spread = spread + dot_nt(jnp.concatenate([refs[b][:cases], ones], axis=0), block)
    live = spread[cases : cases + 8]
    residual = live[0:1] * (fields_ref[:cases].astype(F32) - spread[:cases])
    middle = times_factor(residual.astype(BF16), held_ref, copies).astype(BF16)
    diag = rows_ref[DIR_DIAG : DIR_DIAG + 1]
    out = (0.5 * (diag * residual + dot_nt(middle, held_ref[...]))).astype(BF16)
    for b in range(BLOCKS):
        block_refs[b][...] = dot_nn(out, slots_ref[:, b * cap : (b + 1) * cap]).astype(BF16)
    live_ref[...] = live
    residual_ref[...] = residual
    out_ref[...] = out
    rho = column_to_row(jnp.sum(residual * out.astype(F32), axis=1, keepdims=True))
    rho_ref[...] = jnp.broadcast_to(rho, rho_ref.shape)


def schur_first_body(*refs):
    out_ref, live_ref, rho_ref, rows_ref, fields_ref, mine_ref, factor_ref = refs[
        BLOCKS : BLOCKS + 7
    ]
    direction_ref, middle_ref, send_ref, held_ref, semaphores = refs[BLOCKS + 7 :]
    copies = load_factor(factor_ref, held_ref, semaphores)
    received = to_slots([ref[...] for ref in refs[:BLOCKS]], rows_ref, out_ref.shape[1])
    direction = 0.5 * (live_ref[0:1] * (out_ref[...].astype(F32) - received))
    direction_ref[...] = direction
    operand = direction.astype(BF16)
    wide = times_factor(operand, held_ref, copies)
    middle = wide.astype(BF16)
    middle_ref[...] = middle
    diag = rows_ref[SCHUR_DIAG : SCHUR_DIAG + 1]
    curve = jnp.sum(diag * direction * direction, axis=1, keepdims=True)
    curve = curve + jnp.sum(wide * middle.astype(F32), axis=1, keepdims=True)
    cases = operand.shape[0]
    corner_in = dot_nt(fields_ref[cases : cases + 24], operand)
    zero = jnp.zeros((2, corner_in.shape[1]), F32)
    scalars = three_parts(rho_ref[0:1]) + three_parts(column_to_row(curve)) + [zero]
    tile = fold_rows(jnp.concatenate([corner_in] + scalars, axis=0)).astype(BF16)
    count, depth, _ = send_ref.shape
    send_ref[:, :, :LANES] = jnp.broadcast_to(tile[None], (count, depth, LANES))
    send_ref[:, :, LANES:] = mine_ref[...]


def flat_tiles(tiles):
    count, depth, lanes = tiles.shape
    return tiles.astype(F32).reshape(count * depth, lanes).astype(BF16)


def schur_second_body(
    direction_ref, middle_ref, rows_ref, factor_ref, local_ref, *rest
):
    block_refs, held_ref, semaphores = rest[:-2], rest[-2], rest[-1]
    for copy in load_factor(factor_ref, held_ref, semaphores):
        copy.wait()
    back = dot_nt(middle_ref[...], held_ref[...])
    diag = rows_ref[SCHUR_DIAG : SCHUR_DIAG + 1]
    local = (diag * direction_ref[...] + back).astype(BF16)
    local_ref[...] = local
    for b in range(BLOCKS):
        block_refs[b][...] = from_slots(local, rows_ref, b)


def index_tile(corner_row, depth):
    corners = corner_row.shape[1]
    row = lax.broadcasted_iota(jnp.int32, (depth, corners), 0)
    lane = lax.broadcasted_iota(jnp.int32, (depth, corners), 1)
    place = lax.broadcasted_iota(jnp.int32, (depth, LANES), 1)
    tile = jnp.zeros((depth, LANES), F32)
    for q in range(3):
        mine = jnp.where(lane == 8 * q + row, corner_row, 0.0)
        value = jnp.sum(mine, axis=1, keepdims=True).astype(jnp.int32)
        parts = (value // 32, value % 8, value // 8 % 4)
        for part in range(3):
            tile = jnp.where(place == 3 * q + part, parts[part].astype(F32), tile)
    return tile.astype(BF16)


def deal(rows, store):
    depth, lanes = rows[0].shape
    group = lax.broadcasted_iota(jnp.int32, (depth, lanes), 1) // 32 % 4
    for t in range(4):
        dealt = jnp.zeros((depth, lanes), F32)
        for a in range(4):
            shift = (32 * (a - t)) % lanes
            moved = pltpu.roll(rows[a], shift, 1) if shift else rows[a]
            dealt = jnp.where(group == a, moved, dealt)
        for quad in range(lanes // LANES):
            store(4 * quad + t, dealt[:, quad * LANES : (quad + 1) * LANES].astype(BF16))


def deal_columns_body(shared_ref, rows_ref, send_ref):
    members, depth, _ = shared_ref.shape
    index = index_tile(rows_ref[CORNER_ROW : CORNER_ROW + 1, :LANES], depth)

    def store(other, tile):
        send_ref[other, :, :LANES] = tile
        send_ref[other, :, LANES:] = index

    deal([shared_ref[a].astype(F32) for a in range(members)], store)


def pick_rows_body(dealt_ref, picked_ref, send_ref):
    count, depth, _ = dealt_ref.shape
    dealt = dealt_ref[...].astype(F32)
    columns = dealt[:, :, :LANES].reshape(count * depth, LANES).astype(BF16)
    index = dealt[:, :, LANES:].reshape(count * depth, LANES)
    size = count * depth
    place = lax.broadcasted_iota(jnp.int32, (size, size), 1).astype(F32)
    lane_group = (lax.broadcasted_iota(jnp.int32, (size, LANES), 1) // 32).astype(F32)
    near = lax.broadcasted_iota(jnp.int32, (LANES, LANES), 0)
    far = lax.broadcasted_iota(jnp.int32, (LANES, LANES), 1)
    total = jnp.zeros((size, LANES), F32)
    for q in range(3):
        high = index[:, 3 * q : 3 * q + 1] * 8.0 + index[:, 3 * q + 1 : 3 * q + 2]
        onehot = jnp.where(place == high, 1.0, 0.0).astype(BF16)
        rows = dot_nn(onehot, columns)
        rows = jnp.where(lane_group == index[:, 3 * q + 2 : 3 * q + 3], rows, 0.0).astype(BF16)
        fold = jnp.where((near % 32 == far % 32) & (far // 32 == q), 1.0, 0.0).astype(BF16)
        total = total + dot_nn(rows, fold)
    picked_ref[...] = total.astype(BF16)

    wide = 32 * count
    source = lax.broadcasted_iota(jnp.int32, (size, wide), 0)
    target = lax.broadcasted_iota(jnp.int32, (size, wide), 1)
    same = (source // 8 == target // 32) & (source % 8 == target % 8)
    turned = dot_tn(index.astype(BF16), jnp.where(same, 1.0, 0.0).astype(BF16))
    slot = lax.broadcasted_iota(jnp.int32, (1, wide), 1) // 8 % 4
    high = jnp.full((1, wide), -1.0, F32)
    part = jnp.full((1, wide), -1.0, F32)
    for q in range(3):
        mine = slot == q
        value = turned[3 * q : 3 * q + 1] * 8.0 + turned[3 * q + 1 : 3 * q + 2]
        high = jnp.where(mine, value, high)
        part = jnp.where(mine, turned[3 * q + 2 : 3 * q + 3], part)
    onehot = jnp.where(source.astype(F32) == high, 1.0, 0.0).astype(BF16)
    spread = dot_tn(columns, onehot)
    chosen = jnp.zeros((32, wide), F32)
    for a in range(4):
        chosen = chosen + jnp.where(part == a, spread[32 * a : 32 * a + 32], 0.0)

    def store(other, tile):
        send_ref[other] = tile

    deal([chosen[8 * a : 8 * a + 8] for a in range(4)], store)


def coarse_first_body(corner_ref, picked_ref, *refs):
    local_refs, send_ref, block_refs = refs[:BLOCKS], refs[BLOCKS], refs[BLOCKS + 1 :]
    count, depth, _ = corner_ref.shape
    corner = corner_ref[:, :, :LANES].astype(F32)
    products = dot_tn(picked_ref[...], corner.reshape(count * depth, LANES).astype(BF16))
    middle = products[:32, :32]
    for q in range(1, 3):
        middle = middle + products[32 * q : 32 * q + 32, 32 * q : 32 * q + 32]
    tile = jnp.concatenate([fold_rows(middle), jnp.sum(corner, axis=0)], axis=0)
    send_ref[...] = jnp.broadcast_to(tile[None], send_ref.shape)
    mine = flat_tiles(corner_ref[:, :, LANES:])
    half = mine.shape[0] // 2
    cases = local_refs[0].shape[0]
    for b in range(BLOCKS):
        block_refs[b][:cases] = local_refs[b][...]
        block_refs[b][cases:, :LANES] = mine[:half]
        block_refs[b][cases:, LANES:] = mine[half:]


def coarse_second_body(parts_ref, send_ref, totals_ref):
    parts = parts_ref[...]
    total = parts[0]
    for member in range(1, parts.shape[0]):
        total = total + parts[member]
    send_ref[...] = jnp.broadcast_to(total[None, :8], send_ref.shape).astype(BF16)
    totals_ref[...] = total[8:16]


def diagonal_sum(products):
    total = products[:32, :32]
    for a in range(1, 4):
        total = total + products[32 * a : 32 * a + 32, 32 * a : 32 * a + 32]
    return total


def update_body(*refs):
    others, firsts = refs[:BLOCKS], refs[BLOCKS : 2 * BLOCKS]
    middle_ref, totals_ref, mine_ref, local_ref = refs[2 * BLOCKS : 2 * BLOCKS + 4]
    rows_ref, fields_ref, live_ref, direction_ref, residual_ref = refs[
        2 * BLOCKS + 4 : 2 * BLOCKS + 9
    ]
    multipliers_ref, new_residual_ref = refs[2 * BLOCKS + 9 :]
    middle = flat_tiles(middle_ref[...])
    half = middle.shape[0] // 2
    cases, interface = local_ref.shape
    corners = 24

    wide = middle.astype(F32)
    square = unfold_rows(jnp.sum(wide * wide, axis=0, keepdims=True))
    square = jnp.sum(square, axis=0, keepdims=True)
    scalars = totals_ref[:, 96:]
    rho = jnp.sum(scalars[0:3], axis=0, keepdims=True)
    curve = 2.0 * (jnp.sum(scalars[3:6], axis=0, keepdims=True) + square)
    step = row_to_column(rho / curve)
    multipliers_ref[...] = step * direction_ref[...]

    picked = diagonal_sum(dot_tn(flat_tiles(mine_ref[:, :, LANES:]), middle))[:corners].astype(BF16)
    schur = (local_ref[...].astype(F32) + dot_tn(picked, fields_ref[cases : cases + corners])).astype(BF16)
    blocks = []
    for b in range(BLOCKS):
        products = dot_tn(others[b][cases:, :LANES], middle[:half])
        products = products + dot_tn(others[b][cases:, LANES:], middle[half:])
        picked = diagonal_sum(products)[:corners].astype(BF16)
        corner_out = dot_tn(picked, firsts[b][cases : cases + corners])
        blocks.append((others[b][:cases].astype(F32) + corner_out).astype(BF16))
    received = to_slots(blocks, rows_ref, interface)
    image = live_ref[0:1] * (schur.astype(F32) - received)
    new_residual_ref[...] = residual_ref[...] - step * image


def exchange(blocks):
    count = lax.axis_size("sub")
    received = [None] * BLOCKS
    for b in range(BLOCKS):
        route = [(i, (i + OFFSETS[b]) % count) for i in range(count)]
        received[(b + 3) % BLOCKS] = lax.ppermute(blocks[b], "sub", route)
    return received


def on_device(
    load_source,
    schur_diag,
    schur_factor,
    dir_diag,
    dir_factor,
    corner_map,
    corner_row,
    coarse_factor,
    slot_table,
):
    source = load_source[0, 0]
    schur_factor = schur_factor[0, 0]
    dir_factor = dir_factor[0, 0]
    cases, interface = source.shape
    subs, groups = lax.axis_size("sub"), lax.axis_size("grp")
    table = slot_table.reshape(1, -1)
    total = table.shape[1]
    cap = total // BLOCKS
    field = (cases, interface)
    depth, coarse_size = coarse_factor.shape
    last_rows = cases + subs * depth // 2

    def blocks_of(rows):
        return [((rows, cap), BF16)] * BLOCKS

    corner_row = corner_row[0].astype(F32)
    corner_row = jnp.pad(corner_row, ((0, 0), (0, interface - corner_row.shape[1])))
    rows = jnp.concatenate([table.astype(F32), dir_diag[0], schur_diag[0], corner_row], axis=0)
    fields = jnp.concatenate([source, corner_map[0, 0]], axis=0)
    fields = jnp.pad(fields, ((0, -fields.shape[0] % 16), (0, 0)))
    first_rows = fields.shape[0]
    factor_scratch = [pltpu.VMEM((interface, interface), BF16), pltpu.SemaphoreType.DMA((PIECES,))]

    (shared,) = call(share_rows_body, [((groups, depth, coarse_size), BF16)], 1, coarse_factor)
    shared = lax.all_to_all(shared, "grp", 0, 0, tiled=True)
    blocks = call(first_exchange_body, blocks_of(first_rows), 4, rows, fields)
    firsts = exchange(blocks)
    (dealt,) = call(
        deal_columns_body, [((subs, depth, 2 * LANES), BF16)], 4, shared, rows
    )
    dealt, *firsts = lax.optimization_barrier((dealt, *firsts))
    dealt = lax.all_to_all(dealt, "sub", 0, 0, tiled=True)
    residual, dir_out, live, rho, *blocks = call(
        dirichlet_body,
        [(field, F32), (field, BF16), ((8, interface), F32), ((8, cases), F32)] + blocks_of(cases),
        16,
        *firsts,
        rows,
        fields,
        dir_factor,
        scratch=[pltpu.VMEM((interface, total), BF16)] + factor_scratch,
        in_hbm=(BLOCKS + 2,),
        vmem=50,
    )
    seconds = exchange(blocks)
    picked, mine = call(
        pick_rows_body,
        [((subs * depth, LANES), BF16), ((subs, depth, LANES), BF16)],
        8,
        dealt,
    )
    direction, schur_middle, corner_in = call(
        schur_first_body,
        [(field, F32), (field, BF16), ((subs, depth, 2 * LANES), BF16)],
        16,
        *seconds,
        dir_out,
        live,
        rho,
        rows,
        fields,
        mine,
        schur_factor,
        scratch=factor_scratch,
        in_hbm=(BLOCKS + 6,),
        vmem=50,
    )
    corner_in = lax.all_to_all(corner_in, "sub", 0, 0, tiled=True)
    local, *blocks = call(
        schur_second_body,
        [(field, BF16)] + blocks_of(cases),
        8,
        direction,
        schur_middle,
        rows,
        schur_factor,
        scratch=factor_scratch,
        in_hbm=(3,),
        vmem=50,
    )
    parts, *blocks = call(
        coarse_first_body,
        [((groups, 16, LANES), F32)] + blocks_of(last_rows),
        4,
        corner_in,
        picked,
        *blocks,
    )
    parts = lax.all_to_all(parts, "grp", 0, 0, tiled=True)
    others = exchange(blocks)
    middle, totals = call(
        coarse_second_body, [((subs, 8, LANES), BF16), ((8, LANES), F32)], 2, parts
    )
    middle = lax.all_to_all(middle, "sub", 0, 0, tiled=True)
    multipliers, residual = call(
        update_body,
        [(field, F32), (field, F32)],
        8,
        *others,
        *firsts,
        middle,
        totals,
        corner_in,
        local,
        rows,
        fields,
        live,
        direction,
        residual,
    )
    return (multipliers[None, None], residual[None, None])


def solution(mesh):
    return jax.shard_map(
        on_device,
        mesh=mesh,
        in_specs=(
            P("grp", "sub", None, None),
            P("grp", "sub", None),
            P("grp", "sub", None, None),
            P("grp", "sub", None),
            P("grp", "sub", None, None),
            P("grp", "sub", None, None),
            P("grp", "sub", None),
            P(("sub", "grp"), None),
            P("grp", "sub", None, None),
        ),
        out_specs=(P("grp", "sub", None, None), P("grp", "sub", None, None)),
        check_vma=False,
    )
```

time: 127 us -> 120 us (0.945)
  local copies, waits for them, and re-layouts: 12.4 us -> 0.75 us
  Pallas kernels: 16.8 us -> 24.7 us
  waiting for transfers between devices: 30.4 us -> 25.4 us
  blocking collectives: 6.65 us -> 8.6 us
  starting transfers between devices: 57.8 us -> 56.1 us
  other arithmetic: 1.35 us -> 3.03 us
    all_to_all x2, waiting for transfers between devices: 10.2 us -> 0.01 us  [the longest x1 0.01 us: on_device(): middle = lax.all_to_all(middle, 'sub', 0, 0, tiled=True)]
    unnamed x25 -> x2, local copies, waits for them, and re-layouts: 10.7 us -> 0.75 us
    all_to_all x1, starting transfers between devices: 13.8 us -> 5.17 us  [on_device(): dealt = lax.all_to_all(dealt, 'sub', 0, 0, tiled=True)]
    pallas_call x10, Pallas kernels: 16.8 us -> 24.7 us  [call(): pl.pallas_call(body, out_shape=[jax.ShapeDtypeStruct(shape, dtype) for sh...]
    ppermute x18, waiting for transfers between devices: 10 us -> 16.9 us  [exchange(): received[(b + 3) % BLOCKS] = lax.ppermute(blocks[b], 'sub', route)]
    ppermute x18, starting transfers between devices: 26.5 us -> 31.3 us  [exchange(): received[(b + 3) % BLOCKS] = lax.ppermute(blocks[b], 'sub', route)]
    all_to_all x1, blocking collectives: 6.65 us -> 8.6 us  [on_device(): parts = lax.all_to_all(parts, 'grp', 0, 0, tiled=True)]
    all_to_all x2, starting transfers between devices: 10.4 us -> 12.3 us  [the longest x1 7.41 us: on_device(): middle = lax.all_to_all(middle, 'sub', 0, 0, tiled=True)]
  transfers between devices with their start and end apart: 22 -> 22, of which waited for: 10 -> 7; matrix products, arithmetic and copies ran while one was open for 2% -> 3% of each run, Pallas kernels for 9% -> 13%
where the time goes in v1:
time: 120 us; the launch traced here: 119 us
  starting transfers between devices  56.1 us (47%)
  waiting for transfers between devices  25.4 us (21%)
  Pallas kernels  24.7 us (21%)
  blocking collectives  8.6 us (7%)
  other arithmetic  3.03 us (3%)
    ppermute x18, starting transfers between devices, exchange(): received[(b + 3) % BLOCKS] = lax.ppermute(blocks[b], 'sub', route)  31.3 us
    pallas_call x10, Pallas kernels, call(): pl.pallas_call(body, out_shape=[jax.ShapeDtypeStruct(shape, dtype) for sh...  24.7 us
    ppermute x18, waiting for transfers between devices, exchange(): received[(b + 3) % BLOCKS] = lax.ppermute(blocks[b], 'sub', route)  16.9 us
    all_to_all x1, blocking collectives, on_device(): parts = lax.all_to_all(parts, 'grp', 0, 0, tiled=True)  8.6 us
    all_to_all x1, waiting for transfers between devices, on_device(): corner_in = lax.all_to_all(corner_in, 'sub', 0, 0, tiled=True)  8.47 us
    all_to_all x1, starting transfers between devices, on_device(): middle = lax.all_to_all(middle, 'sub', 0, 0, tiled=True)  7.41 us
    all_to_all x1, starting transfers between devices, on_device(): corner_in = lax.all_to_all(corner_in, 'sub', 0, 0, tiled=True)  7.41 us
    all_to_all x1, starting transfers between devices, on_device(): dealt = lax.all_to_all(dealt, 'sub', 0, 0, tiled=True)  5.17 us
  transfers between devices with their start and end apart: 22, of which 7 were waited for; matrix products, arithmetic and copies ran while one was open for 3% of the time, Pallas kernels for 13%

profile of v1, /device:TPU:1, one launch (start us, length us, event | category | flops | bytes accessed | tf_op | source)
XLA Modules:
  0.0 119.3 jit_solution(13190908731850887140)
XLA Ops:
  2.1 4.8 %all-to-all-start = ((bf16[4,8,2048]{2,1,0:T(8,128)(2,1)}), bf16[4,8,2048]{2,1,0:T(8,128)(2,1)S(1)}, u32[]{:S(2)}, u32[]{:S(2)}) async-start(bf16[4,8,2048]{2,1,0:T(8,128)(2,1)} %shard_map.104), calls=%async_computation | async-start | bytes 262144 | tf_op jit(solution)/shard_map/all_to_all | solution.py:395
  10.9 1.8 %collective-permute-start = (bf16[64,256]{1,0:T(8,128)(2,1)S(1)}, bf16[64,256]{1,0:T(8,128)(2,1)S(1)}, u32[]{:S(2)}, u32[]{:S(2)}) collective-permute-start(bf16[64,256]{1,0:T(8,128)(2,1)S(1)} %get-tuple-element.48), channel_id=1, source_target_pairs={{0,252},{4,0},{8,4},{12,8},{16,12},{20,16},{24,20},{28,24},{32,28}... | collective-permute-start | bytes 98312 | tf_op jit(solution)/shard_map/ppermute | solution.py:356
  12.7 7.3 %collective-permute-start.1 = (bf16[64,256]{1,0:T(8,128)(2,1)S(1)}, bf16[64,256]{1,0:T(8,128)(2,1)S(1)}, u32[]{:S(2)}, u32[]{:S(2)}) collective-permute-start(bf16[64,256]{1,0:T(8,128)(2,1)S(1)} %get-tuple-element.49), channel_id=1, source_target_pairs={{0,248},{4,252},{8,0},{12,4},{16,8},{20,12},{24,16},{28,20},{32,24... | collective-permute-start | bytes 98312 | tf_op jit(solution)/shard_map/ppermute | solution.py:356
  21.6 2.2 %collective-permute-start.5 = (bf16[64,256]{1,0:T(8,128)(2,1)S(1)}, bf16[64,256]{1,0:T(8,128)(2,1)S(1)}, u32[]{:S(2)}, u32[]{:S(2)}) collective-permute-start(bf16[64,256]{1,0:T(8,128)(2,1)S(1)} %get-tuple-element.53), channel_id=1, source_target_pairs={{0,20},{4,24},{8,28},{12,32},{16,36},{20,40},{24,44},{28,48},{32,5... | collective-permute-start | bytes 98312 | tf_op jit(solution)/shard_map/ppermute | solution.py:356
  24.8 2.3 %collective-permute-done.4.refs_4_.refs_10_ = bf16[64,256]{1,0:T(8,128)(2,1)S(1)} collective-permute-done((bf16[64,256]{1,0:T(8,128)(2,1)S(1)}, bf16[64,256]{1,0:T(8,128)(2,1)S(1)}, u32[]{:S(2)}, u32[]{:S(2)}) %collective-permute-start.4) | collective-permute-done | bytes 32800 | tf_op jit(solution)/shard_map/ppermute | solution.py:356
  27.1 1.6 %collective-permute-done.5.refs_5_.refs_11_ = bf16[64,256]{1,0:T(8,128)(2,1)S(1)} collective-permute-done((bf16[64,256]{1,0:T(8,128)(2,1)S(1)}, bf16[64,256]{1,0:T(8,128)(2,1)S(1)}, u32[]{:S(2)}, u32[]{:S(2)}) %collective-permute-start.5) | collective-permute-done | bytes 32800 | tf_op jit(solution)/shard_map/ppermute | solution.py:356
  28.7 5.2 %all-to-all-start.1 = ((bf16[64,8,256]{2,1,0:T(8,128)(2,1)}), bf16[64,8,256]{2,1,0:T(8,128)(2,1)S(1)}, u32[]{:S(2)}, u32[]{:S(2)}) async-start(bf16[64,8,256]{2,1,0:T(8,128)(2,1)} %shard_map.105), calls=%async_computation.1 | async-start | bytes 524288 | tf_op jit(solution)/shard_map/all_to_all | solution.py:402
  33.8 6.3 %shard_map.107 = (f32[32,1536]{1,0:T(8,128)S(1)}, bf16[32,1536]{1,0:T(8,128)(2,1)S(1)}, f32[8,1536]{1,0:T(8,128)S(1)}, f32[8,32]{1,0:T(8,128)S(1)}, bf16[32,256]...) custom-call(bf16[64,256]{1,0:T(8,128)(2,1)S(1)} %collective-permute-, ...), custom_call_target="tpu_custom_call" | custom-call | flops 16777216 | bytes 16777216 | tf_op jit(solution)/shard_map/pallas_call | solution.py:62
  40.7 4.9 %collective-permute-start.7 = (bf16[32,256]{1,0:T(8,128)(2,1)S(1)}, bf16[32,256]{1,0:T(8,128)(2,1)S(1)}, u32[]{:S(2)}, u32[]{:S(2)}) collective-permute-start(bf16[32,256]{1,0:T(8,128)(2,1)S(1)} %get-tuple-element.61), channel_id=1, source_target_pairs={{0,248},{4,252},{8,0},{12,4},{16,8},{20,12},{24,16},{28,20},{32,24... | collective-permute-start | bytes 49160 | tf_op jit(solution)/shard_map/ppermute | solution.py:356
  45.6 1.0 collective-permute-start.8
  47.3 2.7 %collective-permute-start.11 = (bf16[32,256]{1,0:T(8,128)(2,1)S(1)}, bf16[32,256]{1,0:T(8,128)(2,1)S(1)}, u32[]{:S(2)}, u32[]{:S(2)}) collective-permute-start(bf16[32,256]{1,0:T(8,128)(2,1)S(1)} %get-tuple-element.65), channel_id=1, source_target_pairs={{0,20},{4,24},{8,28},{12,32},{16,36},{20,40},{24,44},{28,48},{32,5... | collective-permute-start | bytes 49160 | tf_op jit(solution)/shard_map/ppermute | solution.py:356
  50.0 1.8 %shard_map.108 = (bf16[512,128]{1,0:T(8,128)(2,1)S(1)}, bf16[64,8,128]{2,1,0:T(8,128)(2,1)S(1)}) custom-call(bf16[64,8,256]{2,1,0:T(8,128)(2,1)S(1)} %all-to-all-done.1.dealt_ref), custom_call_target="tpu_custom_call" | custom-call | flops 8388608 | bytes 8388608 | tf_op jit(solution)/shard_map/pallas_call | solution.py:62
  51.9 1.3 %collective-permute-done.10.refs_4_ = bf16[32,256]{1,0:T(8,128)(2,1)S(1)} collective-permute-done((bf16[32,256]{1,0:T(8,128)(2,1)S(1)}, bf16[32,256]{1,0:T(8,128)(2,1)S(1)}, u32[]{:S(2)}, u32[]{:S(2)}) %collective-permute-start.10) | collective-permute-done | bytes 16416 | tf_op jit(solution)/shard_map/ppermute | solution.py:356
  54.1 4.2 %shard_map.109 = (f32[32,1536]{1,0:T(8,128)S(1)}, bf16[32,1536]{1,0:T(8,128)(2,1)S(1)}, bf16[64,8,256]{2,1,0:T(8,128)(2,1)}) custom-call(bf16[32,256]{1,0:T(8,128)(2,1)S(1)} %collective-permute-done.6.refs_0_, bf16[32,256]{1,0:T(8,128)(2,1)S(1)} %collective-permute-done.7.refs_1_, bf16[32,256]{1,0:T(8,128)(2,1)S(1)} %collective-permute-done.8.refs_2_, ...), custom_call_target="tpu_custom_call" | custom-call | flops 16777216 | bytes 16777216 | tf_op jit(solution)/shard_map/pallas_call | solution.py:62
  58.2 7.4 %all-to-all-start.2 = ((bf16[64,8,256]{2,1,0:T(8,128)(2,1)}), bf16[64,8,256]{2,1,0:T(8,128)(2,1)S(1)}, u32[]{:S(2)}, u32[]{:S(2)}) async-start(bf16[64,8,256]{2,1,0:T(8,128)(2,1)} %get-tuple-element.71), calls=%async_computation.2 | async-start | bytes 524288 | tf_op jit(solution)/shard_map/all_to_all | solution.py:438
  65.6 4.7 %shard_map.110 = (bf16[32,1536]{1,0:T(8,128)(2,1)S(1)}, bf16[32,256]{1,0:T(8,128)(2,1)S(1)}, bf16[32,256]{1,0:T(8,128)(2,1)S(1)}, bf16[32,256]{1,0:T(8,128)(2,1)...) custom-call(f32[32,1536]{1,0:T(8,128)S(1)} %get-tuple-element.73.direction_ref.refs_19_,, ...), custom_call_target="tpu_custom_call" | custom-call | flops 8388608 | bytes 8388608 | tf_op jit(solution)/shard_map/pallas_call | solution.py:62
  70.3 8.5 %all-to-all-done.2.corner_ref.refs_14_ = bf16[64,8,256]{2,1,0:T(8,128)(2,1)S(1)} async-done(((bf16[64,8,256]{2,1,0:T(8,128)(2,1)}), bf16[64,8,256]{2,1,0:T(8,128)(2,1)S(1)}, u32[]{:S(2)}, u32[]{:S(2)}) %all-to-all-start.2) | async-done | bytes 262176 | tf_op jit(solution)/shard_map/all_to_all | solution.py:438
  79.5 8.6 %all_to_all.25.parts_ref = f32[4,16,128]{2,1,0:T(8,128)S(1)} all-to-all(f32[4,16,128]{2,1,0:T(8,128)S(1)} %get-tuple-element.87), channel_id=1, replica_groups=mesh['sub'=64,'grp'=4] {'grp'}, dimensions={0} | all-to-all | bytes 65536 | tf_op jit(solution)/shard_map/all_to_all | solution.py:459
  88.8 7.4 %all-to-all-start.4 = ((bf16[64,8,128]{2,1,0:T(8,128)(2,1)}), bf16[64,8,128]{2,1,0:T(8,128)(2,1)S(1)}, u32[]{:S(2)}, u32[]{:S(2)}) async-start(bf16[64,8,128]{2,1,0:T(8,128)(2,1)} %get-tuple-element.88), calls=%async_computation.4 | async-start | bytes 262144 | tf_op jit(solution)/shard_map/all_to_all | solution.py:464
  96.2 5.1 %collective-permute-start.13 = (bf16[288,256]{1,0:T(8,128)(2,1)S(1)}, bf16[288,256]{1,0:T(8,128)(2,1)S(1)}, u32[]{:S(2)}, u32[]{:S(2)}) collective-permute-start(bf16[288,256]{1,0:T(8,128)(2,1)S(1)} %get-tuple-element.82), channel_id=1, source_target_pairs={{0,248},{4,252},{8,0},{12,4},{16,8},{20,12},{24,16},{28,20},{32,24... | collective-permute-start | bytes 442376 | tf_op jit(solution)/shard_map/ppermute | solution.py:356
  101.3 1.1 collective-permute-start.14
  103.0 1.3 %collective-permute-start.17 = (bf16[288,256]{1,0:T(8,128)(2,1)S(1)}, bf16[288,256]{1,0:T(8,128)(2,1)S(1)}, u32[]{:S(2)}, u32[]{:S(2)}) collective-permute-start(bf16[288,256]{1,0:T(8,128)(2,1)S(1)} %get-tuple-element.86), channel_id=1, source_target_pairs={{0,20},{4,24},{8,28},{12,32},{16,36},{20,40},{24,44},{28,48},{32,5... | collective-permute-start | bytes 442376 | tf_op jit(solution)/shard_map/ppermute | solution.py:356
  104.3 10.8 %collective-permute-done.14.refs_2_ = bf16[288,256]{1,0:T(8,128)(2,1)S(1)} collective-permute-done((bf16[288,256]{1,0:T(8,128)(2,1)S(1)}, bf16[288,256]{1,0:T(8,128)(2,1)S(1)}, u32[]{:S(2)}, u32[]{:S(2)}) %collective-permute-start.14) | collective-permute-done | bytes 147488 | tf_op jit(solution)/shard_map/ppermute | solution.py:356
  115.1 4.2 %shard_map.113 = (f32[32,1536]{1,0:T(8,128)}, f32[32,1536]{1,0:T(8,128)}) custom-call(bf16[288,256]{1,0:T(8,128)(2,1)S(1)} %collective-permute-done.12.refs_0_, bf16[288,256]{1,0:T(8,128)(2,1)S(1)} %collective-permute-done.13.refs_1_, bf16[288,256]{1,0:T(8,128)(2,1)S(1)} %collective-permute-done.14.refs_2_, ...), custom_call_target="tpu_custom_call" | custom-call | flops 8388608 | bytes 8388608 | tf_op jit(solution)/shard_map/pallas_call | solution.py:62
  (37 shorter events, 12.2 us)
Async XLA Ops:
  0.6 0.8 copy-start
  2.1 21.8 %all-to-all-start = ((bf16[4,8,2048]{2,1,0:T(8,128)(2,1)}), bf16[4,8,2048]{2,1,0:T(8,128)(2,1)S(1)}, u32[]{:S(2)}, u32[]{:S(2)}) async-start(bf16[4,8,2048]{2,1,0:T(8,128)(2,1)} %shard_map.104), calls=%async_computation | async-start | bytes 262144 | tf_op jit(solution)/shard_map/all_to_all | solution.py:395
  10.9 10.7 %collective-permute-start = (bf16[64,256]{1,0:T(8,128)(2,1)S(1)}, bf16[64,256]{1,0:T(8,128)(2,1)S(1)}, u32[]{:S(2)}, u32[]{:S(2)}) collective-permute-start(bf16[64,256]{1,0:T(8,128)(2,1)S(1)} %get-tuple-element.48), channel_id=1, source_target_pairs={{0,252},{4,0},{8,4},{12,8},{16,12},{20,16},{24,20},{28,24},{32,28}... | collective-permute-start | bytes 98312 | tf_op jit(solution)/shard_map/ppermute | solution.py:356
  12.7 12.0 %collective-permute-start.1 = (bf16[64,256]{1,0:T(8,128)(2,1)S(1)}, bf16[64,256]{1,0:T(8,128)(2,1)S(1)}, u32[]{:S(2)}, u32[]{:S(2)}) collective-permute-start(bf16[64,256]{1,0:T(8,128)(2,1)S(1)} %get-tuple-element.49), channel_id=1, source_target_pairs={{0,248},{4,252},{8,0},{12,4},{16,8},{20,12},{24,16},{28,20},{32,24... | collective-permute-start | bytes 98312 | tf_op jit(solution)/shard_map/ppermute | solution.py:356
  20.0 4.9 %collective-permute-start.2 = (bf16[64,256]{1,0:T(8,128)(2,1)S(1)}, bf16[64,256]{1,0:T(8,128)(2,1)S(1)}, u32[]{:S(2)}, u32[]{:S(2)}) collective-permute-start(bf16[64,256]{1,0:T(8,128)(2,1)S(1)} %get-tuple-element.50), channel_id=1, source_target_pairs={{0,236},{4,240},{8,244},{12,248},{16,252},{20,0},{24,4},{28,8},{32... | collective-permute-start | bytes 98312 | tf_op jit(solution)/shard_map/ppermute | solution.py:356
  20.5 4.3 %collective-permute-start.3 = (bf16[64,256]{1,0:T(8,128)(2,1)S(1)}, bf16[64,256]{1,0:T(8,128)(2,1)S(1)}, u32[]{:S(2)}, u32[]{:S(2)}) collective-permute-start(bf16[64,256]{1,0:T(8,128)(2,1)S(1)} %get-tuple-element.51), channel_id=1, source_target_pairs={{0,4},{4,8},{8,12},{12,16},{16,20},{20,24},{24,28},{28,32},{32,36}... | collective-permute-start | bytes 98312 | tf_op jit(solution)/shard_map/ppermute | solution.py:356
  21.0 6.1 %collective-permute-start.4 = (bf16[64,256]{1,0:T(8,128)(2,1)S(1)}, bf16[64,256]{1,0:T(8,128)(2,1)S(1)}, u32[]{:S(2)}, u32[]{:S(2)}) collective-permute-start(bf16[64,256]{1,0:T(8,128)(2,1)S(1)} %get-tuple-element.52), channel_id=1, source_target_pairs={{0,8},{4,12},{8,16},{12,20},{16,24},{20,28},{24,32},{28,36},{32,40... | collective-permute-start | bytes 98312 | tf_op jit(solution)/shard_map/ppermute | solution.py:356
  21.6 7.1 %collective-permute-start.5 = (bf16[64,256]{1,0:T(8,128)(2,1)S(1)}, bf16[64,256]{1,0:T(8,128)(2,1)S(1)}, u32[]{:S(2)}, u32[]{:S(2)}) collective-permute-start(bf16[64,256]{1,0:T(8,128)(2,1)S(1)} %get-tuple-element.53), channel_id=1, source_target_pairs={{0,20},{4,24},{8,28},{12,32},{16,36},{20,40},{24,44},{28,48},{32,5... | collective-permute-start | bytes 98312 | tf_op jit(solution)/shard_map/ppermute | solution.py:356
  28.7 21.4 %all-to-all-start.1 = ((bf16[64,8,256]{2,1,0:T(8,128)(2,1)}), bf16[64,8,256]{2,1,0:T(8,128)(2,1)S(1)}, u32[]{:S(2)}, u32[]{:S(2)}) async-start(bf16[64,8,256]{2,1,0:T(8,128)(2,1)} %shard_map.105), calls=%async_computation.1 | async-start | bytes 524288 | tf_op jit(solution)/shard_map/all_to_all | solution.py:402
  40.1 7.2 %collective-permute-start.6 = (bf16[32,256]{1,0:T(8,128)(2,1)S(1)}, bf16[32,256]{1,0:T(8,128)(2,1)S(1)}, u32[]{:S(2)}, u32[]{:S(2)}) collective-permute-start(bf16[32,256]{1,0:T(8,128)(2,1)S(1)} %get-tuple-element.60), channel_id=1, source_target_pairs={{0,252},{4,0},{8,4},{12,8},{16,12},{20,16},{24,20},{28,24},{32,28}... | collective-permute-start | bytes 49160 | tf_op jit(solution)/shard_map/ppermute | solution.py:356
  40.7 11.2 %collective-permute-start.7 = (bf16[32,256]{1,0:T(8,128)(2,1)S(1)}, bf16[32,256]{1,0:T(8,128)(2,1)S(1)}, u32[]{:S(2)}, u32[]{:S(2)}) collective-permute-start(bf16[32,256]{1,0:T(8,128)(2,1)S(1)} %get-tuple-element.61), channel_id=1, source_target_pairs={{0,248},{4,252},{8,0},{12,4},{16,8},{20,12},{24,16},{28,20},{32,24... | collective-permute-start | bytes 49160 | tf_op jit(solution)/shard_map/ppermute | solution.py:356
  45.6 6.3 %collective-permute-start.8 = (bf16[32,256]{1,0:T(8,128)(2,1)S(1)}, bf16[32,256]{1,0:T(8,128)(2,1)S(1)}, u32[]{:S(2)}, u32[]{:S(2)}) collective-permute-start(bf16[32,256]{1,0:T(8,128)(2,1)S(1)} %get-tuple-element.62), channel_id=1, source_target_pairs={{0,236},{4,240},{8,244},{12,248},{16,252},{20,0},{24,4},{28,8},{32... | collective-permute-start | bytes 49160 | tf_op jit(solution)/shard_map/ppermute | solution.py:356
  46.6 5.3 %collective-permute-start.9 = (bf16[32,256]{1,0:T(8,128)(2,1)S(1)}, bf16[32,256]{1,0:T(8,128)(2,1)S(1)}, u32[]{:S(2)}, u32[]{:S(2)}) collective-permute-start(bf16[32,256]{1,0:T(8,128)(2,1)S(1)} %get-tuple-element.63), channel_id=1, source_target_pairs={{0,4},{4,8},{8,12},{12,16},{16,20},{20,24},{24,28},{28,32},{32,36}... | collective-permute-start | bytes 49160 | tf_op jit(solution)/shard_map/ppermute | solution.py:356
  47.2 5.9 %collective-permute-start.10 = (bf16[32,256]{1,0:T(8,128)(2,1)S(1)}, bf16[32,256]{1,0:T(8,128)(2,1)S(1)}, u32[]{:S(2)}, u32[]{:S(2)}) collective-permute-start(bf16[32,256]{1,0:T(8,128)(2,1)S(1)} %get-tuple-element.64), channel_id=1, source_target_pairs={{0,8},{4,12},{8,16},{12,20},{16,24},{20,28},{24,32},{28,36},{32,40... | collective-permute-start | bytes 49160 | tf_op jit(solution)/shard_map/ppermute | solution.py:356
  47.3 6.8 %collective-permute-start.11 = (bf16[32,256]{1,0:T(8,128)(2,1)S(1)}, bf16[32,256]{1,0:T(8,128)(2,1)S(1)}, u32[]{:S(2)}, u32[]{:S(2)}) collective-permute-start(bf16[32,256]{1,0:T(8,128)(2,1)S(1)} %get-tuple-element.65), channel_id=1, source_target_pairs={{0,20},{4,24},{8,28},{12,32},{16,36},{20,40},{24,44},{28,48},{32,5... | collective-permute-start | bytes 49160 | tf_op jit(solution)/shard_map/ppermute | solution.py:356
  58.2 20.6 %all-to-all-start.2 = ((bf16[64,8,256]{2,1,0:T(8,128)(2,1)}), bf16[64,8,256]{2,1,0:T(8,128)(2,1)S(1)}, u32[]{:S(2)}, u32[]{:S(2)}) async-start(bf16[64,8,256]{2,1,0:T(8,128)(2,1)} %get-tuple-element.71), calls=%async_computation.2 | async-start | bytes 524288 | tf_op jit(solution)/shard_map/all_to_all | solution.py:438
  79.2 23.8 %collective-permute-start.12 = (bf16[288,256]{1,0:T(8,128)(2,1)S(1)}, bf16[288,256]{1,0:T(8,128)(2,1)S(1)}, u32[]{:S(2)}, u32[]{:S(2)}) collective-permute-start(bf16[288,256]{1,0:T(8,128)(2,1)S(1)} %get-tuple-element.81), channel_id=1, source_target_pairs={{0,252},{4,0},{8,4},{12,8},{16,12},{20,16},{24,20},{28,24},{32,28}... | collective-permute-start | bytes 442376 | tf_op jit(solution)/shard_map/ppermute | solution.py:356
  88.8 26.3 %all-to-all-start.4 = ((bf16[64,8,128]{2,1,0:T(8,128)(2,1)}), bf16[64,8,128]{2,1,0:T(8,128)(2,1)S(1)}, u32[]{:S(2)}, u32[]{:S(2)}) async-start(bf16[64,8,128]{2,1,0:T(8,128)(2,1)} %get-tuple-element.88), calls=%async_computation.4 | async-start | bytes 262144 | tf_op jit(solution)/shard_map/all_to_all | solution.py:464
  96.2 8.1 %collective-permute-start.13 = (bf16[288,256]{1,0:T(8,128)(2,1)S(1)}, bf16[288,256]{1,0:T(8,128)(2,1)S(1)}, u32[]{:S(2)}, u32[]{:S(2)}) collective-permute-start(bf16[288,256]{1,0:T(8,128)(2,1)S(1)} %get-tuple-element.82), channel_id=1, source_target_pairs={{0,248},{4,252},{8,0},{12,4},{16,8},{20,12},{24,16},{28,20},{32,24... | collective-permute-start | bytes 442376 | tf_op jit(solution)/shard_map/ppermute | solution.py:356
  101.3 13.8 %collective-permute-start.14 = (bf16[288,256]{1,0:T(8,128)(2,1)S(1)}, bf16[288,256]{1,0:T(8,128)(2,1)S(1)}, u32[]{:S(2)}, u32[]{:S(2)}) collective-permute-start(bf16[288,256]{1,0:T(8,128)(2,1)S(1)} %get-tuple-element.83), channel_id=1, source_target_pairs={{0,236},{4,240},{8,244},{12,248},{16,252},{20,0},{24,4},{28,8},{32... | collective-permute-start | bytes 442376 | tf_op jit(solution)/shard_map/ppermute | solution.py:356
  102.3 12.7 %collective-permute-start.15 = (bf16[288,256]{1,0:T(8,128)(2,1)S(1)}, bf16[288,256]{1,0:T(8,128)(2,1)S(1)}, u32[]{:S(2)}, u32[]{:S(2)}) collective-permute-start(bf16[288,256]{1,0:T(8,128)(2,1)S(1)} %get-tuple-element.84), channel_id=1, source_target_pairs={{0,4},{4,8},{8,12},{12,16},{16,20},{20,24},{24,28},{28,32},{32,36}... | collective-permute-start | bytes 442376 | tf_op jit(solution)/shard_map/ppermute | solution.py:356
  102.3 12.7 %collective-permute-start.16 = (bf16[288,256]{1,0:T(8,128)(2,1)S(1)}, bf16[288,256]{1,0:T(8,128)(2,1)S(1)}, u32[]{:S(2)}, u32[]{:S(2)}) collective-permute-start(bf16[288,256]{1,0:T(8,128)(2,1)S(1)} %get-tuple-element.85), channel_id=1, source_target_pairs={{0,8},{4,12},{8,16},{12,20},{16,24},{20,28},{24,32},{28,36},{32,40... | collective-permute-start | bytes 442376 | tf_op jit(solution)/shard_map/ppermute | solution.py:356
  103.0 12.1 %collective-permute-start.17 = (bf16[288,256]{1,0:T(8,128)(2,1)S(1)}, bf16[288,256]{1,0:T(8,128)(2,1)S(1)}, u32[]{:S(2)}, u32[]{:S(2)}) collective-permute-start(bf16[288,256]{1,0:T(8,128)(2,1)S(1)} %get-tuple-element.86), channel_id=1, source_target_pairs={{0,20},{4,24},{8,28},{12,32},{16,36},{20,40},{24,44},{28,48},{32,5... | collective-permute-start | bytes 442376 | tf_op jit(solution)/shard_map/ppermute | solution.py:356

commit v2 on v1

v2 whole, which is shorter than its diff:
```python
import jax
import jax.numpy as jnp
from jax import lax
from jax.experimental import pallas as pl
from jax.experimental.pallas import tpu as pltpu
from jax.sharding import PartitionSpec as P

OFFSETS = (1, 2, 5, -1, -2, -5)
BLOCKS = len(OFFSETS)
F32 = jnp.float32
BF16 = jnp.bfloat16
LANES = 128
PIECES = 3
TABLE, DIR_DIAG, SCHUR_DIAG, CORNER_ROW = 0, 1, 2, 3


def dot_nn(a, b):
    return jnp.dot(a, b, preferred_element_type=F32)


def dot_nt(a, b):
    return lax.dot_general(a, b, (((1,), (1,)), ((), ())), preferred_element_type=F32)


def dot_tn(a, b):
    return lax.dot_general(a, b, (((0,), (0,)), ((), ())), preferred_element_type=F32)


def column_to_row(column):
    n = column.shape[0]
    same = lax.broadcasted_iota(jnp.int32, (n, n), 0) == lax.broadcasted_iota(jnp.int32, (n, n), 1)
    return jnp.sum(jnp.where(same, column, 0.0), axis=0, keepdims=True)


def row_to_column(row):
    n = row.shape[1]
    same = lax.broadcasted_iota(jnp.int32, (n, n), 0) == lax.broadcasted_iota(jnp.int32, (n, n), 1)
    return jnp.sum(jnp.where(same, row, 0.0), axis=1, keepdims=True)


def three_parts(value):
    first = value.astype(BF16).astype(F32)
    rest = value - first
    second = rest.astype(BF16).astype(F32)
    third = (rest - second).astype(BF16).astype(F32)
    return [first, second, third]


def fold_rows(rows):
    n = rows.shape[0] // 4
    return jnp.concatenate([rows[n * i : n * i + n] for i in range(4)], axis=1)


def unfold_rows(tile):
    n = tile.shape[1] // 4
    return jnp.concatenate([tile[:, n * i : n * i + n] for i in range(4)], axis=0)


def call(body, outs, weight, *args, scratch=(), in_hbm=(), vmem=20):
    in_vmem = pl.BlockSpec(memory_space=pltpu.VMEM)
    left = pl.BlockSpec(memory_space=pltpu.HBM)
    return pl.pallas_call(
        body,
        out_shape=[jax.ShapeDtypeStruct(shape, dtype) for shape, dtype in outs],
        in_specs=[left if i in in_hbm else in_vmem for i in range(len(args))],
        out_specs=[in_vmem] * len(outs),
        scratch_shapes=list(scratch),
        compiler_params=pltpu.CompilerParams(vmem_limit_bytes=vmem * 1024 * 1024),
        cost_estimate=pl.CostEstimate(
            flops=weight << 20, bytes_accessed=weight << 20, transcendentals=0
        ),
    )(*args)


def slot_block(rows_ref, b, interface):
    cap = rows_ref.shape[1] // BLOCKS
    rows = lax.broadcasted_iota(jnp.int32, (interface, cap), 0).astype(F32)
    named = rows == rows_ref[TABLE : TABLE + 1, b * cap : (b + 1) * cap]
    return jnp.where(named, 1.0, 0.0).astype(BF16)


def from_slots(values, rows_ref, b):
    return dot_nn(values, slot_block(rows_ref, b, values.shape[1])).astype(BF16)


def to_slots(blocks, rows_ref, interface):
    total = dot_nt(blocks[0], slot_block(rows_ref, 0, interface))
    for b in range(1, BLOCKS):
        total = total + dot_nt(blocks[b], slot_block(rows_ref, b, interface))
    return total


def first_exchange_body(rows_ref, fields_ref, *block_refs):
    values = fields_ref[: block_refs[0].shape[0]]
    for b in range(BLOCKS):
        block_refs[b][...] = from_slots(values, rows_ref, b)


def load_factor(factor_ref, held_ref, semaphores):
    size = held_ref.shape[0] // PIECES
    copies = []
    for i in range(PIECES):
        piece = pl.ds(size * i, size)
        copies.append(
            pltpu.make_async_copy(factor_ref.at[piece], held_ref.at[piece], semaphores.at[i])
        )
        copies[i].start()
    return copies


def times_factor(operand, held_ref, copies):
    size = held_ref.shape[0] // PIECES
    total = None
    for i in range(PIECES):
        copies[i].wait()
        part = dot_nn(operand[:, size * i : size * i + size], held_ref[size * i : size * i + size])
        total = part if total is None else total + part
    return total


def dirichlet_body(*refs):
    rows_ref, fields_ref, factor_ref = refs[BLOCKS : BLOCKS + 3]
    residual_ref, out_ref, live_ref, rho_ref, *block_refs = refs[BLOCKS + 3 : -3]
    slots_ref, held_ref, semaphores = refs[-3:]
    copies = load_factor(factor_ref, held_ref, semaphores)
    cases, interface = residual_ref.shape
    cap = block_refs[0].shape[1]
    ones = jnp.ones((16, cap), BF16)
    spread = jnp.zeros((cases + 16, interface), F32)
    for b in range(BLOCKS):
        block = slot_block(rows_ref, b, interface)
        slots_ref[:, b * cap : (b + 1) * cap] = block
        spread = spread + dot_nt(jnp.concatenate([refs[b][:cases], ones], axis=0), block)
    live = spread[cases : cases + 8]
    residual = live[0:1] * (fields_ref[:cases].astype(F32) - spread[:cases])
    middle = times_factor(residual.astype(BF16), held_ref, copies).astype(BF16)
    diag = rows_ref[DIR_DIAG : DIR_DIAG + 1]
    out = (0.5 * (diag * residual + dot_nt(middle, held_ref[...]))).astype(BF16)
    for b in range(BLOCKS):
        block_refs[b][...] = dot_nn(out, slots_ref[:, b * cap : (b + 1) * cap]).astype(BF16)
    live_ref[...] = live
    residual_ref[...] = residual
    out_ref[...] = out
    rho = column_to_row(jnp.sum(residual * out.astype(F32), axis=1, keepdims=True))
    rho_ref[...] = jnp.broadcast_to(rho, rho_ref.shape)


def schur_first_body(*refs):
    out_ref, live_ref, rho_ref, rows_ref, fields_ref, dealt_ref, factor_ref = refs[
        BLOCKS : BLOCKS + 7
    ]
    direction_ref, middle_ref, send_ref, held_ref, semaphores = refs[BLOCKS + 7 :]
    copies = load_factor(factor_ref, held_ref, semaphores)
    received = to_slots([ref[...] for ref in refs[:BLOCKS]], rows_ref, out_ref.shape[1])
    direction = 0.5 * (live_ref[0:1] * (out_ref[...].astype(F32) - received))
    direction_ref[...] = direction
    operand = direction.astype(BF16)
    wide = times_factor(operand, held_ref, copies)
    middle = wide.astype(BF16)
    middle_ref[...] = middle
    diag = rows_ref[SCHUR_DIAG : SCHUR_DIAG + 1]
    curve = jnp.sum(diag * direction * direction, axis=1, keepdims=True)
    curve = curve + jnp.sum(wide * middle.astype(F32), axis=1, keepdims=True)
    cases = operand.shape[0]
    corner_in = dot_nt(fields_ref[cases : cases + 24], operand)
    rho_parts, curve_parts = three_parts(rho_ref[0:1]), three_parts(column_to_row(curve))
    extra = extra_lanes(rho_parts + curve_parts, rows_ref[CORNER_ROW : CORNER_ROW + 1, :LANES])
    groups = [corner_in[0:8], corner_in[8:16], corner_in[16:24], extra]
    tile = jnp.concatenate(groups, axis=1).astype(BF16)
    count, depth, _ = send_ref.shape
    send_ref[:, :, :LANES] = jnp.broadcast_to(tile[None], (count, depth, LANES))
    send_ref[:, :, LANES:] = dealt_ref[...]


def schur_second_body(
    direction_ref, middle_ref, rows_ref, factor_ref, local_ref, held_ref, semaphores
):
    for copy in load_factor(factor_ref, held_ref, semaphores):
        copy.wait()
    back = dot_nt(middle_ref[...], held_ref[...])
    local_ref[...] = rows_ref[SCHUR_DIAG : SCHUR_DIAG + 1] * direction_ref[...] + back


def extra_lanes(parts, corner_row):
    cases, corners = parts[0].shape[1], corner_row.shape[1]
    row = lax.broadcasted_iota(jnp.int32, (8, corners), 0)
    lane = lax.broadcasted_iota(jnp.int32, (8, corners), 1)
    near = lax.broadcasted_iota(jnp.int32, (8, cases), 0)
    far = lax.broadcasted_iota(jnp.int32, (8, cases), 1)
    place = lax.broadcasted_iota(jnp.int32, (8, 32), 1)
    tile = jnp.zeros((8, 32), F32)
    for q in range(3):
        mine = jnp.where(lane == 8 * q + row, corner_row, 0.0)
        value = jnp.sum(mine, axis=1, keepdims=True).astype(jnp.int32)
        tile = jnp.where(place == 2 * q, (value // 8).astype(F32), tile)
        tile = jnp.where(place == 2 * q + 1, (value % 8).astype(F32), tile)
    for p, part in enumerate(parts):
        for j in range(4):
            value = jnp.sum(jnp.where(far == 4 * near + j, part, 0.0), axis=1, keepdims=True)
            tile = jnp.where(place == 8 + 4 * p + j, value, tile)
    return tile


def part_row(tile, p, cases):
    near = lax.broadcasted_iota(jnp.int32, (8, cases), 0)
    far = lax.broadcasted_iota(jnp.int32, (8, cases), 1)
    total = jnp.zeros((8, cases), F32)
    for j in range(4):
        lane = 96 + 8 + 4 * p + j
        total = jnp.where(far == 4 * near + j, tile[:, lane : lane + 1], total)
    return jnp.sum(total, axis=0, keepdims=True)


def deal_columns_body(own_ref, one_ref, two_ref, three_ref, send_ref):
    rows = [ref[...].astype(F32) for ref in (own_ref, one_ref, two_ref, three_ref)]
    depth, lanes = rows[0].shape
    group = lax.broadcasted_iota(jnp.int32, (depth, lanes), 1) // 32 % 4
    for t in range(4):
        dealt = jnp.zeros((depth, lanes), F32)
        for a in range(4):
            shift = (32 * (a - t)) % lanes
            moved = pltpu.roll(rows[a], shift, 1) if shift else rows[a]
            dealt = jnp.where(group == a, moved, dealt)
        for quad in range(lanes // LANES):
            tile = dealt[:, quad * LANES : (quad + 1) * LANES]
            send_ref[4 * quad + t] = tile.astype(BF16)


def coarse_first_body(sent_ref, picked_ref, send_ref):
    count, depth, _ = sent_ref.shape
    size = count * depth
    sent = sent_ref[...].astype(F32)
    tiles = sent[:, :, :LANES]
    corner = tiles.reshape(size, LANES)
    columns = sent[:, :, LANES:].reshape(size, LANES).astype(BF16)
    place = lax.broadcasted_iota(jnp.int32, (size, size), 1).astype(F32)
    lane_group = (lax.broadcasted_iota(jnp.int32, (size, LANES), 1) // 32).astype(F32)
    near = lax.broadcasted_iota(jnp.int32, (LANES, LANES), 0)
    far = lax.broadcasted_iota(jnp.int32, (LANES, LANES), 1)
    total = jnp.zeros((size, LANES), F32)
    for q in range(3):
        upper, lower = corner[:, 96 + 2 * q : 97 + 2 * q], corner[:, 97 + 2 * q : 98 + 2 * q]
        member = jnp.floor(upper * 0.25)
        onehot = jnp.where(place == member * 8.0 + lower, 1.0, 0.0).astype(BF16)
        rows = dot_nn(onehot, columns)
        rows = jnp.where(lane_group == upper - 4.0 * member, rows, 0.0).astype(BF16)
        fold = jnp.where((near % 32 == far % 32) & (far // 32 == q), 1.0, 0.0).astype(BF16)
        total = total + dot_nn(rows, fold)
    picked = total.astype(BF16)
    picked_ref[...] = picked
    products = dot_tn(picked, corner.astype(BF16))
    middle = products[:32, :32]
    for q in range(1, 3):
        middle = middle + products[32 * q : 32 * q + 32, 32 * q : 32 * q + 32]
    send_ref[...] = jnp.concatenate([fold_rows(middle), jnp.sum(tiles, axis=0)], axis=0)


def coarse_second_body(own_ref, one_ref, two_ref, three_ref, picked_ref, send_ref, totals_ref):
    total = (own_ref[...] + two_ref[...]) + (one_ref[...] + three_ref[...])
    middle = unfold_rows(total[:8])
    rounded = middle.astype(BF16)
    square = jnp.sum(middle * rounded.astype(F32), axis=0, keepdims=True)
    wide = jnp.concatenate([middle] * 4, axis=1)
    wide = jnp.concatenate([wide] * 4, axis=0)
    near = lax.broadcasted_iota(jnp.int32, wide.shape, 0) // 32
    far = lax.broadcasted_iota(jnp.int32, wide.shape, 1) // 32
    diagonal = jnp.where(near == far, wide, 0.0).astype(BF16)
    out = dot_nn(picked_ref[...], diagonal)
    zero = jnp.zeros((5, 96 // 3), F32)
    scalars = jnp.concatenate(three_parts(square) + [zero], axis=0)
    extra = jnp.concatenate([jnp.zeros((8, 96), F32), scalars], axis=1)
    send_ref[...] = (out.reshape(send_ref.shape) + extra[None]).astype(BF16)
    totals_ref[...] = total[8:16]


def schur_last_body(coarse_ref, totals_ref, local_ref, fields_ref, rows_ref, *out_refs):
    schur_ref, step_ref, *block_refs = out_refs
    cases = local_ref.shape[0]
    rows = unfold_rows(jnp.sum(coarse_ref[...].astype(F32), axis=0))
    picked = rows[:24].astype(BF16)
    schur = local_ref[...] + dot_tn(picked, fields_ref[cases : cases + 24])
    schur = schur.astype(BF16)
    schur_ref[...] = schur
    for b in range(BLOCKS):
        block_refs[b][...] = from_slots(schur, rows_ref, b)
    square = jnp.sum(rows[24:27], axis=0, keepdims=True)
    parts = [part_row(totals_ref[...], p, cases) for p in range(6)]
    rho = parts[0] + parts[1] + parts[2]
    curve = 2.0 * (parts[3] + parts[4] + parts[5] + square)
    step_ref[...] = jnp.broadcast_to(row_to_column(rho / curve), step_ref.shape)


def update_body(*refs):
    schur_ref, step_ref, live_ref, direction_ref, residual_ref, rows_ref = refs[
        BLOCKS : BLOCKS + 6
    ]
    multipliers_ref, new_residual_ref = refs[BLOCKS + 6 :]
    received = to_slots([ref[...] for ref in refs[:BLOCKS]], rows_ref, schur_ref.shape[1])
    image = live_ref[0:1] * (schur_ref[...].astype(F32) - received)
    step = step_ref[:, 0:1]
    multipliers_ref[...] = step * direction_ref[...]
    new_residual_ref[...] = residual_ref[...] - step * image


def exchange(blocks):
    count = lax.axis_size("sub")
    received = [None] * BLOCKS
    for b in (2, 5, 1, 4, 0, 3):
        route = [(i, (i + OFFSETS[b]) % count) for i in range(count)]
        received[(b + 3) % BLOCKS] = lax.ppermute(blocks[b], "sub", route)
    return received


def to_groups(block):
    count = lax.axis_size("grp")
    return [
        lax.ppermute(block, "grp", [(i, (i + k) % count) for i in range(count)])
        for k in range(1, count)
    ]


def on_device(
    load_source,
    schur_diag,
    schur_factor,
    dir_diag,
    dir_factor,
    corner_map,
    corner_row,
    coarse_factor,
    slot_table,
):
    source = load_source[0, 0]
    schur_factor = schur_factor[0, 0]
    dir_factor = dir_factor[0, 0]
    cases, interface = source.shape
    subs, groups = lax.axis_size("sub"), lax.axis_size("grp")
    table = slot_table.reshape(1, -1)
    total = table.shape[1]
    cap = total // BLOCKS
    field = (cases, interface)
    depth, coarse_size = coarse_factor.shape

    def blocks_of(rows):
        return [((rows, cap), BF16)] * BLOCKS

    corner = corner_row[0]
    away = (lax.axis_index("grp") - corner // 8 % 4) % groups
    corner = ((corner // 32 * 4 + away) * 8 + corner % 8).astype(F32)
    corner_row = jnp.pad(corner, ((0, 0), (0, interface - corner.shape[1])))
    rows = jnp.concatenate([table.astype(F32), dir_diag[0], schur_diag[0], corner_row], axis=0)
    fields = jnp.concatenate([source, corner_map[0, 0]], axis=0)
    fields = jnp.pad(fields, ((0, -fields.shape[0] % 16), (0, 0)))
    factor_scratch = [pltpu.VMEM((interface, interface), BF16), pltpu.SemaphoreType.DMA((PIECES,))]

    coarse_rows = [coarse_factor] + to_groups(coarse_factor)
    blocks = call(first_exchange_body, blocks_of(cases), 4, rows, fields)
    firsts = exchange(blocks)
    residual, dir_out, live, rho, *blocks = call(
        dirichlet_body,
        [(field, F32), (field, BF16), ((8, interface), F32), ((8, cases), F32)] + blocks_of(cases),
        16,
        *firsts,
        rows,
        fields,
        dir_factor,
        scratch=[pltpu.VMEM((interface, total), BF16)] + factor_scratch,
        in_hbm=(BLOCKS + 2,),
        vmem=50,
    )
    seconds = exchange(blocks)
    *coarse_rows, rho = lax.optimization_barrier((*coarse_rows, rho))
    (dealt,) = call(deal_columns_body, [((subs, depth, LANES), BF16)], 2, *coarse_rows)
    direction, schur_middle, corner_in = call(
        schur_first_body,
        [(field, F32), (field, BF16), ((subs, depth, 2 * LANES), BF16)],
        16,
        *seconds,
        dir_out,
        live,
        rho,
        rows,
        fields,
        dealt,
        schur_factor,
        scratch=factor_scratch,
        in_hbm=(BLOCKS + 6,),
        vmem=50,
    )
    corner_in = lax.all_to_all(corner_in, "sub", 0, 0, tiled=True)
    (local,) = call(
        schur_second_body,
        [(field, F32)],
        8,
        direction,
        schur_middle,
        rows,
        schur_factor,
        scratch=factor_scratch,
        in_hbm=(3,),
        vmem=50,
    )
    picked, parts = call(
        coarse_first_body,
        [((subs * depth, LANES), BF16), ((16, LANES), F32)],
        4,
        corner_in,
    )
    local, parts = lax.optimization_barrier((local, parts))
    coarse, totals = call(
        coarse_second_body,
        [((subs, 8, LANES), BF16), ((8, LANES), F32)],
        2,
        parts,
        *to_groups(parts),
        picked,
    )
    coarse = lax.all_to_all(coarse, "sub", 0, 0, tiled=True)
    schur_out, step, *blocks = call(
        schur_last_body,
        [(field, BF16), ((cases, LANES), F32)] + blocks_of(cases),
        8,
        coarse,
        totals,
        local,
        fields,
        rows,
    )
    multipliers, residual = call(
        update_body,
        [(field, F32), (field, F32)],
        8,
        *exchange(blocks),
        schur_out,
        step,
        live,
        direction,
        residual,
        rows,
    )
    return (multipliers[None, None], residual[None, None])


def solution(mesh):
    return jax.shard_map(
        on_device,
        mesh=mesh,
        in_specs=(
            P("grp", "sub", None, None),
            P("grp", "sub", None),
            P("grp", "sub", None, None),
            P("grp", "sub", None),
            P("grp", "sub", None, None),
            P("grp", "sub", None, None),
            P("grp", "sub", None),
            P(("sub", "grp"), None),
            P("grp", "sub", None, None),
        ),
        out_specs=(P("grp", "sub", None, None), P("grp", "sub", None, None)),
        check_vma=False,
    )
```

time: 120 us -> 105 us (0.88)
  starting transfers between devices: 56.1 us -> 43.3 us
  blocking collectives: 8.6 us -> 16.8 us
  waiting for transfers between devices: 25.4 us -> 20.2 us
  Pallas kernels: 24.7 us -> 20.5 us
    all_to_all x3 -> x0, starting transfers between devices: 17.4 us -> none  [the longest x1 7.41 us: on_device(): middle = lax.all_to_all(middle, 'sub', 0, 0, tiled=True)]
    ppermute x18, waiting for transfers between devices: 16.9 us -> 7.24 us  [exchange(): received[(b + 3) % BLOCKS] = lax.ppermute(blocks[b], 'sub', route)]
    all_to_all x1, blocking collectives: 8.6 us -> 16.8 us  [on_device(): coarse = lax.all_to_all(coarse, 'sub', 0, 0, tiled=True)]
    ppermute x0 -> x6, starting transfers between devices: none -> 6.9 us  [to_groups(): lax.ppermute(block, 'grp', [(i, (i + k) % count) for i in range(count)])]
    pallas_call x10 -> x9, Pallas kernels: 24.7 us -> 20.5 us  [call(): pl.pallas_call(body, out_shape=[jax.ShapeDtypeStruct(shape, dtype) for sh...]
    ppermute x0 -> x6, waiting for transfers between devices: none -> 3.66 us  [to_groups(): lax.ppermute(block, 'grp', [(i, (i + k) % count) for i in range(count)])]
    all_to_all x1, starting transfers between devices: 7.41 us -> 5.8 us  [on_device(): corner_in = lax.all_to_all(corner_in, 'sub', 0, 0, tiled=True)]
  transfers between devices with their start and end apart: 22 -> 25, of which waited for: 7 -> 9; matrix products, arithmetic and copies ran while one was open for 3% -> 0% of each run, Pallas kernels for 13% -> 10%
where the time goes in v2:
time: 105 us
  starting transfers between devices  43.3 us (41%)
  Pallas kernels  20.5 us (20%)
  waiting for transfers between devices  20.2 us (19%)
  blocking collectives  16.8 us (16%)
  other arithmetic  3.06 us (3%)
    ppermute x18, starting transfers between devices, exchange(): received[(b + 3) % BLOCKS] = lax.ppermute(blocks[b], 'sub', route)  30.6 us
    pallas_call x9, Pallas kernels, call(): pl.pallas_call(body, out_shape=[jax.ShapeDtypeStruct(shape, dtype) for sh...  20.5 us
    all_to_all x1, blocking collectives, on_device(): coarse = lax.all_to_all(coarse, 'sub', 0, 0, tiled=True)  16.8 us
    all_to_all x1, waiting for transfers between devices, on_device(): corner_in = lax.all_to_all(corner_in, 'sub', 0, 0, tiled=True)  9.3 us
    ppermute x18, waiting for transfers between devices, exchange(): received[(b + 3) % BLOCKS] = lax.ppermute(blocks[b], 'sub', route)  7.24 us
    ppermute x6, starting transfers between devices, to_groups(): lax.ppermute(block, 'grp', [(i, (i + k) % count) for i in range(count)])  6.9 us
    all_to_all x1, starting transfers between devices, on_device(): corner_in = lax.all_to_all(corner_in, 'sub', 0, 0, tiled=True)  5.8 us
    ppermute x6, waiting for transfers between devices, to_groups(): lax.ppermute(block, 'grp', [(i, (i + k) % count) for i in range(count)])  3.66 us
  transfers between devices with their start and end apart: 25, of which 9 were waited for; matrix products, arithmetic and copies ran while one was open for 0% of the time, Pallas kernels for 10%

profile of v2, /device:TPU:1, one launch (start us, length us, event | category | flops | bytes accessed | tf_op | source)
XLA Modules:
  0.0 104.7 jit_solution(5512150925963633433)
XLA Ops:
  4.6 3.3 %collective-permute-start = (bf16[32,256]{1,0:T(8,128)(2,1)S(1)}, bf16[32,256]{1,0:T(8,128)(2,1)S(1)}, u32[]{:S(2)}, u32[]{:S(2)}) collective-permute-start(bf16[32,256]{1,0:T(8,128)(2,1)S(1)} %get-tuple-element.42), channel_id=1, source_target_pairs={{0,252},{4,0},{8,4},{12,8},{16,12},{20,16},{24,20},{28,24},{32,28}... | collective-permute-start | bytes 49160 | tf_op jit(solution)/shard_map/ppermute | solution.py:310
  7.9 6.3 %collective-permute-start.1 = (bf16[32,256]{1,0:T(8,128)(2,1)S(1)}, bf16[32,256]{1,0:T(8,128)(2,1)S(1)}, u32[]{:S(2)}, u32[]{:S(2)}) collective-permute-start(bf16[32,256]{1,0:T(8,128)(2,1)S(1)} %get-tuple-element.43), channel_id=1, source_target_pairs={{0,248},{4,252},{8,0},{12,4},{16,8},{20,12},{24,16},{28,20},{32,24... | collective-permute-start | bytes 49160 | tf_op jit(solution)/shard_map/ppermute | solution.py:310
  15.8 2.5 %collective-permute-start.5 = (bf16[32,256]{1,0:T(8,128)(2,1)S(1)}, bf16[32,256]{1,0:T(8,128)(2,1)S(1)}, u32[]{:S(2)}, u32[]{:S(2)}) collective-permute-start(bf16[32,256]{1,0:T(8,128)(2,1)S(1)} %get-tuple-element.47), channel_id=1, source_target_pairs={{0,20},{4,24},{8,28},{12,32},{16,36},{20,40},{24,44},{28,48},{32,5... | collective-permute-start | bytes 49160 | tf_op jit(solution)/shard_map/ppermute | solution.py:310
  18.3 2.7 %collective-permute-start.13 = (bf16[8,2048]{1,0:T(8,128)(2,1)}, bf16[8,2048]{1,0:T(8,128)(2,1)S(1)}, u32[]{:S(2)}, u32[]{:S(2)}) collective-permute-start(bf16[8,2048]{1,0:T(8,128)(2,1)} %own_ref), channel_id=1, source_target_pairs={{0,2},{1,3},{2,0},{3,1},{4,6},{5,7},{6,4},{7,5},{8,10},{9,11},{10,... | collective-permute-start | bytes 98312 | tf_op jit(solution)/shard_map/ppermute | solution.py:317
  21.4 2.4 %collective-permute-start.14 = (bf16[8,2048]{1,0:T(8,128)(2,1)}, bf16[8,2048]{1,0:T(8,128)(2,1)S(1)}, u32[]{:S(2)}, u32[]{:S(2)}) collective-permute-start(bf16[8,2048]{1,0:T(8,128)(2,1)} %own_ref), channel_id=1, source_target_pairs={{0,3},{1,0},{2,1},{3,2},{4,7},{5,4},{6,5},{7,6},{8,11},{9,8},{10,9... | collective-permute-start | bytes 98312 | tf_op jit(solution)/shard_map/ppermute | solution.py:317
  23.8 6.3 %shard_map.105 = (f32[32,1536]{1,0:T(8,128)S(1)}, bf16[32,1536]{1,0:T(8,128)(2,1)S(1)}, f32[8,1536]{1,0:T(8,128)S(1)}, f32[8,32]{1,0:T(8,128)S(1)}, bf16[32,256]...) custom-call(bf16[32,256]{1,0:T(8,128)(2,1)S(1)} %collective-permute-, ...), custom_call_target="tpu_custom_call" | custom-call | flops 16777216 | bytes 16777216 | tf_op jit(solution)/shard_map/pallas_call | solution.py:62
  30.0 2.1 %collective-permute-start.6 = (bf16[32,256]{1,0:T(8,128)(2,1)S(1)}, bf16[32,256]{1,0:T(8,128)(2,1)S(1)}, u32[]{:S(2)}, u32[]{:S(2)}) collective-permute-start(bf16[32,256]{1,0:T(8,128)(2,1)S(1)} %get-tuple-element.48), channel_id=1, source_target_pairs={{0,252},{4,0},{8,4},{12,8},{16,12},{20,16},{24,20},{28,24},{32,28}... | collective-permute-start | bytes 49160 | tf_op jit(solution)/shard_map/ppermute | solution.py:310
  32.1 3.4 %collective-permute-start.7 = (bf16[32,256]{1,0:T(8,128)(2,1)S(1)}, bf16[32,256]{1,0:T(8,128)(2,1)S(1)}, u32[]{:S(2)}, u32[]{:S(2)}) collective-permute-start(bf16[32,256]{1,0:T(8,128)(2,1)S(1)} %get-tuple-element.49), channel_id=1, source_target_pairs={{0,248},{4,252},{8,0},{12,4},{16,8},{20,12},{24,16},{28,20},{32,24... | collective-permute-start | bytes 49160 | tf_op jit(solution)/shard_map/ppermute | solution.py:310
  36.7 2.2 %collective-permute-start.11 = (bf16[32,256]{1,0:T(8,128)(2,1)S(1)}, bf16[32,256]{1,0:T(8,128)(2,1)S(1)}, u32[]{:S(2)}, u32[]{:S(2)}) collective-permute-start(bf16[32,256]{1,0:T(8,128)(2,1)S(1)} %get-tuple-element.53), channel_id=1, source_target_pairs={{0,20},{4,24},{8,28},{12,32},{16,36},{20,40},{24,44},{28,48},{32,5... | collective-permute-start | bytes 49160 | tf_op jit(solution)/shard_map/ppermute | solution.py:310
  39.1 1.1 %collective-permute-done.8.refs_2_ = bf16[32,256]{1,0:T(8,128)(2,1)S(1)} collective-permute-done((bf16[32,256]{1,0:T(8,128)(2,1)S(1)}, bf16[32,256]{1,0:T(8,128)(2,1)S(1)}, u32[]{:S(2)}, u32[]{:S(2)}) %collective-permute-start.8) | collective-permute-done | bytes 16416 | tf_op jit(solution)/shard_map/ppermute | solution.py:310
  40.2 1.9 %collective-permute-done.10.refs_4_ = bf16[32,256]{1,0:T(8,128)(2,1)S(1)} collective-permute-done((bf16[32,256]{1,0:T(8,128)(2,1)S(1)}, bf16[32,256]{1,0:T(8,128)(2,1)S(1)}, u32[]{:S(2)}, u32[]{:S(2)}) %collective-permute-start.10) | collective-permute-done | bytes 16416 | tf_op jit(solution)/shard_map/ppermute | solution.py:310
  42.1 1.4 %collective-permute-done.11.refs_5_ = bf16[32,256]{1,0:T(8,128)(2,1)S(1)} collective-permute-done((bf16[32,256]{1,0:T(8,128)(2,1)S(1)}, bf16[32,256]{1,0:T(8,128)(2,1)S(1)}, u32[]{:S(2)}, u32[]{:S(2)}) %collective-permute-start.11) | collective-permute-done | bytes 16416 | tf_op jit(solution)/shard_map/ppermute | solution.py:310
  43.5 4.2 %shard_map.107 = (f32[32,1536]{1,0:T(8,128)S(1)}, bf16[32,1536]{1,0:T(8,128)(2,1)S(1)}, bf16[64,8,256]{2,1,0:T(8,128)(2,1)}) custom-call(bf16[32,256]{1,0:T(8,128)(2,1)S(1)} %collective-permute-done.6.refs_0_, bf16[32,256]{1,0:T(8,128)(2,1)S(1)} %collective-permute-done.7.refs_1_, bf16[32,256]{1,0:T(8,128)(2,1)S(1)} %collective-permute-done.8.refs_2_, ...), custom_call_target="tpu_custom_call" | custom-call | flops 16777216 | bytes 16777216 | tf_op jit(solution)/shard_map/pallas_call | solution.py:62
  47.7 5.8 %all-to-all-start = ((bf16[64,8,256]{2,1,0:T(8,128)(2,1)}), bf16[64,8,256]{2,1,0:T(8,128)(2,1)S(1)}, u32[]{:S(2)}, u32[]{:S(2)}) async-start(bf16[64,8,256]{2,1,0:T(8,128)(2,1)} %get-tuple-element.64), calls=%async_computation | async-start | bytes 524288 | tf_op jit(solution)/shard_map/all_to_all | solution.py:390
  53.5 3.9 %shard_map.108.local_ref = f32[32,1536]{1,0:T(8,128)S(1)} custom-call(f32[32,1536]{1,0:T(8,128)S(1)} %get-tuple-element.62.direction_ref.refs_9_, bf16[32,1536]{1,0:T(8,128)(2,1)S(1)} %get-tuple-element.63.middle_ref, f32[4,1536]{1,0:T(4,128)S(1)} %select_maximum_fusion.rows_ref.refs_6_.refs_9_.refs_11_, bf16[1536,1536]{1,0:T(8,128)(2,1)} %bitcast.28), custom_call_target="tpu_custom_call" | custom-call | flops 8388608 | bytes 8388608 | tf_op jit(solution)/shard_map/pallas_call | solution.py:62
  57.4 9.3 %all-to-all-done.sent_ref = bf16[64,8,256]{2,1,0:T(8,128)(2,1)S(1)} async-done(((bf16[64,8,256]{2,1,0:T(8,128)(2,1)}), bf16[64,8,256]{2,1,0:T(8,128)(2,1)S(1)}, u32[]{:S(2)}, u32[]{:S(2)}) %all-to-all-start) | async-done | bytes 262176 | tf_op jit(solution)/shard_map/all_to_all | solution.py:390
  66.7 1.3 %shard_map.109 = (bf16[512,128]{1,0:T(8,128)(2,1)S(1)}, f32[16,128]{1,0:T(8,128)S(1)}) custom-call(bf16[64,8,256]{2,1,0:T(8,128)(2,1)S(1)} %all-to-all-done.sent_ref), custom_call_target="tpu_custom_call" | custom-call | flops 4194304 | bytes 4194304 | tf_op jit(solution)/shard_map/pallas_call | solution.py:62
  70.6 1.6 %collective-permute-done.16.two_ref = f32[16,128]{1,0:T(8,128)S(1)} collective-permute-done((f32[16,128]{1,0:T(8,128)S(1)}, f32[16,128]{1,0:T(8,128)S(1)}, u32[]{:S(2)}, u32[]{:S(2)}) %collective-permute-start.16) | collective-permute-done | bytes 8224 | tf_op jit(solution)/shard_map/ppermute | solution.py:317
  73.5 16.8 %all_to_all.10.coarse_ref = bf16[64,8,128]{2,1,0:T(8,128)(2,1)S(1)} all-to-all(bf16[64,8,128]{2,1,0:T(8,128)(2,1)S(1)} %get-tuple-element.68), channel_id=1, replica_groups=mesh['sub'=64,'grp'=4] {'sub'}, dimensions={0} | all-to-all | bytes 262144 | tf_op jit(solution)/shard_map/all_to_all | solution.py:418
  90.3 1.2 %shard_map.111 = (bf16[32,1536]{1,0:T(8,128)(2,1)S(1)}, f32[32,128]{1,0:T(8,128)S(1)}, bf16[32,256]{1,0:T(8,128)(2,1)S(1)}, bf16[32,256]{1,0:T(8,128)(2,1)S(1)},...) custom-call(bf16[64,8,128]{2,1,0:T(8,128)(2,1)S(1)} %all_to_all.10.c, ...), custom_call_target="tpu_custom_call" | custom-call | flops 8388608 | bytes 8388608 | tf_op jit(solution)/shard_map/pallas_call | solution.py:62
  93.0 2.5 %collective-permute-start.20 = (bf16[32,256]{1,0:T(8,128)(2,1)S(1)}, bf16[32,256]{1,0:T(8,128)(2,1)S(1)}, u32[]{:S(2)}, u32[]{:S(2)}) collective-permute-start(bf16[32,256]{1,0:T(8,128)(2,1)S(1)} %get-tuple-element.73), channel_id=1, source_target_pairs={{0,236},{4,240},{8,244},{12,248},{16,252},{20,0},{24,4},{28,8},{32... | collective-permute-start | bytes 49160 | tf_op jit(solution)/shard_map/ppermute | solution.py:310
  95.6 4.1 %collective-permute-start.23 = (bf16[32,256]{1,0:T(8,128)(2,1)S(1)}, bf16[32,256]{1,0:T(8,128)(2,1)S(1)}, u32[]{:S(2)}, u32[]{:S(2)}) collective-permute-start(bf16[32,256]{1,0:T(8,128)(2,1)S(1)} %get-tuple-element.76), channel_id=1, source_target_pairs={{0,20},{4,24},{8,28},{12,32},{16,36},{20,40},{24,44},{28,48},{32,5... | collective-permute-start | bytes 49160 | tf_op jit(solution)/shard_map/ppermute | solution.py:310
  99.7 1.8 %collective-permute-done.22.refs_4_ = bf16[32,256]{1,0:T(8,128)(2,1)S(1)} collective-permute-done((bf16[32,256]{1,0:T(8,128)(2,1)S(1)}, bf16[32,256]{1,0:T(8,128)(2,1)S(1)}, u32[]{:S(2)}, u32[]{:S(2)}) %collective-permute-start.22) | collective-permute-done | bytes 16416 | tf_op jit(solution)/shard_map/ppermute | solution.py:310
  102.5 2.2 %shard_map.112 = (f32[32,1536]{1,0:T(8,128)}, f32[32,1536]{1,0:T(8,128)}) custom-call(bf16[32,256]{1,0:T(8,128)(2,1)S(1)} %collective-permute-done.18.refs_0_, bf16[32,256]{1,0:T(8,128)(2,1)S(1)} %collective-permute-done.19.refs_1_, bf16[32,256]{1,0:T(8,128)(2,1)S(1)} %collective-permute-done.20.refs_2_, ...), custom_call_target="tpu_custom_call" | custom-call | flops 8388608 | bytes 8388608 | tf_op jit(solution)/shard_map/pallas_call | solution.py:62
  (42 shorter events, 13.6 us)
Async XLA Ops:
  4.6 11.2 %collective-permute-start = (bf16[32,256]{1,0:T(8,128)(2,1)S(1)}, bf16[32,256]{1,0:T(8,128)(2,1)S(1)}, u32[]{:S(2)}, u32[]{:S(2)}) collective-permute-start(bf16[32,256]{1,0:T(8,128)(2,1)S(1)} %get-tuple-element.42), channel_id=1, source_target_pairs={{0,252},{4,0},{8,4},{12,8},{16,12},{20,16},{24,20},{28,24},{32,28}... | collective-permute-start | bytes 49160 | tf_op jit(solution)/shard_map/ppermute | solution.py:310
  7.9 10.4 %collective-permute-start.1 = (bf16[32,256]{1,0:T(8,128)(2,1)S(1)}, bf16[32,256]{1,0:T(8,128)(2,1)S(1)}, u32[]{:S(2)}, u32[]{:S(2)}) collective-permute-start(bf16[32,256]{1,0:T(8,128)(2,1)S(1)} %get-tuple-element.43), channel_id=1, source_target_pairs={{0,248},{4,252},{8,0},{12,4},{16,8},{20,12},{24,16},{28,20},{32,24... | collective-permute-start | bytes 49160 | tf_op jit(solution)/shard_map/ppermute | solution.py:310
  14.2 6.9 %collective-permute-start.2 = (bf16[32,256]{1,0:T(8,128)(2,1)S(1)}, bf16[32,256]{1,0:T(8,128)(2,1)S(1)}, u32[]{:S(2)}, u32[]{:S(2)}) collective-permute-start(bf16[32,256]{1,0:T(8,128)(2,1)S(1)} %get-tuple-element.44), channel_id=1, source_target_pairs={{0,236},{4,240},{8,244},{12,248},{16,252},{20,0},{24,4},{28,8},{32... | collective-permute-start | bytes 49160 | tf_op jit(solution)/shard_map/ppermute | solution.py:310
  14.8 6.6 %collective-permute-start.3 = (bf16[32,256]{1,0:T(8,128)(2,1)S(1)}, bf16[32,256]{1,0:T(8,128)(2,1)S(1)}, u32[]{:S(2)}, u32[]{:S(2)}) collective-permute-start(bf16[32,256]{1,0:T(8,128)(2,1)S(1)} %get-tuple-element.45), channel_id=1, source_target_pairs={{0,4},{4,8},{8,12},{12,16},{16,20},{20,24},{24,28},{28,32},{32,36}... | collective-permute-start | bytes 49160 | tf_op jit(solution)/shard_map/ppermute | solution.py:310
  15.5 8.2 %collective-permute-start.4 = (bf16[32,256]{1,0:T(8,128)(2,1)S(1)}, bf16[32,256]{1,0:T(8,128)(2,1)S(1)}, u32[]{:S(2)}, u32[]{:S(2)}) collective-permute-start(bf16[32,256]{1,0:T(8,128)(2,1)S(1)} %get-tuple-element.46), channel_id=1, source_target_pairs={{0,8},{4,12},{8,16},{12,20},{16,24},{20,28},{24,32},{28,36},{32,40... | collective-permute-start | bytes 49160 | tf_op jit(solution)/shard_map/ppermute | solution.py:310
  15.8 8.0 %collective-permute-start.5 = (bf16[32,256]{1,0:T(8,128)(2,1)S(1)}, bf16[32,256]{1,0:T(8,128)(2,1)S(1)}, u32[]{:S(2)}, u32[]{:S(2)}) collective-permute-start(bf16[32,256]{1,0:T(8,128)(2,1)S(1)} %get-tuple-element.47), channel_id=1, source_target_pairs={{0,20},{4,24},{8,28},{12,32},{16,36},{20,40},{24,44},{28,48},{32,5... | collective-permute-start | bytes 49160 | tf_op jit(solution)/shard_map/ppermute | solution.py:310
  18.3 17.2 %collective-permute-start.13 = (bf16[8,2048]{1,0:T(8,128)(2,1)}, bf16[8,2048]{1,0:T(8,128)(2,1)S(1)}, u32[]{:S(2)}, u32[]{:S(2)}) collective-permute-start(bf16[8,2048]{1,0:T(8,128)(2,1)} %own_ref), channel_id=1, source_target_pairs={{0,2},{1,3},{2,0},{3,1},{4,6},{5,7},{6,4},{7,5},{8,10},{9,11},{10,... | collective-permute-start | bytes 98312 | tf_op jit(solution)/shard_map/ppermute | solution.py:317
  21.1 14.9 %collective-permute-start.12 = (bf16[8,2048]{1,0:T(8,128)(2,1)}, bf16[8,2048]{1,0:T(8,128)(2,1)S(1)}, u32[]{:S(2)}, u32[]{:S(2)}) collective-permute-start(bf16[8,2048]{1,0:T(8,128)(2,1)} %own_ref), channel_id=1, source_target_pairs={{0,1},{1,2},{2,3},{3,0},{4,5},{5,6},{6,7},{7,4},{8,9},{9,10},{10,1... | collective-permute-start | bytes 98312 | tf_op jit(solution)/shard_map/ppermute | solution.py:317
  21.4 14.7 %collective-permute-start.14 = (bf16[8,2048]{1,0:T(8,128)(2,1)}, bf16[8,2048]{1,0:T(8,128)(2,1)S(1)}, u32[]{:S(2)}, u32[]{:S(2)}) collective-permute-start(bf16[8,2048]{1,0:T(8,128)(2,1)} %own_ref), channel_id=1, source_target_pairs={{0,3},{1,0},{2,1},{3,2},{4,7},{5,4},{6,5},{7,6},{8,11},{9,8},{10,9... | collective-permute-start | bytes 98312 | tf_op jit(solution)/shard_map/ppermute | solution.py:317
  30.0 6.6 %collective-permute-start.6 = (bf16[32,256]{1,0:T(8,128)(2,1)S(1)}, bf16[32,256]{1,0:T(8,128)(2,1)S(1)}, u32[]{:S(2)}, u32[]{:S(2)}) collective-permute-start(bf16[32,256]{1,0:T(8,128)(2,1)S(1)} %get-tuple-element.48), channel_id=1, source_target_pairs={{0,252},{4,0},{8,4},{12,8},{16,12},{20,16},{24,20},{28,24},{32,28}... | collective-permute-start | bytes 49160 | tf_op jit(solution)/shard_map/ppermute | solution.py:310
  32.1 7.0 %collective-permute-start.7 = (bf16[32,256]{1,0:T(8,128)(2,1)S(1)}, bf16[32,256]{1,0:T(8,128)(2,1)S(1)}, u32[]{:S(2)}, u32[]{:S(2)}) collective-permute-start(bf16[32,256]{1,0:T(8,128)(2,1)S(1)} %get-tuple-element.49), channel_id=1, source_target_pairs={{0,248},{4,252},{8,0},{12,4},{16,8},{20,12},{24,16},{28,20},{32,24... | collective-permute-start | bytes 49160 | tf_op jit(solution)/shard_map/ppermute | solution.py:310
  35.6 4.6 %collective-permute-start.8 = (bf16[32,256]{1,0:T(8,128)(2,1)S(1)}, bf16[32,256]{1,0:T(8,128)(2,1)S(1)}, u32[]{:S(2)}, u32[]{:S(2)}) collective-permute-start(bf16[32,256]{1,0:T(8,128)(2,1)S(1)} %get-tuple-element.50), channel_id=1, source_target_pairs={{0,236},{4,240},{8,244},{12,248},{16,252},{20,0},{24,4},{28,8},{32... | collective-permute-start | bytes 49160 | tf_op jit(solution)/shard_map/ppermute | solution.py:310
  36.0 4.2 %collective-permute-start.9 = (bf16[32,256]{1,0:T(8,128)(2,1)S(1)}, bf16[32,256]{1,0:T(8,128)(2,1)S(1)}, u32[]{:S(2)}, u32[]{:S(2)}) collective-permute-start(bf16[32,256]{1,0:T(8,128)(2,1)S(1)} %get-tuple-element.51), channel_id=1, source_target_pairs={{0,4},{4,8},{8,12},{12,16},{16,20},{20,24},{24,28},{28,32},{32,36}... | collective-permute-start | bytes 49160 | tf_op jit(solution)/shard_map/ppermute | solution.py:310
  36.1 6.0 %collective-permute-start.10 = (bf16[32,256]{1,0:T(8,128)(2,1)S(1)}, bf16[32,256]{1,0:T(8,128)(2,1)S(1)}, u32[]{:S(2)}, u32[]{:S(2)}) collective-permute-start(bf16[32,256]{1,0:T(8,128)(2,1)S(1)} %get-tuple-element.52), channel_id=1, source_target_pairs={{0,8},{4,12},{8,16},{12,20},{16,24},{20,28},{24,32},{28,36},{32,40... | collective-permute-start | bytes 49160 | tf_op jit(solution)/shard_map/ppermute | solution.py:310
  36.7 6.8 %collective-permute-start.11 = (bf16[32,256]{1,0:T(8,128)(2,1)S(1)}, bf16[32,256]{1,0:T(8,128)(2,1)S(1)}, u32[]{:S(2)}, u32[]{:S(2)}) collective-permute-start(bf16[32,256]{1,0:T(8,128)(2,1)S(1)} %get-tuple-element.53), channel_id=1, source_target_pairs={{0,20},{4,24},{8,28},{12,32},{16,36},{20,40},{24,44},{28,48},{32,5... | collective-permute-start | bytes 49160 | tf_op jit(solution)/shard_map/ppermute | solution.py:310
  47.7 19.0 %all-to-all-start = ((bf16[64,8,256]{2,1,0:T(8,128)(2,1)}), bf16[64,8,256]{2,1,0:T(8,128)(2,1)S(1)}, u32[]{:S(2)}, u32[]{:S(2)}) async-start(bf16[64,8,256]{2,1,0:T(8,128)(2,1)} %get-tuple-element.64), calls=%async_computation | async-start | bytes 524288 | tf_op jit(solution)/shard_map/all_to_all | solution.py:390
  68.1 4.1 %collective-permute-start.16 = (f32[16,128]{1,0:T(8,128)S(1)}, f32[16,128]{1,0:T(8,128)S(1)}, u32[]{:S(2)}, u32[]{:S(2)}) collective-permute-start(f32[16,128]{1,0:T(8,128)S(1)} %get-tuple-element.66.own_ref), channel_id=1, source_target_pairs={{0,2},{1,3},{2,0},{3,1},{4,6},{5,7},{6,4},{7,5},{8,10},{9,11},{10,... | collective-permute-start | bytes 24584 | tf_op jit(solution)/shard_map/ppermute | solution.py:317
  68.9 4.2 %collective-permute-start.15 = (f32[16,128]{1,0:T(8,128)S(1)}, f32[16,128]{1,0:T(8,128)S(1)}, u32[]{:S(2)}, u32[]{:S(2)}) collective-permute-start(f32[16,128]{1,0:T(8,128)S(1)} %get-tuple-element.66.own_ref), channel_id=1, source_target_pairs={{0,1},{1,2},{2,3},{3,0},{4,5},{5,6},{6,7},{7,4},{8,9},{9,10},{10,1... | collective-permute-start | bytes 24584 | tf_op jit(solution)/shard_map/ppermute | solution.py:317
  91.5 4.0 %collective-permute-start.18 = (bf16[32,256]{1,0:T(8,128)(2,1)S(1)}, bf16[32,256]{1,0:T(8,128)(2,1)S(1)}, u32[]{:S(2)}, u32[]{:S(2)}) collective-permute-start(bf16[32,256]{1,0:T(8,128)(2,1)S(1)} %get-tuple-element.71), channel_id=1, source_target_pairs={{0,252},{4,0},{8,4},{12,8},{16,12},{20,16},{24,20},{28,24},{32,28}... | collective-permute-start | bytes 49160 | tf_op jit(solution)/shard_map/ppermute | solution.py:310
  92.0 7.7 %collective-permute-start.19 = (bf16[32,256]{1,0:T(8,128)(2,1)S(1)}, bf16[32,256]{1,0:T(8,128)(2,1)S(1)}, u32[]{:S(2)}, u32[]{:S(2)}) collective-permute-start(bf16[32,256]{1,0:T(8,128)(2,1)S(1)} %get-tuple-element.72), channel_id=1, source_target_pairs={{0,248},{4,252},{8,0},{12,4},{16,8},{20,12},{24,16},{28,20},{32,24... | collective-permute-start | bytes 49160 | tf_op jit(solution)/shard_map/ppermute | solution.py:310
  93.0 6.7 %collective-permute-start.20 = (bf16[32,256]{1,0:T(8,128)(2,1)S(1)}, bf16[32,256]{1,0:T(8,128)(2,1)S(1)}, u32[]{:S(2)}, u32[]{:S(2)}) collective-permute-start(bf16[32,256]{1,0:T(8,128)(2,1)S(1)} %get-tuple-element.73), channel_id=1, source_target_pairs={{0,236},{4,240},{8,244},{12,248},{16,252},{20,0},{24,4},{28,8},{32... | collective-permute-start | bytes 49160 | tf_op jit(solution)/shard_map/ppermute | solution.py:310
  95.5 4.1 %collective-permute-start.21 = (bf16[32,256]{1,0:T(8,128)(2,1)S(1)}, bf16[32,256]{1,0:T(8,128)(2,1)S(1)}, u32[]{:S(2)}, u32[]{:S(2)}) collective-permute-start(bf16[32,256]{1,0:T(8,128)(2,1)S(1)} %get-tuple-element.74), channel_id=1, source_target_pairs={{0,4},{4,8},{8,12},{12,16},{16,20},{20,24},{24,28},{28,32},{32,36}... | collective-permute-start | bytes 49160 | tf_op jit(solution)/shard_map/ppermute | solution.py:310
  95.5 5.9 %collective-permute-start.22 = (bf16[32,256]{1,0:T(8,128)(2,1)S(1)}, bf16[32,256]{1,0:T(8,128)(2,1)S(1)}, u32[]{:S(2)}, u32[]{:S(2)}) collective-permute-start(bf16[32,256]{1,0:T(8,128)(2,1)S(1)} %get-tuple-element.75), channel_id=1, source_target_pairs={{0,8},{4,12},{8,16},{12,20},{16,24},{20,28},{24,32},{28,36},{32,40... | collective-permute-start | bytes 49160 | tf_op jit(solution)/shard_map/ppermute | solution.py:310
  95.6 6.9 %collective-permute-start.23 = (bf16[32,256]{1,0:T(8,128)(2,1)S(1)}, bf16[32,256]{1,0:T(8,128)(2,1)S(1)}, u32[]{:S(2)}, u32[]{:S(2)}) collective-permute-start(bf16[32,256]{1,0:T(8,128)(2,1)S(1)} %get-tuple-element.76), channel_id=1, source_target_pairs={{0,20},{4,24},{8,28},{12,32},{16,36},{20,40},{24,44},{28,48},{32,5... | collective-permute-start | bytes 49160 | tf_op jit(solution)/shard_map/ppermute | solution.py:310
  (2 other events, 40.8 us)

commit v3 on v2

v3 whole, which is shorter than its diff:
```python
import jax
import jax.numpy as jnp
from jax import lax
from jax.experimental import pallas as pl
from jax.experimental.pallas import tpu as pltpu
from jax.sharding import PartitionSpec as P

OFFSETS = (1, 2, 5, -1, -2, -5)
BLOCKS = len(OFFSETS)
F32 = jnp.float32
BF16 = jnp.bfloat16
LANES = 128
PIECES = 3
RECEIVE_ORDER = (2, 1, 0, 5, 4, 3)
TABLE, DIR_DIAG, SCHUR_DIAG = 0, 1, 2


def dot_nn(a, b):
    return jnp.dot(a, b, preferred_element_type=F32)


def dot_nt(a, b):
    return lax.dot_general(a, b, (((1,), (1,)), ((), ())), preferred_element_type=F32)


def dot_tn(a, b):
    return lax.dot_general(a, b, (((0,), (0,)), ((), ())), preferred_element_type=F32)


def column_to_row(column):
    n = column.shape[0]
    same = lax.broadcasted_iota(jnp.int32, (n, n), 0) == lax.broadcasted_iota(jnp.int32, (n, n), 1)
    return jnp.sum(jnp.where(same, column, 0.0), axis=0, keepdims=True)


def row_to_column(row):
    n = row.shape[1]
    same = lax.broadcasted_iota(jnp.int32, (n, n), 0) == lax.broadcasted_iota(jnp.int32, (n, n), 1)
    return jnp.sum(jnp.where(same, row, 0.0), axis=1, keepdims=True)


def three_parts(value):
    first = value.astype(BF16).astype(F32)
    rest = value - first
    second = rest.astype(BF16).astype(F32)
    third = (rest - second).astype(BF16).astype(F32)
    return [first, second, third]


def fold_rows(rows):
    n = rows.shape[0] // 4
    return jnp.concatenate([rows[n * i : n * i + n] for i in range(4)], axis=1)


def unfold_rows(tile):
    n = tile.shape[1] // 4
    return jnp.concatenate([tile[:, n * i : n * i + n] for i in range(4)], axis=0)


def call(body, outs, weight, *args, scratch=(), in_hbm=(), vmem=20):
    in_vmem = pl.BlockSpec(memory_space=pltpu.VMEM)
    left = pl.BlockSpec(memory_space=pltpu.HBM)
    return pl.pallas_call(
        body,
        out_shape=[jax.ShapeDtypeStruct(shape, dtype) for shape, dtype in outs],
        in_specs=[left if i in in_hbm else in_vmem for i in range(len(args))],
        out_specs=[in_vmem] * len(outs),
        scratch_shapes=list(scratch),
        compiler_params=pltpu.CompilerParams(vmem_limit_bytes=vmem * 1024 * 1024),
        cost_estimate=pl.CostEstimate(
            flops=weight << 20, bytes_accessed=weight << 20, transcendentals=0
        ),
    )(*args)


def at_slots(values, table, b):
    cap, interface = table.shape[1] // BLOCKS, values.shape[1]
    slot = lax.broadcasted_iota(jnp.int32, (interface, cap), 0).astype(F32)
    named = slot == table[:, b * cap : (b + 1) * cap]
    return dot_nn(values, jnp.where(named, 1.0, 0.0).astype(BF16))


def from_slots(values, table, b):
    return at_slots(values, table, b).astype(BF16)


def to_slots(blocks, columns_ref, interface):
    slot = lax.broadcasted_iota(jnp.int32, (columns_ref.shape[0], interface), 1).astype(F32)
    total = None
    for block, b in zip(blocks, RECEIVE_ORDER):
        named = slot == columns_ref[:, b : b + 1]
        part = dot_nn(block, jnp.where(named, 1.0, 0.0).astype(BF16))
        total = part if total is None else total + part
    return total


def first_exchange_body(rows_ref, fields_ref, columns_ref, *block_refs):
    cases, cap = block_refs[0].shape
    table = rows_ref[TABLE : TABLE + 1]
    for b in range(BLOCKS):
        block_refs[b][...] = from_slots(fields_ref[:cases], table, b)
    lane = lax.broadcasted_iota(jnp.int32, columns_ref.shape, 1)
    columns = jnp.zeros(columns_ref.shape, F32)
    for b in range(BLOCKS):
        column = row_to_column(table[:, b * cap : (b + 1) * cap])
        columns = jnp.where(lane == b, column, columns)
    columns_ref[...] = columns


def load_factor(factor_ref, held_ref, semaphores):
    size = held_ref.shape[0] // PIECES
    copies = []
    for i in range(PIECES):
        piece = pl.ds(size * i, size)
        copies.append(
            pltpu.make_async_copy(factor_ref.at[piece], held_ref.at[piece], semaphores.at[i])
        )
        copies[i].start()
    return copies


def times_factor(operand, held_ref, copies):
    size = held_ref.shape[0] // PIECES
    total = None
    for i in range(PIECES):
        copies[i].wait()
        part = dot_nn(operand[:, size * i : size * i + size], held_ref[size * i : size * i + size])
        total = part if total is None else total + part
    return total


def dirichlet_body(*refs):
    columns_ref, rows_ref, fields_ref, factor_ref = refs[BLOCKS : BLOCKS + 4]
    residual_ref, out_ref, live_ref, rho_ref, *block_refs = refs[BLOCKS + 4 : -2]
    held_ref, semaphores = refs[-2:]
    copies = load_factor(factor_ref, held_ref, semaphores)
    cases, interface = residual_ref.shape
    ones = jnp.ones((16, block_refs[0].shape[1]), BF16)
    blocks = [jnp.concatenate([ref[...], ones], axis=0) for ref in refs[:BLOCKS]]
    spread = to_slots(blocks, columns_ref, interface)
    live = spread[cases : cases + 8]
    residual = live[0:1] * (fields_ref[:cases].astype(F32) - spread[:cases])
    middle = times_factor(residual.astype(BF16), held_ref, copies).astype(BF16)
    diag = rows_ref[DIR_DIAG : DIR_DIAG + 1]
    out = (0.5 * (diag * residual + dot_nt(middle, held_ref[...]))).astype(BF16)
    table = rows_ref[TABLE : TABLE + 1]
    for b in range(BLOCKS):
        block_refs[b][...] = from_slots(out, table, b)
    live_ref[...] = live
    residual_ref[...] = residual
    out_ref[...] = out
    rho = column_to_row(jnp.sum(residual * out.astype(F32), axis=1, keepdims=True))
    rho_ref[...] = jnp.broadcast_to(rho, rho_ref.shape)


def schur_first_body(*refs):
    out_ref, live_ref, columns_ref, fields_ref, index_ref, dealt_ref = refs[BLOCKS : BLOCKS + 6]
    direction_ref, send_ref = refs[BLOCKS + 6 :]
    cases, interface = out_ref.shape
    received = to_slots([ref[...] for ref in refs[:BLOCKS]], columns_ref, interface)
    direction = 0.5 * (live_ref[0:1] * (out_ref[...].astype(F32) - received))
    direction_ref[...] = direction
    corner_in = dot_nt(fields_ref[cases : cases + 24], direction.astype(BF16))
    groups = [corner_in[0:8], corner_in[8:16], corner_in[16:24], index_lanes(index_ref[...])]
    tile = jnp.concatenate(groups, axis=1).astype(BF16)
    count, depth, _ = send_ref.shape
    send_ref[:, :, :LANES] = jnp.broadcast_to(tile[None], (count, depth, LANES))
    send_ref[:, :, LANES:] = dealt_ref[...]


def schur_second_body(
    direction_ref,
    rho_ref,
    rows_ref,
    fields_ref,
    factor_ref,
    local_ref,
    sent_ref,
    maps_ref,
    scalars_ref,
    held_ref,
    semaphores,
):
    copies = load_factor(factor_ref, held_ref, semaphores)
    direction = direction_ref[...]
    wide = times_factor(direction.astype(BF16), held_ref, copies)
    middle = wide.astype(BF16)
    scaled = rows_ref[SCHUR_DIAG : SCHUR_DIAG + 1] * direction
    local = scaled + dot_nt(middle, held_ref[...])
    local_ref[...] = local
    cases, interface = local.shape
    values = [part.astype(BF16) for part in three_parts(local)] + [fields_ref[cases:]]
    values = jnp.concatenate(values, axis=0)
    cap = interface // BLOCKS
    for b in range(BLOCKS):
        picked = at_slots(values, rows_ref[TABLE : TABLE + 1], b)
        exact = (picked[:cases] + picked[cases : 2 * cases]) + picked[2 * cases : 3 * cases]
        sent_ref[:, b * cap : (b + 1) * cap] = exact
        maps_ref[:, b * cap : (b + 1) * cap] = picked[3 * cases :].astype(BF16)
    curve = jnp.sum(scaled * direction, axis=1, keepdims=True)
    curve = curve + jnp.sum(wide * middle.astype(F32), axis=1, keepdims=True)
    scalars = [rho_ref[0:1], column_to_row(curve), jnp.zeros((6, curve.shape[0]), F32)]
    scalars = jnp.concatenate(scalars, axis=0)
    scalars_ref[...] = jnp.concatenate([scalars, jnp.zeros((8, 96), F32)], axis=1)


def index_lanes(corner_row):
    corners = corner_row.shape[1]
    row = lax.broadcasted_iota(jnp.int32, (8, corners), 0)
    lane = lax.broadcasted_iota(jnp.int32, (8, corners), 1)
    place = lax.broadcasted_iota(jnp.int32, (8, 32), 1)
    tile = jnp.zeros((8, 32), F32)
    for q in range(3):
        mine = jnp.where(lane == 8 * q + row, corner_row, 0.0)
        value = jnp.sum(mine, axis=1, keepdims=True).astype(jnp.int32)
        tile = jnp.where(place == 2 * q, (value // 8).astype(F32), tile)
        tile = jnp.where(place == 2 * q + 1, (value % 8).astype(F32), tile)
    return tile


def deal_columns_body(own_ref, one_ref, two_ref, three_ref, send_ref):
    rows = [ref[...].astype(F32) for ref in (own_ref, one_ref, two_ref, three_ref)]
    depth, lanes = rows[0].shape
    group = lax.broadcasted_iota(jnp.int32, (depth, lanes), 1) // 32 % 4
    for t in range(4):
        dealt = jnp.zeros((depth, lanes), F32)
        for a in range(4):
            shift = (32 * (a - t)) % lanes
            moved = pltpu.roll(rows[a], shift, 1) if shift else rows[a]
            dealt = jnp.where(group == a, moved, dealt)
        for quad in range(lanes // LANES):
            tile = dealt[:, quad * LANES : (quad + 1) * LANES]
            send_ref[4 * quad + t] = tile.astype(BF16)


def coarse_first_body(sent_ref, scalars_ref, picked_ref, send_ref):
    count, depth, _ = sent_ref.shape
    size = count * depth
    sent = sent_ref[...].astype(F32)
    corner = sent[:, :, :LANES].reshape(size, LANES)
    columns = sent[:, :, LANES:].reshape(size, LANES).astype(BF16)
    place = lax.broadcasted_iota(jnp.int32, (size, size), 1).astype(F32)
    lane_group = (lax.broadcasted_iota(jnp.int32, (size, LANES), 1) // 32).astype(F32)
    near = lax.broadcasted_iota(jnp.int32, (LANES, LANES), 0)
    far = lax.broadcasted_iota(jnp.int32, (LANES, LANES), 1)
    total = jnp.zeros((size, LANES), F32)
    for q in range(3):
        upper, lower = corner[:, 96 + 2 * q : 97 + 2 * q], corner[:, 97 + 2 * q : 98 + 2 * q]
        member = jnp.floor(upper * 0.25)
        onehot = jnp.where(place == member * 8.0 + lower, 1.0, 0.0).astype(BF16)
        rows = dot_nn(onehot, columns)
        rows = jnp.where(lane_group == upper - 4.0 * member, rows, 0.0).astype(BF16)
        fold = jnp.where((near % 32 == far % 32) & (far // 32 == q), 1.0, 0.0).astype(BF16)
        total = total + dot_nn(rows, fold)
    picked = total.astype(BF16)
    picked_ref[...] = picked
    products = dot_tn(picked, corner.astype(BF16))
    middle = products[:32, :32]
    for q in range(1, 3):
        middle = middle + products[32 * q : 32 * q + 32, 32 * q : 32 * q + 32]
    send_ref[...] = jnp.concatenate([fold_rows(middle), scalars_ref[...]], axis=0)


def coarse_second_body(own_ref, one_ref, two_ref, three_ref, picked_ref, send_ref):
    total = (own_ref[...] + two_ref[...]) + (one_ref[...] + three_ref[...])
    middle = unfold_rows(total[:8])
    rounded = middle.astype(BF16)
    square = jnp.sum(middle * rounded.astype(F32), axis=0, keepdims=True)
    wide = jnp.concatenate([middle] * 4, axis=1)
    wide = jnp.concatenate([wide] * 4, axis=0)
    near = lax.broadcasted_iota(jnp.int32, wide.shape, 0) // 32
    far = lax.broadcasted_iota(jnp.int32, wide.shape, 1) // 32
    diagonal = jnp.where(near == far, wide, 0.0).astype(BF16)
    out = dot_nn(picked_ref[...], diagonal)
    rho, curve = total[8:9, :32], total[9:10, :32] + square
    zero = jnp.zeros((2, 32), F32)
    scalars = jnp.concatenate(three_parts(rho) + three_parts(curve) + [zero], axis=0)
    extra = jnp.concatenate([jnp.zeros((8, 96), F32), scalars], axis=1)
    send_ref[...] = (out.reshape(send_ref.shape) + extra[None]).astype(BF16)


def schur_last_body(coarse_ref, local_ref, fields_ref, sent_ref, maps_ref, *out_refs):
    schur_ref, step_ref, *block_refs = out_refs
    cases = local_ref.shape[0]
    rows = unfold_rows(jnp.sum(coarse_ref[...].astype(F32), axis=0))
    picked = rows[:24].astype(BF16)
    cap = block_refs[0].shape[1]
    blocks = (sent_ref[...] + dot_tn(picked, maps_ref[:24])).astype(BF16)
    for b in range(BLOCKS):
        block_refs[b][...] = blocks[:, b * cap : (b + 1) * cap]
    schur = local_ref[...] + dot_tn(picked, fields_ref[cases : cases + 24])
    schur_ref[...] = schur.astype(BF16)
    rho = jnp.sum(rows[24:27], axis=0, keepdims=True)
    curve = 2.0 * jnp.sum(rows[27:30], axis=0, keepdims=True)
    step_ref[...] = jnp.broadcast_to(row_to_column(rho / curve), step_ref.shape)


def update_body(*refs):
    schur_ref, step_ref, live_ref, direction_ref, residual_ref, columns_ref = refs[
        BLOCKS : BLOCKS + 6
    ]
    multipliers_ref, new_residual_ref = refs[BLOCKS + 6 :]
    multipliers_ref[...] = step_ref[:, 0:1] * direction_ref[...]
    received = to_slots([ref[...] for ref in refs[:BLOCKS]], columns_ref, schur_ref.shape[1])
    image = live_ref[0:1] * (schur_ref[...].astype(F32) - received)
    new_residual_ref[...] = residual_ref[...] - step_ref[:, 0:1] * image


def exchange(blocks):
    count = lax.axis_size("sub")
    received = [None] * BLOCKS
    for b in range(BLOCKS):
        route = [(i, (i + OFFSETS[b]) % count) for i in range(count)]
        received[(b + 3) % BLOCKS] = lax.ppermute(blocks[b], "sub", route)
    return [received[b] for b in RECEIVE_ORDER]


def to_groups(block):
    count = lax.axis_size("grp")
    return [
        lax.ppermute(block, "grp", [(i, (i + k) % count) for i in range(count)])
        for k in range(1, count)
    ]


def on_device(
    load_source,
    schur_diag,
    schur_factor,
    dir_diag,
    dir_factor,
    corner_map,
    corner_row,
    coarse_factor,
    slot_table,
):
    source = load_source[0, 0]
    schur_factor = schur_factor[0, 0]
    dir_factor = dir_factor[0, 0]
    cases, interface = source.shape
    subs, groups = lax.axis_size("sub"), lax.axis_size("grp")
    table = slot_table.reshape(1, -1)
    total = table.shape[1]
    cap = total // BLOCKS
    field = (cases, interface)
    depth, coarse_size = coarse_factor.shape

    def blocks_of(rows):
        return [((rows, cap), BF16)] * BLOCKS

    coarse_rows = [coarse_factor] + to_groups(coarse_factor)
    rows = jnp.concatenate([table.astype(F32), dir_diag[0], schur_diag[0]], axis=0)
    fields = jnp.concatenate([source, corner_map[0, 0]], axis=0)
    fields = jnp.pad(fields, ((0, -fields.shape[0] % 16), (0, 0)))
    columns, *blocks = call(
        first_exchange_body, [((cap, LANES), F32)] + blocks_of(cases), 4, rows, fields
    )
    factor_scratch = [pltpu.VMEM((interface, interface), BF16), pltpu.SemaphoreType.DMA((PIECES,))]
    firsts = exchange(blocks)
    residual, dir_out, live, rho, *blocks = call(
        dirichlet_body,
        [(field, F32), (field, BF16), ((8, interface), F32), ((8, cases), F32)] + blocks_of(cases),
        16,
        *firsts,
        columns,
        rows,
        fields,
        dir_factor,
        scratch=factor_scratch,
        in_hbm=(BLOCKS + 3,),
        vmem=50,
    )
    seconds = exchange(blocks)
    *coarse_rows, corner, rho = lax.optimization_barrier((*coarse_rows, corner_row[0], rho))
    away = (lax.axis_index("grp") - corner // 8 % 4) % groups
    corner = ((corner // 32 * 4 + away) * 8 + corner % 8).astype(F32)
    corner = jnp.pad(corner, ((0, 0), (0, LANES - corner.shape[1])))
    (dealt,) = call(deal_columns_body, [((subs, depth, LANES), BF16)], 2, *coarse_rows)
    direction, corner_in = call(
        schur_first_body,
        [(field, F32), ((subs, depth, 2 * LANES), BF16)],
        16,
        *seconds,
        dir_out,
        live,
        columns,
        fields,
        corner,
        dealt,
    )
    corner_in = lax.all_to_all(corner_in, "sub", 0, 0, tiled=True)
    spare = fields.shape[0] - cases
    local, sent, maps, scalars = call(
        schur_second_body,
        [(field, F32), (field, F32), ((spare, total), BF16), ((8, LANES), F32)],
        8,
        direction,
        rho,
        rows,
        fields,
        schur_factor,
        scratch=factor_scratch,
        in_hbm=(4,),
        vmem=50,
    )
    picked, parts = call(
        coarse_first_body,
        [((subs * depth, LANES), BF16), ((16, LANES), F32)],
        4,
        corner_in,
        scalars,
    )
    local, parts = lax.optimization_barrier((local, parts))
    (coarse,) = call(
        coarse_second_body,
        [((subs, 8, LANES), BF16)],
        2,
        parts,
        *to_groups(parts),
        picked,
    )
    coarse = lax.all_to_all(coarse, "sub", 0, 0, tiled=True)
    schur_out, step, *blocks = call(
        schur_last_body,
        [(field, BF16), ((cases, LANES), F32)] + blocks_of(cases),
        8,
        coarse,
        local,
        fields,
        sent,
        maps,
    )
    multipliers, residual = call(
        update_body,
        [(field, F32), (field, F32)],
        8,
        *exchange(blocks),
        schur_out,
        step,
        live,
        direction,
        residual,
        columns,
    )
    return (multipliers[None, None], residual[None, None])


def solution(mesh):
    return jax.shard_map(
        on_device,
        mesh=mesh,
        in_specs=(
            P("grp", "sub", None, None),
            P("grp", "sub", None),
            P("grp", "sub", None, None),
            P("grp", "sub", None),
            P("grp", "sub", None, None),
            P("grp", "sub", None, None),
            P("grp", "sub", None),
            P(("sub", "grp"), None),
            P("grp", "sub", None, None),
        ),
        out_specs=(P("grp", "sub", None, None), P("grp", "sub", None, None)),
        check_vma=False,
    )
```

time: 105 us -> 98.9 us (0.942)
  Pallas kernels: 20.5 us -> 17 us
  starting transfers between devices: 43.3 us -> 40.3 us
    pallas_call x9, Pallas kernels: 20.5 us -> 17 us  [call(): pl.pallas_call(body, out_shape=[jax.ShapeDtypeStruct(shape, dtype) for sh...]
    ppermute x18, starting transfers between devices: 30.6 us -> 28.2 us  [exchange(): received[(b + 3) % BLOCKS] = lax.ppermute(blocks[b], 'sub', route)]
    ppermute x18, waiting for transfers between devices: 7.24 us -> 9.14 us  [exchange(): received[(b + 3) % BLOCKS] = lax.ppermute(blocks[b], 'sub', route)]
  transfers between devices with their start and end apart: 25 -> 25, of which waited for: 9 -> 9; matrix products, arithmetic and copies ran while one was open for 0% -> 0% of each run, Pallas kernels for 10% -> 11%
where the time goes in v3:
time: 98.9 us; the launch traced here: 98.6 us
  starting transfers between devices  40.3 us (41%)
  waiting for transfers between devices  21.2 us (21%)
  Pallas kernels  17 us (17%)
  blocking collectives  16.8 us (17%)
  other arithmetic  2.41 us (2%)
    ppermute x18, starting transfers between devices, exchange(): received[(b + 3) % BLOCKS] = lax.ppermute(blocks[b], 'sub', route)  28.2 us
    pallas_call x9, Pallas kernels, call(): pl.pallas_call(body, out_shape=[jax.ShapeDtypeStruct(shape, dtype) for sh...  17 us
    all_to_all x1, blocking collectives, on_device(): coarse = lax.all_to_all(coarse, 'sub', 0, 0, tiled=True)  16.8 us
    ppermute x18, waiting for transfers between devices, exchange(): received[(b + 3) % BLOCKS] = lax.ppermute(blocks[b], 'sub', route)  9.14 us
    all_to_all x1, waiting for transfers between devices, on_device(): corner_in = lax.all_to_all(corner_in, 'sub', 0, 0, tiled=True)  8.34 us
    ppermute x6, starting transfers between devices, to_groups(): lax.ppermute(block, 'grp', [(i, (i + k) % count) for i in range(count)])  7.02 us
    all_to_all x1, starting transfers between devices, on_device(): corner_in = lax.all_to_all(corner_in, 'sub', 0, 0, tiled=True)  5.1 us
    ppermute x6, waiting for transfers between devices, to_groups(): lax.ppermute(block, 'grp', [(i, (i + k) % count) for i in range(count)])  3.69 us
  transfers between devices with their start and end apart: 25, of which 9 were waited for; matrix products, arithmetic and copies ran while one was open for 0% of the time, Pallas kernels for 11%

profile of v3, /device:TPU:1, one launch (start us, length us, event | category | flops | bytes accessed | tf_op | source)
XLA Modules:
  0.0 98.6 jit_solution(16046804235863146848)
XLA Ops:
  4.0 9.6 %collective-permute-start = (bf16[32,256]{1,0:T(8,128)(2,1)S(1)}, bf16[32,256]{1,0:T(8,128)(2,1)S(1)}, u32[]{:S(2)}, u32[]{:S(2)}) collective-permute-start(bf16[32,256]{1,0:T(8,128)(2,1)S(1)} %get-tuple-element.45), channel_id=1, source_target_pairs={{0,236},{4,240},{8,244},{12,248},{16,252},{20,0},{24,4},{28,8},{32... | collective-permute-start | bytes 49160 | tf_op jit(solution)/shard_map/ppermute | solution.py:314
  14.4 2.0 %collective-permute-start.3 = (bf16[32,256]{1,0:T(8,128)(2,1)S(1)}, bf16[32,256]{1,0:T(8,128)(2,1)S(1)}, u32[]{:S(2)}, u32[]{:S(2)}) collective-permute-start(bf16[32,256]{1,0:T(8,128)(2,1)S(1)} %get-tuple-element.48), channel_id=1, source_target_pairs={{0,20},{4,24},{8,28},{12,32},{16,36},{20,40},{24,44},{28,48},{32,5... | collective-permute-start | bytes 49160 | tf_op jit(solution)/shard_map/ppermute | solution.py:314
  17.1 2.7 %collective-permute-start.13 = (bf16[8,2048]{1,0:T(8,128)(2,1)}, bf16[8,2048]{1,0:T(8,128)(2,1)S(1)}, u32[]{:S(2)}, u32[]{:S(2)}) collective-permute-start(bf16[8,2048]{1,0:T(8,128)(2,1)} %own_ref), channel_id=1, source_target_pairs={{0,2},{1,3},{2,0},{3,1},{4,6},{5,7},{6,4},{7,5},{8,10},{9,11},{10,... | collective-permute-start | bytes 98312 | tf_op jit(solution)/shard_map/ppermute | solution.py:321
  20.2 1.2 %collective-permute-done.3.refs_3_ = bf16[32,256]{1,0:T(8,128)(2,1)S(1)} collective-permute-done((bf16[32,256]{1,0:T(8,128)(2,1)S(1)}, bf16[32,256]{1,0:T(8,128)(2,1)S(1)}, u32[]{:S(2)}, u32[]{:S(2)}) %collective-permute-start.3) | collective-permute-done | bytes 16416 | tf_op jit(solution)/shard_map/ppermute | solution.py:314
  21.3 2.5 %collective-permute-start.14 = (bf16[8,2048]{1,0:T(8,128)(2,1)}, bf16[8,2048]{1,0:T(8,128)(2,1)S(1)}, u32[]{:S(2)}, u32[]{:S(2)}) collective-permute-start(bf16[8,2048]{1,0:T(8,128)(2,1)} %own_ref), channel_id=1, source_target_pairs={{0,3},{1,0},{2,1},{3,2},{4,7},{5,4},{6,5},{7,6},{8,11},{9,8},{10,9... | collective-permute-start | bytes 98312 | tf_op jit(solution)/shard_map/ppermute | solution.py:321
  23.8 5.4 %shard_map.105 = (f32[32,1536]{1,0:T(8,128)S(1)}, bf16[32,1536]{1,0:T(8,128)(2,1)S(1)}, f32[8,1536]{1,0:T(8,128)S(1)}, f32[8,32]{1,0:T(8,128)S(1)}, bf16[32,256]...) custom-call(bf16[32,256]{1,0:T(8,128)(2,1)S(1)} %collective-permute-, ...), custom_call_target="tpu_custom_call" | custom-call | flops 16777216 | bytes 16777216 | tf_op jit(solution)/shard_map/pallas_call | solution.py:63
  29.2 4.0 %collective-permute-start.6 = (bf16[32,256]{1,0:T(8,128)(2,1)S(1)}, bf16[32,256]{1,0:T(8,128)(2,1)S(1)}, u32[]{:S(2)}, u32[]{:S(2)}) collective-permute-start(bf16[32,256]{1,0:T(8,128)(2,1)S(1)} %get-tuple-element.52), channel_id=1, source_target_pairs={{0,236},{4,240},{8,244},{12,248},{16,252},{20,0},{24,4},{28,8},{32... | collective-permute-start | bytes 49160 | tf_op jit(solution)/shard_map/ppermute | solution.py:314
  33.1 1.1 %collective-permute-start.7 = (bf16[32,256]{1,0:T(8,128)(2,1)S(1)}, bf16[32,256]{1,0:T(8,128)(2,1)S(1)}, u32[]{:S(2)}, u32[]{:S(2)}) collective-permute-start(bf16[32,256]{1,0:T(8,128)(2,1)S(1)} %get-tuple-element.53), channel_id=1, source_target_pairs={{0,248},{4,252},{8,0},{12,4},{16,8},{20,12},{24,16},{28,20},{32,24... | collective-permute-start | bytes 49160 | tf_op jit(solution)/shard_map/ppermute | solution.py:314
  34.2 2.0 %collective-permute-start.9 = (bf16[32,256]{1,0:T(8,128)(2,1)S(1)}, bf16[32,256]{1,0:T(8,128)(2,1)S(1)}, u32[]{:S(2)}, u32[]{:S(2)}) collective-permute-start(bf16[32,256]{1,0:T(8,128)(2,1)S(1)} %get-tuple-element.55), channel_id=1, source_target_pairs={{0,20},{4,24},{8,28},{12,32},{16,36},{20,40},{24,44},{28,48},{32,5... | collective-permute-start | bytes 49160 | tf_op jit(solution)/shard_map/ppermute | solution.py:314
  37.4 3.8 %collective-permute-done.9.refs_3_ = bf16[32,256]{1,0:T(8,128)(2,1)S(1)} collective-permute-done((bf16[32,256]{1,0:T(8,128)(2,1)S(1)}, bf16[32,256]{1,0:T(8,128)(2,1)S(1)}, u32[]{:S(2)}, u32[]{:S(2)}) %collective-permute-start.9) | collective-permute-done | bytes 16416 | tf_op jit(solution)/shard_map/ppermute | solution.py:314
  42.1 1.9 %shard_map.107 = (f32[32,1536]{1,0:T(8,128)S(1)}, bf16[64,8,256]{2,1,0:T(8,128)(2,1)}) custom-call(bf16[32,256]{1,0:T(8,128)(2,1)S(1)} %collective-permute-done.6.refs_0_, bf16[32,256]{1,0:T(8,128)(2,1)S(1)} %collective-permute-done.7.refs_1_, bf16[32,256]{1,0:T(8,128)(2,1)S(1)} %collective-permute-done.8.refs_2_, ...), custom_call_target="tpu_custom_call" | custom-call | flops 16777216 | bytes 16777216 | tf_op jit(solution)/shard_map/pallas_call | solution.py:63
  44.1 5.1 %all-to-all-start = ((bf16[64,8,256]{2,1,0:T(8,128)(2,1)}), bf16[64,8,256]{2,1,0:T(8,128)(2,1)S(1)}, u32[]{:S(2)}, u32[]{:S(2)}) async-start(bf16[64,8,256]{2,1,0:T(8,128)(2,1)} %get-tuple-element.69), calls=%async_computation | async-start | bytes 524288 | tf_op jit(solution)/shard_map/all_to_all | solution.py:391
  49.2 4.9 %shard_map.108 = (f32[32,1536]{1,0:T(8,128)S(1)}, f32[32,1536]{1,0:T(8,128)S(1)}, bf16[32,1536]{1,0:T(8,128)(2,1)S(1)}, f32[8,128]{1,0:T(8,128)S(1)}) custom-call(f32[32,1536]{1,0:T(8,128)S(1)} %get-tuple-element.66.direction_ref.refs_9_, f32[8,32]{1,0:T(8,128)S(1)} %get-tuple-element.67.rho_ref, f32[3,1536]{1,0:T(4,128)S(1)} %pad_maximum_fusion.rows_ref.refs_7_, ...), custom_call_target="tpu_custom_call" | custom-call | flops 8388608 | bytes 8388608 | tf_op jit(solution)/shard_map/pallas_call | solution.py:63
  54.1 8.3 %all-to-all-done.sent_ref = bf16[64,8,256]{2,1,0:T(8,128)(2,1)S(1)} async-done(((bf16[64,8,256]{2,1,0:T(8,128)(2,1)}), bf16[64,8,256]{2,1,0:T(8,128)(2,1)S(1)}, u32[]{:S(2)}, u32[]{:S(2)}) %all-to-all-start) | async-done | bytes 262176 | tf_op jit(solution)/shard_map/all_to_all | solution.py:391
  62.4 1.3 %shard_map.109 = (bf16[512,128]{1,0:T(8,128)(2,1)S(1)}, f32[16,128]{1,0:T(8,128)S(1)}) custom-call(bf16[64,8,256]{2,1,0:T(8,128)(2,1)S(1)} %all-to-all-done.sent_ref, f32[8,128]{1,0:T(8,128)S(1)} %get-tuple-element.70.scalars_ref), custom_call_target="tpu_custom_call" | custom-call | flops 4194304 | bytes 4194304 | tf_op jit(solution)/shard_map/pallas_call | solution.py:63
  65.3 1.0 %collective-permute-done.17.three_ref = f32[16,128]{1,0:T(8,128)S(1)} collective-permute-done((f32[16,128]{1,0:T(8,128)S(1)}, f32[16,128]{1,0:T(8,128)S(1)}, u32[]{:S(2)}, u32[]{:S(2)}) %collective-permute-start.17) | collective-permute-done | bytes 8224 | tf_op jit(solution)/shard_map/ppermute | solution.py:321
  66.3 1.6 %collective-permute-done.16.two_ref = f32[16,128]{1,0:T(8,128)S(1)} collective-permute-done((f32[16,128]{1,0:T(8,128)S(1)}, f32[16,128]{1,0:T(8,128)S(1)}, u32[]{:S(2)}, u32[]{:S(2)}) %collective-permute-start.16) | collective-permute-done | bytes 8224 | tf_op jit(solution)/shard_map/ppermute | solution.py:321
  67.9 1.0 %collective-permute-done.15.one_ref = f32[16,128]{1,0:T(8,128)S(1)} collective-permute-done((f32[16,128]{1,0:T(8,128)S(1)}, f32[16,128]{1,0:T(8,128)S(1)}, u32[]{:S(2)}, u32[]{:S(2)}) %collective-permute-start.15) | collective-permute-done | bytes 8224 | tf_op jit(solution)/shard_map/ppermute | solution.py:321
  69.3 16.8 %all_to_all.10.coarse_ref = bf16[64,8,128]{2,1,0:T(8,128)(2,1)S(1)} all-to-all(bf16[64,8,128]{2,1,0:T(8,128)(2,1)S(1)} %shard_map.110), channel_id=1, replica_groups=mesh['sub'=64,'grp'=4] {'sub'}, dimensions={0} | all-to-all | bytes 262144 | tf_op jit(solution)/shard_map/all_to_all | solution.py:422
  87.4 1.9 %collective-permute-start.19 = (bf16[32,256]{1,0:T(8,128)(2,1)S(1)}, bf16[32,256]{1,0:T(8,128)(2,1)S(1)}, u32[]{:S(2)}, u32[]{:S(2)}) collective-permute-start(bf16[32,256]{1,0:T(8,128)(2,1)S(1)} %get-tuple-element.78), channel_id=1, source_target_pairs={{0,248},{4,252},{8,0},{12,4},{16,8},{20,12},{24,16},{28,20},{32,24... | collective-permute-start | bytes 49160 | tf_op jit(solution)/shard_map/ppermute | solution.py:314
  90.8 1.9 %collective-permute-start.22 = (bf16[32,256]{1,0:T(8,128)(2,1)S(1)}, bf16[32,256]{1,0:T(8,128)(2,1)S(1)}, u32[]{:S(2)}, u32[]{:S(2)}) collective-permute-start(bf16[32,256]{1,0:T(8,128)(2,1)S(1)} %get-tuple-element.81), channel_id=1, source_target_pairs={{0,8},{4,12},{8,16},{12,20},{16,24},{20,28},{24,32},{28,36},{32,40... | collective-permute-start | bytes 49160 | tf_op jit(solution)/shard_map/ppermute | solution.py:314
  92.7 1.3 %collective-permute-start.23 = (bf16[32,256]{1,0:T(8,128)(2,1)S(1)}, bf16[32,256]{1,0:T(8,128)(2,1)S(1)}, u32[]{:S(2)}, u32[]{:S(2)}) collective-permute-start(bf16[32,256]{1,0:T(8,128)(2,1)S(1)} %get-tuple-element.82), channel_id=1, source_target_pairs={{0,4},{4,8},{8,12},{12,16},{16,20},{20,24},{24,28},{28,32},{32,36}... | collective-permute-start | bytes 49160 | tf_op jit(solution)/shard_map/ppermute | solution.py:314
  94.0 2.9 %collective-permute-done.21.refs_3_ = bf16[32,256]{1,0:T(8,128)(2,1)S(1)} collective-permute-done((bf16[32,256]{1,0:T(8,128)(2,1)S(1)}, bf16[32,256]{1,0:T(8,128)(2,1)S(1)}, u32[]{:S(2)}, u32[]{:S(2)}) %collective-permute-start.21) | collective-permute-done | bytes 16416 | tf_op jit(solution)/shard_map/ppermute | solution.py:314
  96.9 1.7 %shard_map.112 = (f32[32,1536]{1,0:T(8,128)}, f32[32,1536]{1,0:T(8,128)}) custom-call(bf16[32,256]{1,0:T(8,128)(2,1)S(1)} %collective-permute-done.18.refs_0_, bf16[32,256]{1,0:T(8,128)(2,1)S(1)} %collective-permute-done.19.refs_1_, bf16[32,256]{1,0:T(8,128)(2,1)S(1)} %collective-permute-done.20.refs_2_, ...), custom_call_target="tpu_custom_call" | custom-call | flops 8388608 | bytes 8388608 | tf_op jit(solution)/shard_map/pallas_call | solution.py:63
  (45 shorter events, 11.8 us)
Async XLA Ops:
  4.0 12.4 %collective-permute-start = (bf16[32,256]{1,0:T(8,128)(2,1)S(1)}, bf16[32,256]{1,0:T(8,128)(2,1)S(1)}, u32[]{:S(2)}, u32[]{:S(2)}) collective-permute-start(bf16[32,256]{1,0:T(8,128)(2,1)S(1)} %get-tuple-element.45), channel_id=1, source_target_pairs={{0,236},{4,240},{8,244},{12,248},{16,252},{20,0},{24,4},{28,8},{32... | collective-permute-start | bytes 49160 | tf_op jit(solution)/shard_map/ppermute | solution.py:314
  13.6 3.5 %collective-permute-start.1 = (bf16[32,256]{1,0:T(8,128)(2,1)S(1)}, bf16[32,256]{1,0:T(8,128)(2,1)S(1)}, u32[]{:S(2)}, u32[]{:S(2)}) collective-permute-start(bf16[32,256]{1,0:T(8,128)(2,1)S(1)} %get-tuple-element.46), channel_id=1, source_target_pairs={{0,248},{4,252},{8,0},{12,4},{16,8},{20,12},{24,16},{28,20},{32,24... | collective-permute-start | bytes 49160 | tf_op jit(solution)/shard_map/ppermute | solution.py:314
  14.4 5.5 %collective-permute-start.2 = (bf16[32,256]{1,0:T(8,128)(2,1)S(1)}, bf16[32,256]{1,0:T(8,128)(2,1)S(1)}, u32[]{:S(2)}, u32[]{:S(2)}) collective-permute-start(bf16[32,256]{1,0:T(8,128)(2,1)S(1)} %get-tuple-element.47), channel_id=1, source_target_pairs={{0,252},{4,0},{8,4},{12,8},{16,12},{20,16},{24,20},{28,24},{32,28}... | collective-permute-start | bytes 49160 | tf_op jit(solution)/shard_map/ppermute | solution.py:314
  14.4 6.9 %collective-permute-start.3 = (bf16[32,256]{1,0:T(8,128)(2,1)S(1)}, bf16[32,256]{1,0:T(8,128)(2,1)S(1)}, u32[]{:S(2)}, u32[]{:S(2)}) collective-permute-start(bf16[32,256]{1,0:T(8,128)(2,1)S(1)} %get-tuple-element.48), channel_id=1, source_target_pairs={{0,20},{4,24},{8,28},{12,32},{16,36},{20,40},{24,44},{28,48},{32,5... | collective-permute-start | bytes 49160 | tf_op jit(solution)/shard_map/ppermute | solution.py:314
  16.3 7.5 %collective-permute-start.4 = (bf16[32,256]{1,0:T(8,128)(2,1)S(1)}, bf16[32,256]{1,0:T(8,128)(2,1)S(1)}, u32[]{:S(2)}, u32[]{:S(2)}) collective-permute-start(bf16[32,256]{1,0:T(8,128)(2,1)S(1)} %get-tuple-element.49), channel_id=1, source_target_pairs={{0,8},{4,12},{8,16},{12,20},{16,24},{20,28},{24,32},{28,36},{32,40... | collective-permute-start | bytes 49160 | tf_op jit(solution)/shard_map/ppermute | solution.py:314
  16.3 7.4 %collective-permute-start.5 = (bf16[32,256]{1,0:T(8,128)(2,1)S(1)}, bf16[32,256]{1,0:T(8,128)(2,1)S(1)}, u32[]{:S(2)}, u32[]{:S(2)}) collective-permute-start(bf16[32,256]{1,0:T(8,128)(2,1)S(1)} %get-tuple-element.50), channel_id=1, source_target_pairs={{0,4},{4,8},{8,12},{12,16},{16,20},{20,24},{24,28},{28,32},{32,36}... | collective-permute-start | bytes 49160 | tf_op jit(solution)/shard_map/ppermute | solution.py:314
  17.1 17.1 %collective-permute-start.13 = (bf16[8,2048]{1,0:T(8,128)(2,1)}, bf16[8,2048]{1,0:T(8,128)(2,1)S(1)}, u32[]{:S(2)}, u32[]{:S(2)}) collective-permute-start(bf16[8,2048]{1,0:T(8,128)(2,1)} %own_ref), channel_id=1, source_target_pairs={{0,2},{1,3},{2,0},{3,1},{4,6},{5,7},{6,4},{7,5},{8,10},{9,11},{10,... | collective-permute-start | bytes 98312 | tf_op jit(solution)/shard_map/ppermute | solution.py:321
  19.8 14.4 %collective-permute-start.12 = (bf16[8,2048]{1,0:T(8,128)(2,1)}, bf16[8,2048]{1,0:T(8,128)(2,1)S(1)}, u32[]{:S(2)}, u32[]{:S(2)}) collective-permute-start(bf16[8,2048]{1,0:T(8,128)(2,1)} %own_ref), channel_id=1, source_target_pairs={{0,1},{1,2},{2,3},{3,0},{4,5},{5,6},{6,7},{7,4},{8,9},{9,10},{10,1... | collective-permute-start | bytes 98312 | tf_op jit(solution)/shard_map/ppermute | solution.py:321
  21.3 14.9 %collective-permute-start.14 = (bf16[8,2048]{1,0:T(8,128)(2,1)}, bf16[8,2048]{1,0:T(8,128)(2,1)S(1)}, u32[]{:S(2)}, u32[]{:S(2)}) collective-permute-start(bf16[8,2048]{1,0:T(8,128)(2,1)} %own_ref), channel_id=1, source_target_pairs={{0,3},{1,0},{2,1},{3,2},{4,7},{5,4},{6,5},{7,6},{8,11},{9,8},{10,9... | collective-permute-start | bytes 98312 | tf_op jit(solution)/shard_map/ppermute | solution.py:321
  29.2 7.0 %collective-permute-start.6 = (bf16[32,256]{1,0:T(8,128)(2,1)S(1)}, bf16[32,256]{1,0:T(8,128)(2,1)S(1)}, u32[]{:S(2)}, u32[]{:S(2)}) collective-permute-start(bf16[32,256]{1,0:T(8,128)(2,1)S(1)} %get-tuple-element.52), channel_id=1, source_target_pairs={{0,236},{4,240},{8,244},{12,248},{16,252},{20,0},{24,4},{28,8},{32... | collective-permute-start | bytes 49160 | tf_op jit(solution)/shard_map/ppermute | solution.py:314
  33.1 3.9 %collective-permute-start.7 = (bf16[32,256]{1,0:T(8,128)(2,1)S(1)}, bf16[32,256]{1,0:T(8,128)(2,1)S(1)}, u32[]{:S(2)}, u32[]{:S(2)}) collective-permute-start(bf16[32,256]{1,0:T(8,128)(2,1)S(1)} %get-tuple-element.53), channel_id=1, source_target_pairs={{0,248},{4,252},{8,0},{12,4},{16,8},{20,12},{24,16},{28,20},{32,24... | collective-permute-start | bytes 49160 | tf_op jit(solution)/shard_map/ppermute | solution.py:314
  34.2 3.2 %collective-permute-start.8 = (bf16[32,256]{1,0:T(8,128)(2,1)S(1)}, bf16[32,256]{1,0:T(8,128)(2,1)S(1)}, u32[]{:S(2)}, u32[]{:S(2)}) collective-permute-start(bf16[32,256]{1,0:T(8,128)(2,1)S(1)} %get-tuple-element.54), channel_id=1, source_target_pairs={{0,252},{4,0},{8,4},{12,8},{16,12},{20,16},{24,20},{28,24},{32,28}... | collective-permute-start | bytes 49160 | tf_op jit(solution)/shard_map/ppermute | solution.py:314
  34.2 6.9 %collective-permute-start.9 = (bf16[32,256]{1,0:T(8,128)(2,1)S(1)}, bf16[32,256]{1,0:T(8,128)(2,1)S(1)}, u32[]{:S(2)}, u32[]{:S(2)}) collective-permute-start(bf16[32,256]{1,0:T(8,128)(2,1)S(1)} %get-tuple-element.55), channel_id=1, source_target_pairs={{0,20},{4,24},{8,28},{12,32},{16,36},{20,40},{24,44},{28,48},{32,5... | collective-permute-start | bytes 49160 | tf_op jit(solution)/shard_map/ppermute | solution.py:314
  36.2 5.9 %collective-permute-start.10 = (bf16[32,256]{1,0:T(8,128)(2,1)S(1)}, bf16[32,256]{1,0:T(8,128)(2,1)S(1)}, u32[]{:S(2)}, u32[]{:S(2)}) collective-permute-start(bf16[32,256]{1,0:T(8,128)(2,1)S(1)} %get-tuple-element.56), channel_id=1, source_target_pairs={{0,8},{4,12},{8,16},{12,20},{16,24},{20,28},{24,32},{28,36},{32,40... | collective-permute-start | bytes 49160 | tf_op jit(solution)/shard_map/ppermute | solution.py:314
  36.2 5.9 %collective-permute-start.11 = (bf16[32,256]{1,0:T(8,128)(2,1)S(1)}, bf16[32,256]{1,0:T(8,128)(2,1)S(1)}, u32[]{:S(2)}, u32[]{:S(2)}) collective-permute-start(bf16[32,256]{1,0:T(8,128)(2,1)S(1)} %get-tuple-element.57), channel_id=1, source_target_pairs={{0,4},{4,8},{8,12},{12,16},{16,20},{20,24},{24,28},{28,32},{32,36}... | collective-permute-start | bytes 49160 | tf_op jit(solution)/shard_map/ppermute | solution.py:314
  44.1 18.4 %all-to-all-start = ((bf16[64,8,256]{2,1,0:T(8,128)(2,1)}), bf16[64,8,256]{2,1,0:T(8,128)(2,1)S(1)}, u32[]{:S(2)}, u32[]{:S(2)}) async-start(bf16[64,8,256]{2,1,0:T(8,128)(2,1)} %get-tuple-element.69), calls=%async_computation | async-start | bytes 524288 | tf_op jit(solution)/shard_map/all_to_all | solution.py:391
  63.8 4.1 %collective-permute-start.16 = (f32[16,128]{1,0:T(8,128)S(1)}, f32[16,128]{1,0:T(8,128)S(1)}, u32[]{:S(2)}, u32[]{:S(2)}) collective-permute-start(f32[16,128]{1,0:T(8,128)S(1)} %get-tuple-element.72.own_ref), channel_id=1, source_target_pairs={{0,2},{1,3},{2,0},{3,1},{4,6},{5,7},{6,4},{7,5},{8,10},{9,11},{10,... | collective-permute-start | bytes 24584 | tf_op jit(solution)/shard_map/ppermute | solution.py:321
  64.7 4.3 %collective-permute-start.15 = (f32[16,128]{1,0:T(8,128)S(1)}, f32[16,128]{1,0:T(8,128)S(1)}, u32[]{:S(2)}, u32[]{:S(2)}) collective-permute-start(f32[16,128]{1,0:T(8,128)S(1)} %get-tuple-element.72.own_ref), channel_id=1, source_target_pairs={{0,1},{1,2},{2,3},{3,0},{4,5},{5,6},{6,7},{7,4},{8,9},{9,10},{10,1... | collective-permute-start | bytes 24584 | tf_op jit(solution)/shard_map/ppermute | solution.py:321
  86.5 6.3 %collective-permute-start.18 = (bf16[32,256]{1,0:T(8,128)(2,1)S(1)}, bf16[32,256]{1,0:T(8,128)(2,1)S(1)}, u32[]{:S(2)}, u32[]{:S(2)}) collective-permute-start(bf16[32,256]{1,0:T(8,128)(2,1)S(1)} %get-tuple-element.77), channel_id=1, source_target_pairs={{0,236},{4,240},{8,244},{12,248},{16,252},{20,0},{24,4},{28,8},{32... | collective-permute-start | bytes 49160 | tf_op jit(solution)/shard_map/ppermute | solution.py:314
  87.4 6.7 %collective-permute-start.19 = (bf16[32,256]{1,0:T(8,128)(2,1)S(1)}, bf16[32,256]{1,0:T(8,128)(2,1)S(1)}, u32[]{:S(2)}, u32[]{:S(2)}) collective-permute-start(bf16[32,256]{1,0:T(8,128)(2,1)S(1)} %get-tuple-element.78), channel_id=1, source_target_pairs={{0,248},{4,252},{8,0},{12,4},{16,8},{20,12},{24,16},{28,20},{32,24... | collective-permute-start | bytes 49160 | tf_op jit(solution)/shard_map/ppermute | solution.py:314
  89.3 4.7 %collective-permute-start.20 = (bf16[32,256]{1,0:T(8,128)(2,1)S(1)}, bf16[32,256]{1,0:T(8,128)(2,1)S(1)}, u32[]{:S(2)}, u32[]{:S(2)}) collective-permute-start(bf16[32,256]{1,0:T(8,128)(2,1)S(1)} %get-tuple-element.79), channel_id=1, source_target_pairs={{0,252},{4,0},{8,4},{12,8},{16,12},{20,16},{24,20},{28,24},{32,28}... | collective-permute-start | bytes 49160 | tf_op jit(solution)/shard_map/ppermute | solution.py:314
  90.1 6.8 %collective-permute-start.21 = (bf16[32,256]{1,0:T(8,128)(2,1)S(1)}, bf16[32,256]{1,0:T(8,128)(2,1)S(1)}, u32[]{:S(2)}, u32[]{:S(2)}) collective-permute-start(bf16[32,256]{1,0:T(8,128)(2,1)S(1)} %get-tuple-element.80), channel_id=1, source_target_pairs={{0,20},{4,24},{8,28},{12,32},{16,36},{20,40},{24,44},{28,48},{32,5... | collective-permute-start | bytes 49160 | tf_op jit(solution)/shard_map/ppermute | solution.py:314
  90.8 6.1 %collective-permute-start.22 = (bf16[32,256]{1,0:T(8,128)(2,1)S(1)}, bf16[32,256]{1,0:T(8,128)(2,1)S(1)}, u32[]{:S(2)}, u32[]{:S(2)}) collective-permute-start(bf16[32,256]{1,0:T(8,128)(2,1)S(1)} %get-tuple-element.81), channel_id=1, source_target_pairs={{0,8},{4,12},{8,16},{12,20},{16,24},{20,28},{24,32},{28,36},{32,40... | collective-permute-start | bytes 49160 | tf_op jit(solution)/shard_map/ppermute | solution.py:314
  92.7 4.2 %collective-permute-start.23 = (bf16[32,256]{1,0:T(8,128)(2,1)S(1)}, bf16[32,256]{1,0:T(8,128)(2,1)S(1)}, u32[]{:S(2)}, u32[]{:S(2)}) collective-permute-start(bf16[32,256]{1,0:T(8,128)(2,1)S(1)} %get-tuple-element.82), channel_id=1, source_target_pairs={{0,4},{4,8},{8,12},{12,16},{16,20},{20,24},{24,28},{28,32},{32,36}... | collective-permute-start | bytes 49160 | tf_op jit(solution)/shard_map/ppermute | solution.py:314
  (3 other events, 74.8 us)

commit v4 on v3

--- a/solution.py
+++ b/solution.py
@@ -10,7 +10,7 @@
 F32 = jnp.float32
 BF16 = jnp.bfloat16
 LANES = 128
-PIECES = 3
+PIECES = 6
 RECEIVE_ORDER = (2, 1, 0, 5, 4, 3)
 TABLE, DIR_DIAG, SCHUR_DIAG = 0, 1, 2
 
@@ -154,13 +154,12 @@
 
 
 def schur_first_body(*refs):
-    out_ref, live_ref, columns_ref, fields_ref, index_ref, dealt_ref = refs[BLOCKS : BLOCKS + 6]
-    direction_ref, send_ref = refs[BLOCKS + 6 :]
-    cases, interface = out_ref.shape
-    received = to_slots([ref[...] for ref in refs[:BLOCKS]], columns_ref, interface)
-    direction = 0.5 * (live_ref[0:1] * (out_ref[...].astype(F32) - received))
-    direction_ref[...] = direction
-    corner_in = dot_nt(fields_ref[cases : cases + 24], direction.astype(BF16))
+    maps_ref, mine_ref, index_ref, dealt_ref, send_ref = refs[BLOCKS:]
+    cap = refs[0].shape[1]
+    corner_in = mine_ref[...]
+    for ref, b in zip(refs[:BLOCKS], RECEIVE_ORDER):
+        corner_in = corner_in - dot_nt(maps_ref[:24, b * cap : (b + 1) * cap], ref[...])
+    corner_in = 0.5 * corner_in
     groups = [corner_in[0:8], corner_in[8:16], corner_in[16:24], index_lanes(index_ref[...])]
     tile = jnp.concatenate(groups, axis=1).astype(BF16)
     count, depth, _ = send_ref.shape
@@ -168,35 +167,25 @@
     send_ref[:, :, LANES:] = dealt_ref[...]
 
 
-def schur_second_body(
-    direction_ref,
-    rho_ref,
-    rows_ref,
-    fields_ref,
-    factor_ref,
-    local_ref,
-    sent_ref,
-    maps_ref,
-    scalars_ref,
-    held_ref,
-    semaphores,
-):
+def schur_second_body(*refs):
+    out_ref, live_ref, columns_ref, rho_ref, rows_ref, factor_ref = refs[BLOCKS : BLOCKS + 6]
+    direction_ref, local_ref, sent_ref, scalars_ref, held_ref, semaphores = refs[BLOCKS + 6 :]
     copies = load_factor(factor_ref, held_ref, semaphores)
-    direction = direction_ref[...]
+    received = to_slots([ref[...] for ref in refs[:BLOCKS]], columns_ref, out_ref.shape[1])
+    direction = 0.5 * (live_ref[0:1] * (out_ref[...].astype(F32) - received))
+    direction_ref[...] = direction
     wide = times_factor(direction.astype(BF16), held_ref, copies)
     middle = wide.astype(BF16)
     scaled = rows_ref[SCHUR_DIAG : SCHUR_DIAG + 1] * direction
     local = scaled + dot_nt(middle, held_ref[...])
     local_ref[...] = local
     cases, interface = local.shape
-    values = [part.astype(BF16) for part in three_parts(local)] + [fields_ref[cases:]]
-    values = jnp.concatenate(values, axis=0)
+    values = jnp.concatenate([part.astype(BF16) for part in three_parts(local)], axis=0)
     cap = interface // BLOCKS
     for b in range(BLOCKS):
         picked = at_slots(values, rows_ref[TABLE : TABLE + 1], b)
-        exact = (picked[:cases] + picked[cases : 2 * cases]) + picked[2 * cases : 3 * cases]
+        exact = (picked[:cases] + picked[cases : 2 * cases]) + picked[2 * cases :]
         sent_ref[:, b * cap : (b + 1) * cap] = exact
-        maps_ref[:, b * cap : (b + 1) * cap] = picked[3 * cases :].astype(BF16)
     curve = jnp.sum(scaled * direction, axis=1, keepdims=True)
     curve = curve + jnp.sum(wide * middle.astype(F32), axis=1, keepdims=True)
     scalars = [rho_ref[0:1], column_to_row(curve), jnp.zeros((6, curve.shape[0]), F32)]
@@ -218,8 +207,15 @@
     return tile
 
 
-def deal_columns_body(own_ref, one_ref, two_ref, three_ref, send_ref):
-    rows = [ref[...].astype(F32) for ref in (own_ref, one_ref, two_ref, three_ref)]
+def deal_columns_body(*refs):
+    out_ref, live_ref, rows_ref, fields_ref, send_ref, maps_ref, mine_ref = refs[4:]
+    cases, cap = out_ref.shape[0], rows_ref.shape[1] // BLOCKS
+    for b in range(BLOCKS):
+        picked = at_slots(fields_ref[cases:], rows_ref[TABLE : TABLE + 1], b)
+        maps_ref[:, b * cap : (b + 1) * cap] = picked.astype(BF16)
+    shared = (live_ref[0:1] * out_ref[...].astype(F32)).astype(BF16)
+    mine_ref[...] = dot_nt(fields_ref[cases : cases + 24], shared)
+    rows = [ref[...].astype(F32) for ref in refs[:4]]
     depth, lanes = rows[0].shape
     group = lax.broadcasted_iota(jnp.int32, (depth, lanes), 1) // 32 % 4
     for t in range(4):
@@ -375,32 +371,41 @@
     away = (lax.axis_index("grp") - corner // 8 % 4) % groups
     corner = ((corner // 32 * 4 + away) * 8 + corner % 8).astype(F32)
     corner = jnp.pad(corner, ((0, 0), (0, LANES - corner.shape[1])))
-    (dealt,) = call(deal_columns_body, [((subs, depth, LANES), BF16)], 2, *coarse_rows)
-    direction, corner_in = call(
+    spare = fields.shape[0] - cases
+    dealt, maps, mine = call(
+        deal_columns_body,
+        [((subs, depth, LANES), BF16), ((spare, total), BF16), ((24, cases), F32)],
+        2,
+        *coarse_rows,
+        dir_out,
+        live,
+        rows,
+        fields,
+    )
+    (corner_in,) = call(
         schur_first_body,
-        [(field, F32), ((subs, depth, 2 * LANES), BF16)],
-        16,
+        [((subs, depth, 2 * LANES), BF16)],
+        4,
+        *seconds,
+        maps,
+        mine,
+        corner,
+        dealt,
+    )
+    corner_in = lax.all_to_all(corner_in, "sub", 0, 0, tiled=True)
+    direction, local, sent, scalars = call(
+        schur_second_body,
+        [(field, F32), (field, F32), (field, F32), ((8, LANES), F32)],
+        8,
         *seconds,
         dir_out,
         live,
         columns,
-        fields,
-        corner,
-        dealt,
-    )
-    corner_in = lax.all_to_all(corner_in, "sub", 0, 0, tiled=True)
-    spare = fields.shape[0] - cases
-    local, sent, maps, scalars = call(
-        schur_second_body,
-        [(field, F32), (field, F32), ((spare, total), BF16), ((8, LANES), F32)],
-        8,
-        direction,
         rho,
         rows,
-        fields,
         schur_factor,
         scratch=factor_scratch,
-        in_hbm=(4,),
+        in_hbm=(BLOCKS + 5,),
         vmem=50,
     )
     picked, parts = call(

time: 98.9 us -> 97.9 us (0.990)
  transfers between devices with their start and end apart: 25 -> 25, of which waited for: 9 -> 8; matrix products, arithmetic and copies ran while one was open for 0% -> 0% of each run, Pallas kernels for 11% -> 12%
where the time goes in v4:
time: 97.9 us; the launch traced here: 97.5 us
  starting transfers between devices  40.3 us (41%)
  waiting for transfers between devices  20.3 us (21%)
  Pallas kernels  16.9 us (17%)
  blocking collectives  16.8 us (17%)
  other arithmetic  2.41 us (2%)
    ppermute x18, starting transfers between devices, exchange(): received[(b + 3) % BLOCKS] = lax.ppermute(blocks[b], 'sub', route)  28.2 us
    pallas_call x9, Pallas kernels, call(): pl.pallas_call(body, out_shape=[jax.ShapeDtypeStruct(shape, dtype) for sh...  16.9 us
    all_to_all x1, blocking collectives, on_device(): coarse = lax.all_to_all(coarse, 'sub', 0, 0, tiled=True)  16.8 us
    ppermute x18, waiting for transfers between devices, exchange(): received[(b + 3) % BLOCKS] = lax.ppermute(blocks[b], 'sub', route)  8.34 us
    all_to_all x1, waiting for transfers between devices, on_device(): corner_in = lax.all_to_all(corner_in, 'sub', 0, 0, tiled=True)  8.24 us
    ppermute x6, starting transfers between devices, to_groups(): lax.ppermute(block, 'grp', [(i, (i + k) % count) for i in range(count)])  7.02 us
    all_to_all x1, starting transfers between devices, on_device(): corner_in = lax.all_to_all(corner_in, 'sub', 0, 0, tiled=True)  5.1 us
    ppermute x6, waiting for transfers between devices, to_groups(): lax.ppermute(block, 'grp', [(i, (i + k) % count) for i in range(count)])  3.69 us
  transfers between devices with their start and end apart: 25, of which 8 were waited for; matrix products, arithmetic and copies ran while one was open for 0% of the time, Pallas kernels for 12%

profile of v4, /device:TPU:1, one launch (start us, length us, event | category | flops | bytes accessed | tf_op | source)
XLA Modules:
  0.0 97.5 jit_solution(5661080151958790108)
XLA Ops:
  4.0 9.6 %collective-permute-start = (bf16[32,256]{1,0:T(8,128)(2,1)S(1)}, bf16[32,256]{1,0:T(8,128)(2,1)S(1)}, u32[]{:S(2)}, u32[]{:S(2)}) collective-permute-start(bf16[32,256]{1,0:T(8,128)(2,1)S(1)} %get-tuple-element.46), channel_id=1, source_target_pairs={{0,236},{4,240},{8,244},{12,248},{16,252},{20,0},{24,4},{28,8},{32... | collective-permute-start | bytes 49160 | tf_op jit(solution)/shard_map/ppermute | solution.py:310
  14.4 2.0 %collective-permute-start.3 = (bf16[32,256]{1,0:T(8,128)(2,1)S(1)}, bf16[32,256]{1,0:T(8,128)(2,1)S(1)}, u32[]{:S(2)}, u32[]{:S(2)}) collective-permute-start(bf16[32,256]{1,0:T(8,128)(2,1)S(1)} %get-tuple-element.49), channel_id=1, source_target_pairs={{0,20},{4,24},{8,28},{12,32},{16,36},{20,40},{24,44},{28,48},{32,5... | collective-permute-start | bytes 49160 | tf_op jit(solution)/shard_map/ppermute | solution.py:310
  17.1 2.7 %collective-permute-start.13 = (bf16[8,2048]{1,0:T(8,128)(2,1)}, bf16[8,2048]{1,0:T(8,128)(2,1)S(1)}, u32[]{:S(2)}, u32[]{:S(2)}) collective-permute-start(bf16[8,2048]{1,0:T(8,128)(2,1)} %refs_0_), channel_id=1, source_target_pairs={{0,2},{1,3},{2,0},{3,1},{4,6},{5,7},{6,4},{7,5},{8,10},{9,11},{10,... | collective-permute-start | bytes 98312 | tf_op jit(solution)/shard_map/ppermute | solution.py:317
  20.2 1.2 %collective-permute-done.3.refs_3_ = bf16[32,256]{1,0:T(8,128)(2,1)S(1)} collective-permute-done((bf16[32,256]{1,0:T(8,128)(2,1)S(1)}, bf16[32,256]{1,0:T(8,128)(2,1)S(1)}, u32[]{:S(2)}, u32[]{:S(2)}) %collective-permute-start.3) | collective-permute-done | bytes 16416 | tf_op jit(solution)/shard_map/ppermute | solution.py:310
  21.3 2.5 %collective-permute-start.14 = (bf16[8,2048]{1,0:T(8,128)(2,1)}, bf16[8,2048]{1,0:T(8,128)(2,1)S(1)}, u32[]{:S(2)}, u32[]{:S(2)}) collective-permute-start(bf16[8,2048]{1,0:T(8,128)(2,1)} %refs_0_), channel_id=1, source_target_pairs={{0,3},{1,0},{2,1},{3,2},{4,7},{5,4},{6,5},{7,6},{8,11},{9,8},{10,9... | collective-permute-start | bytes 98312 | tf_op jit(solution)/shard_map/ppermute | solution.py:317
  23.8 5.3 %shard_map.105 = (f32[32,1536]{1,0:T(8,128)S(1)}, bf16[32,1536]{1,0:T(8,128)(2,1)S(1)}, f32[8,1536]{1,0:T(8,128)S(1)}, f32[8,32]{1,0:T(8,128)S(1)}, bf16[32,256]...) custom-call(bf16[32,256]{1,0:T(8,128)(2,1)S(1)} %collective-permute-, ...), custom_call_target="tpu_custom_call" | custom-call | flops 16777216 | bytes 16777216 | tf_op jit(solution)/shard_map/pallas_call | solution.py:63
  29.2 4.0 %collective-permute-start.6 = (bf16[32,256]{1,0:T(8,128)(2,1)S(1)}, bf16[32,256]{1,0:T(8,128)(2,1)S(1)}, u32[]{:S(2)}, u32[]{:S(2)}) collective-permute-start(bf16[32,256]{1,0:T(8,128)(2,1)S(1)} %get-tuple-element.53), channel_id=1, source_target_pairs={{0,236},{4,240},{8,244},{12,248},{16,252},{20,0},{24,4},{28,8},{32... | collective-permute-start | bytes 49160 | tf_op jit(solution)/shard_map/ppermute | solution.py:310
  33.1 1.1 %collective-permute-start.7 = (bf16[32,256]{1,0:T(8,128)(2,1)S(1)}, bf16[32,256]{1,0:T(8,128)(2,1)S(1)}, u32[]{:S(2)}, u32[]{:S(2)}) collective-permute-start(bf16[32,256]{1,0:T(8,128)(2,1)S(1)} %get-tuple-element.54), channel_id=1, source_target_pairs={{0,248},{4,252},{8,0},{12,4},{16,8},{20,12},{24,16},{28,20},{32,24... | collective-permute-start | bytes 49160 | tf_op jit(solution)/shard_map/ppermute | solution.py:310
  34.2 2.0 %collective-permute-start.9 = (bf16[32,256]{1,0:T(8,128)(2,1)S(1)}, bf16[32,256]{1,0:T(8,128)(2,1)S(1)}, u32[]{:S(2)}, u32[]{:S(2)}) collective-permute-start(bf16[32,256]{1,0:T(8,128)(2,1)S(1)} %get-tuple-element.56), channel_id=1, source_target_pairs={{0,20},{4,24},{8,28},{12,32},{16,36},{20,40},{24,44},{28,48},{32,5... | collective-permute-start | bytes 49160 | tf_op jit(solution)/shard_map/ppermute | solution.py:310
  36.8 1.0 %shard_map.107 = (bf16[64,8,128]{2,1,0:T(8,128)(2,1)S(1)}, bf16[32,1536]{1,0:T(8,128)(2,1)S(1)}, f32[24,32]{1,0:T(8,128)S(1)}) custom-call(bf16[8,2048]{1,0:T(8,128)(2,1)S(1)} %copy-done, bf16[8,2048]{1,0:T(8,128)(2,1)S(1)} %collective-permute-done.12.refs_1_, bf16[8,2048]{1,0:T(8,128)(2,1)S(1)} %collective-permute-done.13.refs_2_, ...), custom_call_target="tpu_custom_call" | custom-call | flops 2097152 | bytes 2097152 | tf_op jit(solution)/shard_map/pallas_call | solution.py:63
  37.8 3.4 %collective-permute-done.9.refs_3_ = bf16[32,256]{1,0:T(8,128)(2,1)S(1)} collective-permute-done((bf16[32,256]{1,0:T(8,128)(2,1)S(1)}, bf16[32,256]{1,0:T(8,128)(2,1)S(1)}, u32[]{:S(2)}, u32[]{:S(2)}) %collective-permute-start.9) | collective-permute-done | bytes 16416 | tf_op jit(solution)/shard_map/ppermute | solution.py:310
  43.0 5.1 %all-to-all-start = ((bf16[64,8,256]{2,1,0:T(8,128)(2,1)}), bf16[64,8,256]{2,1,0:T(8,128)(2,1)S(1)}, u32[]{:S(2)}, u32[]{:S(2)}) async-start(bf16[64,8,256]{2,1,0:T(8,128)(2,1)} %shard_map.108), calls=%async_computation | async-start | bytes 524288 | tf_op jit(solution)/shard_map/all_to_all | solution.py:395
  48.1 5.0 %shard_map.106 = (f32[32,1536]{1,0:T(8,128)S(1)}, f32[32,1536]{1,0:T(8,128)S(1)}, f32[32,1536]{1,0:T(8,128)S(1)}, f32[8,128]{1,0:T(8,128)S(1)}) custom-call(bf16[32,256]{1,0:T(8,128)(2,1)S(1)} %collective-permute-done.6.refs_0_, bf16[32,256]{1,0:T(8,128)(2,1)S(1)} %collective-permute-done.7.refs_1_, bf16[32,256]{1,0:T(8,128)(2,1)S(1)} %collective-permute-done.8.refs_2_, ...), custom_call_target="tpu_custom_call" | custom-call | flops 8388608 | bytes 8388608 | tf_op jit(solution)/shard_map/pallas_call | solution.py:63
  53.2 8.2 %all-to-all-done.sent_ref = bf16[64,8,256]{2,1,0:T(8,128)(2,1)S(1)} async-done(((bf16[64,8,256]{2,1,0:T(8,128)(2,1)}), bf16[64,8,256]{2,1,0:T(8,128)(2,1)S(1)}, u32[]{:S(2)}, u32[]{:S(2)}) %all-to-all-start) | async-done | bytes 262176 | tf_op jit(solution)/shard_map/all_to_all | solution.py:395
  61.4 1.3 %shard_map.109 = (bf16[512,128]{1,0:T(8,128)(2,1)S(1)}, f32[16,128]{1,0:T(8,128)S(1)}) custom-call(bf16[64,8,256]{2,1,0:T(8,128)(2,1)S(1)} %all-to-all-done.sent_ref, f32[8,128]{1,0:T(8,128)S(1)} %get-tuple-element.72.scalars_ref), custom_call_target="tpu_custom_call" | custom-call | flops 4194304 | bytes 4194304 | tf_op jit(solution)/shard_map/pallas_call | solution.py:63
  64.2 1.0 %collective-permute-done.17.three_ref = f32[16,128]{1,0:T(8,128)S(1)} collective-permute-done((f32[16,128]{1,0:T(8,128)S(1)}, f32[16,128]{1,0:T(8,128)S(1)}, u32[]{:S(2)}, u32[]{:S(2)}) %collective-permute-start.17) | collective-permute-done | bytes 8224 | tf_op jit(solution)/shard_map/ppermute | solution.py:317
  65.3 1.6 %collective-permute-done.16.two_ref = f32[16,128]{1,0:T(8,128)S(1)} collective-permute-done((f32[16,128]{1,0:T(8,128)S(1)}, f32[16,128]{1,0:T(8,128)S(1)}, u32[]{:S(2)}, u32[]{:S(2)}) %collective-permute-start.16) | collective-permute-done | bytes 8224 | tf_op jit(solution)/shard_map/ppermute | solution.py:317
  66.9 1.0 %collective-permute-done.15.one_ref = f32[16,128]{1,0:T(8,128)S(1)} collective-permute-done((f32[16,128]{1,0:T(8,128)S(1)}, f32[16,128]{1,0:T(8,128)S(1)}, u32[]{:S(2)}, u32[]{:S(2)}) %collective-permute-start.15) | collective-permute-done | bytes 8224 | tf_op jit(solution)/shard_map/ppermute | solution.py:317
  68.2 16.8 %all_to_all.10.coarse_ref = bf16[64,8,128]{2,1,0:T(8,128)(2,1)S(1)} all-to-all(bf16[64,8,128]{2,1,0:T(8,128)(2,1)S(1)} %shard_map.110), channel_id=1, replica_groups=mesh['sub'=64,'grp'=4] {'sub'}, dimensions={0} | all-to-all | bytes 262144 | tf_op jit(solution)/shard_map/all_to_all | solution.py:427
  86.3 1.9 %collective-permute-start.19 = (bf16[32,256]{1,0:T(8,128)(2,1)S(1)}, bf16[32,256]{1,0:T(8,128)(2,1)S(1)}, u32[]{:S(2)}, u32[]{:S(2)}) collective-permute-start(bf16[32,256]{1,0:T(8,128)(2,1)S(1)} %get-tuple-element.79), channel_id=1, source_target_pairs={{0,248},{4,252},{8,0},{12,4},{16,8},{20,12},{24,16},{28,20},{32,24... | collective-permute-start | bytes 49160 | tf_op jit(solution)/shard_map/ppermute | solution.py:310
  89.8 1.9 %collective-permute-start.22 = (bf16[32,256]{1,0:T(8,128)(2,1)S(1)}, bf16[32,256]{1,0:T(8,128)(2,1)S(1)}, u32[]{:S(2)}, u32[]{:S(2)}) collective-permute-start(bf16[32,256]{1,0:T(8,128)(2,1)S(1)} %get-tuple-element.82), channel_id=1, source_target_pairs={{0,8},{4,12},{8,16},{12,20},{16,24},{20,28},{24,32},{28,36},{32,40... | collective-permute-start | bytes 49160 | tf_op jit(solution)/shard_map/ppermute | solution.py:310
  91.7 1.3 %collective-permute-start.23 = (bf16[32,256]{1,0:T(8,128)(2,1)S(1)}, bf16[32,256]{1,0:T(8,128)(2,1)S(1)}, u32[]{:S(2)}, u32[]{:S(2)}) collective-permute-start(bf16[32,256]{1,0:T(8,128)(2,1)S(1)} %get-tuple-element.83), channel_id=1, source_target_pairs={{0,4},{4,8},{8,12},{12,16},{16,20},{20,24},{24,28},{28,32},{32,36}... | collective-permute-start | bytes 49160 | tf_op jit(solution)/shard_map/ppermute | solution.py:310
  93.0 2.9 %collective-permute-done.21.refs_3_ = bf16[32,256]{1,0:T(8,128)(2,1)S(1)} collective-permute-done((bf16[32,256]{1,0:T(8,128)(2,1)S(1)}, bf16[32,256]{1,0:T(8,128)(2,1)S(1)}, u32[]{:S(2)}, u32[]{:S(2)}) %collective-permute-start.21) | collective-permute-done | bytes 16416 | tf_op jit(solution)/shard_map/ppermute | solution.py:310
  95.8 1.7 %shard_map.112 = (f32[32,1536]{1,0:T(8,128)}, f32[32,1536]{1,0:T(8,128)}) custom-call(bf16[32,256]{1,0:T(8,128)(2,1)S(1)} %collective-permute-done.18.refs_0_, bf16[32,256]{1,0:T(8,128)(2,1)S(1)} %collective-permute-done.19.refs_1_, bf16[32,256]{1,0:T(8,128)(2,1)S(1)} %collective-permute-done.20.refs_2_, ...), custom_call_target="tpu_custom_call" | custom-call | flops 8388608 | bytes 8388608 | tf_op jit(solution)/shard_map/pallas_call | solution.py:63
  (45 shorter events, 12.2 us)
Async XLA Ops:
  4.0 12.4 %collective-permute-start = (bf16[32,256]{1,0:T(8,128)(2,1)S(1)}, bf16[32,256]{1,0:T(8,128)(2,1)S(1)}, u32[]{:S(2)}, u32[]{:S(2)}) collective-permute-start(bf16[32,256]{1,0:T(8,128)(2,1)S(1)} %get-tuple-element.46), channel_id=1, source_target_pairs={{0,236},{4,240},{8,244},{12,248},{16,252},{20,0},{24,4},{28,8},{32... | collective-permute-start | bytes 49160 | tf_op jit(solution)/shard_map/ppermute | solution.py:310
  13.6 3.5 %collective-permute-start.1 = (bf16[32,256]{1,0:T(8,128)(2,1)S(1)}, bf16[32,256]{1,0:T(8,128)(2,1)S(1)}, u32[]{:S(2)}, u32[]{:S(2)}) collective-permute-start(bf16[32,256]{1,0:T(8,128)(2,1)S(1)} %get-tuple-element.47), channel_id=1, source_target_pairs={{0,248},{4,252},{8,0},{12,4},{16,8},{20,12},{24,16},{28,20},{32,24... | collective-permute-start | bytes 49160 | tf_op jit(solution)/shard_map/ppermute | solution.py:310
  14.4 5.5 %collective-permute-start.2 = (bf16[32,256]{1,0:T(8,128)(2,1)S(1)}, bf16[32,256]{1,0:T(8,128)(2,1)S(1)}, u32[]{:S(2)}, u32[]{:S(2)}) collective-permute-start(bf16[32,256]{1,0:T(8,128)(2,1)S(1)} %get-tuple-element.48), channel_id=1, source_target_pairs={{0,252},{4,0},{8,4},{12,8},{16,12},{20,16},{24,20},{28,24},{32,28}... | collective-permute-start | bytes 49160 | tf_op jit(solution)/shard_map/ppermute | solution.py:310
  14.4 6.9 %collective-permute-start.3 = (bf16[32,256]{1,0:T(8,128)(2,1)S(1)}, bf16[32,256]{1,0:T(8,128)(2,1)S(1)}, u32[]{:S(2)}, u32[]{:S(2)}) collective-permute-start(bf16[32,256]{1,0:T(8,128)(2,1)S(1)} %get-tuple-element.49), channel_id=1, source_target_pairs={{0,20},{4,24},{8,28},{12,32},{16,36},{20,40},{24,44},{28,48},{32,5... | collective-permute-start | bytes 49160 | tf_op jit(solution)/shard_map/ppermute | solution.py:310
  16.3 7.5 %collective-permute-start.4 = (bf16[32,256]{1,0:T(8,128)(2,1)S(1)}, bf16[32,256]{1,0:T(8,128)(2,1)S(1)}, u32[]{:S(2)}, u32[]{:S(2)}) collective-permute-start(bf16[32,256]{1,0:T(8,128)(2,1)S(1)} %get-tuple-element.50), channel_id=1, source_target_pairs={{0,8},{4,12},{8,16},{12,20},{16,24},{20,28},{24,32},{28,36},{32,40... | collective-permute-start | bytes 49160 | tf_op jit(solution)/shard_map/ppermute | solution.py:310
  16.3 7.4 %collective-permute-start.5 = (bf16[32,256]{1,0:T(8,128)(2,1)S(1)}, bf16[32,256]{1,0:T(8,128)(2,1)S(1)}, u32[]{:S(2)}, u32[]{:S(2)}) collective-permute-start(bf16[32,256]{1,0:T(8,128)(2,1)S(1)} %get-tuple-element.51), channel_id=1, source_target_pairs={{0,4},{4,8},{8,12},{12,16},{16,20},{20,24},{24,28},{28,32},{32,36}... | collective-permute-start | bytes 49160 | tf_op jit(solution)/shard_map/ppermute | solution.py:310
  17.1 17.1 %collective-permute-start.13 = (bf16[8,2048]{1,0:T(8,128)(2,1)}, bf16[8,2048]{1,0:T(8,128)(2,1)S(1)}, u32[]{:S(2)}, u32[]{:S(2)}) collective-permute-start(bf16[8,2048]{1,0:T(8,128)(2,1)} %refs_0_), channel_id=1, source_target_pairs={{0,2},{1,3},{2,0},{3,1},{4,6},{5,7},{6,4},{7,5},{8,10},{9,11},{10,... | collective-permute-start | bytes 98312 | tf_op jit(solution)/shard_map/ppermute | solution.py:317
  19.8 14.4 %collective-permute-start.12 = (bf16[8,2048]{1,0:T(8,128)(2,1)}, bf16[8,2048]{1,0:T(8,128)(2,1)S(1)}, u32[]{:S(2)}, u32[]{:S(2)}) collective-permute-start(bf16[8,2048]{1,0:T(8,128)(2,1)} %refs_0_), channel_id=1, source_target_pairs={{0,1},{1,2},{2,3},{3,0},{4,5},{5,6},{6,7},{7,4},{8,9},{9,10},{10,1... | collective-permute-start | bytes 98312 | tf_op jit(solution)/shard_map/ppermute | solution.py:317
  21.3 14.9 %collective-permute-start.14 = (bf16[8,2048]{1,0:T(8,128)(2,1)}, bf16[8,2048]{1,0:T(8,128)(2,1)S(1)}, u32[]{:S(2)}, u32[]{:S(2)}) collective-permute-start(bf16[8,2048]{1,0:T(8,128)(2,1)} %refs_0_), channel_id=1, source_target_pairs={{0,3},{1,0},{2,1},{3,2},{4,7},{5,4},{6,5},{7,6},{8,11},{9,8},{10,9... | collective-permute-start | bytes 98312 | tf_op jit(solution)/shard_map/ppermute | solution.py:317
  29.2 7.0 %collective-permute-start.6 = (bf16[32,256]{1,0:T(8,128)(2,1)S(1)}, bf16[32,256]{1,0:T(8,128)(2,1)S(1)}, u32[]{:S(2)}, u32[]{:S(2)}) collective-permute-start(bf16[32,256]{1,0:T(8,128)(2,1)S(1)} %get-tuple-element.53), channel_id=1, source_target_pairs={{0,236},{4,240},{8,244},{12,248},{16,252},{20,0},{24,4},{28,8},{32... | collective-permute-start | bytes 49160 | tf_op jit(solution)/shard_map/ppermute | solution.py:310
  33.1 4.7 %collective-permute-start.7 = (bf16[32,256]{1,0:T(8,128)(2,1)S(1)}, bf16[32,256]{1,0:T(8,128)(2,1)S(1)}, u32[]{:S(2)}, u32[]{:S(2)}) collective-permute-start(bf16[32,256]{1,0:T(8,128)(2,1)S(1)} %get-tuple-element.54), channel_id=1, source_target_pairs={{0,248},{4,252},{8,0},{12,4},{16,8},{20,12},{24,16},{28,20},{32,24... | collective-permute-start | bytes 49160 | tf_op jit(solution)/shard_map/ppermute | solution.py:310
  34.2 3.6 %collective-permute-start.8 = (bf16[32,256]{1,0:T(8,128)(2,1)S(1)}, bf16[32,256]{1,0:T(8,128)(2,1)S(1)}, u32[]{:S(2)}, u32[]{:S(2)}) collective-permute-start(bf16[32,256]{1,0:T(8,128)(2,1)S(1)} %get-tuple-element.55), channel_id=1, source_target_pairs={{0,252},{4,0},{8,4},{12,8},{16,12},{20,16},{24,20},{28,24},{32,28}... | collective-permute-start | bytes 49160 | tf_op jit(solution)/shard_map/ppermute | solution.py:310
  34.2 6.9 %collective-permute-start.9 = (bf16[32,256]{1,0:T(8,128)(2,1)S(1)}, bf16[32,256]{1,0:T(8,128)(2,1)S(1)}, u32[]{:S(2)}, u32[]{:S(2)}) collective-permute-start(bf16[32,256]{1,0:T(8,128)(2,1)S(1)} %get-tuple-element.56), channel_id=1, source_target_pairs={{0,20},{4,24},{8,28},{12,32},{16,36},{20,40},{24,44},{28,48},{32,5... | collective-permute-start | bytes 49160 | tf_op jit(solution)/shard_map/ppermute | solution.py:310
  36.2 5.9 %collective-permute-start.10 = (bf16[32,256]{1,0:T(8,128)(2,1)S(1)}, bf16[32,256]{1,0:T(8,128)(2,1)S(1)}, u32[]{:S(2)}, u32[]{:S(2)}) collective-permute-start(bf16[32,256]{1,0:T(8,128)(2,1)S(1)} %get-tuple-element.57), channel_id=1, source_target_pairs={{0,8},{4,12},{8,16},{12,20},{16,24},{20,28},{24,32},{28,36},{32,40... | collective-permute-start | bytes 49160 | tf_op jit(solution)/shard_map/ppermute | solution.py:310
  36.2 5.9 %collective-permute-start.11 = (bf16[32,256]{1,0:T(8,128)(2,1)S(1)}, bf16[32,256]{1,0:T(8,128)(2,1)S(1)}, u32[]{:S(2)}, u32[]{:S(2)}) collective-permute-start(bf16[32,256]{1,0:T(8,128)(2,1)S(1)} %get-tuple-element.58), channel_id=1, source_target_pairs={{0,4},{4,8},{8,12},{12,16},{16,20},{20,24},{24,28},{28,32},{32,36}... | collective-permute-start | bytes 49160 | tf_op jit(solution)/shard_map/ppermute | solution.py:310
  43.0 18.4 %all-to-all-start = ((bf16[64,8,256]{2,1,0:T(8,128)(2,1)}), bf16[64,8,256]{2,1,0:T(8,128)(2,1)S(1)}, u32[]{:S(2)}, u32[]{:S(2)}) async-start(bf16[64,8,256]{2,1,0:T(8,128)(2,1)} %shard_map.108), calls=%async_computation | async-start | bytes 524288 | tf_op jit(solution)/shard_map/all_to_all | solution.py:395
  62.8 4.1 %collective-permute-start.16 = (f32[16,128]{1,0:T(8,128)S(1)}, f32[16,128]{1,0:T(8,128)S(1)}, u32[]{:S(2)}, u32[]{:S(2)}) collective-permute-start(f32[16,128]{1,0:T(8,128)S(1)} %get-tuple-element.74.own_ref), channel_id=1, source_target_pairs={{0,2},{1,3},{2,0},{3,1},{4,6},{5,7},{6,4},{7,5},{8,10},{9,11},{10,... | collective-permute-start | bytes 24584 | tf_op jit(solution)/shard_map/ppermute | solution.py:317
  63.7 4.3 %collective-permute-start.15 = (f32[16,128]{1,0:T(8,128)S(1)}, f32[16,128]{1,0:T(8,128)S(1)}, u32[]{:S(2)}, u32[]{:S(2)}) collective-permute-start(f32[16,128]{1,0:T(8,128)S(1)} %get-tuple-element.74.own_ref), channel_id=1, source_target_pairs={{0,1},{1,2},{2,3},{3,0},{4,5},{5,6},{6,7},{7,4},{8,9},{9,10},{10,1... | collective-permute-start | bytes 24584 | tf_op jit(solution)/shard_map/ppermute | solution.py:317
  85.4 6.3 %collective-permute-start.18 = (bf16[32,256]{1,0:T(8,128)(2,1)S(1)}, bf16[32,256]{1,0:T(8,128)(2,1)S(1)}, u32[]{:S(2)}, u32[]{:S(2)}) collective-permute-start(bf16[32,256]{1,0:T(8,128)(2,1)S(1)} %get-tuple-element.78), channel_id=1, source_target_pairs={{0,236},{4,240},{8,244},{12,248},{16,252},{20,0},{24,4},{28,8},{32... | collective-permute-start | bytes 49160 | tf_op jit(solution)/shard_map/ppermute | solution.py:310
  86.3 6.7 %collective-permute-start.19 = (bf16[32,256]{1,0:T(8,128)(2,1)S(1)}, bf16[32,256]{1,0:T(8,128)(2,1)S(1)}, u32[]{:S(2)}, u32[]{:S(2)}) collective-permute-start(bf16[32,256]{1,0:T(8,128)(2,1)S(1)} %get-tuple-element.79), channel_id=1, source_target_pairs={{0,248},{4,252},{8,0},{12,4},{16,8},{20,12},{24,16},{28,20},{32,24... | collective-permute-start | bytes 49160 | tf_op jit(solution)/shard_map/ppermute | solution.py:310
  88.3 4.7 %collective-permute-start.20 = (bf16[32,256]{1,0:T(8,128)(2,1)S(1)}, bf16[32,256]{1,0:T(8,128)(2,1)S(1)}, u32[]{:S(2)}, u32[]{:S(2)}) collective-permute-start(bf16[32,256]{1,0:T(8,128)(2,1)S(1)} %get-tuple-element.80), channel_id=1, source_target_pairs={{0,252},{4,0},{8,4},{12,8},{16,12},{20,16},{24,20},{28,24},{32,28}... | collective-permute-start | bytes 49160 | tf_op jit(solution)/shard_map/ppermute | solution.py:310
  89.0 6.8 %collective-permute-start.21 = (bf16[32,256]{1,0:T(8,128)(2,1)S(1)}, bf16[32,256]{1,0:T(8,128)(2,1)S(1)}, u32[]{:S(2)}, u32[]{:S(2)}) collective-permute-start(bf16[32,256]{1,0:T(8,128)(2,1)S(1)} %get-tuple-element.81), channel_id=1, source_target_pairs={{0,20},{4,24},{8,28},{12,32},{16,36},{20,40},{24,44},{28,48},{32,5... | collective-permute-start | bytes 49160 | tf_op jit(solution)/shard_map/ppermute | solution.py:310
  89.8 6.1 %collective-permute-start.22 = (bf16[32,256]{1,0:T(8,128)(2,1)S(1)}, bf16[32,256]{1,0:T(8,128)(2,1)S(1)}, u32[]{:S(2)}, u32[]{:S(2)}) collective-permute-start(bf16[32,256]{1,0:T(8,128)(2,1)S(1)} %get-tuple-element.82), channel_id=1, source_target_pairs={{0,8},{4,12},{8,16},{12,20},{16,24},{20,28},{24,32},{28,36},{32,40... | collective-permute-start | bytes 49160 | tf_op jit(solution)/shard_map/ppermute | solution.py:310
  91.7 4.1 %collective-permute-start.23 = (bf16[32,256]{1,0:T(8,128)(2,1)S(1)}, bf16[32,256]{1,0:T(8,128)(2,1)S(1)}, u32[]{:S(2)}, u32[]{:S(2)}) collective-permute-start(bf16[32,256]{1,0:T(8,128)(2,1)S(1)} %get-tuple-element.83), channel_id=1, source_target_pairs={{0,4},{4,8},{8,12},{12,16},{16,20},{20,24},{24,28},{28,32},{32,36}... | collective-permute-start | bytes 49160 | tf_op jit(solution)/shard_map/ppermute | solution.py:310
  (3 other events, 74.7 us)

commit v5 on v4

--- a/solution.py
+++ b/solution.py
@@ -160,7 +160,10 @@
     for ref, b in zip(refs[:BLOCKS], RECEIVE_ORDER):
         corner_in = corner_in - dot_nt(maps_ref[:24, b * cap : (b + 1) * cap], ref[...])
     corner_in = 0.5 * corner_in
-    groups = [corner_in[0:8], corner_in[8:16], corner_in[16:24], index_lanes(index_ref[...])]
+    corner = index_ref[...]
+    away = (lax.axis_index("grp") + 4 - ((corner >> 3) & 3)) & 3
+    corner = ((((corner >> 5) * 4 + away) * 8) + (corner & 7)).astype(F32)
+    groups = [corner_in[0:8], corner_in[8:16], corner_in[16:24], index_lanes(corner)]
     tile = jnp.concatenate(groups, axis=1).astype(BF16)
     count, depth, _ = send_ref.shape
     send_ref[:, :, :LANES] = jnp.broadcast_to(tile[None], (count, depth, LANES))
@@ -367,10 +370,7 @@
         vmem=50,
     )
     seconds = exchange(blocks)
-    *coarse_rows, corner, rho = lax.optimization_barrier((*coarse_rows, corner_row[0], rho))
-    away = (lax.axis_index("grp") - corner // 8 % 4) % groups
-    corner = ((corner // 32 * 4 + away) * 8 + corner % 8).astype(F32)
-    corner = jnp.pad(corner, ((0, 0), (0, LANES - corner.shape[1])))
+    *coarse_rows, rho = lax.optimization_barrier((*coarse_rows, rho))
     spare = fields.shape[0] - cases
     dealt, maps, mine = call(
         deal_columns_body,
@@ -389,7 +389,7 @@
         *seconds,
         maps,
         mine,
-        corner,
+        corner_row[0],
         dealt,
     )
     corner_in = lax.all_to_all(corner_in, "sub", 0, 0, tiled=True)

time: 97.9 us -> 97.9 us (level)
  no operation moved by 1% of the time
where the time goes in v5:
time: 97.9 us; the launch traced here: 97.5 us
  starting transfers between devices  40.3 us (41%)
  waiting for transfers between devices  20.3 us (21%)
  Pallas kernels  16.9 us (17%)
  blocking collectives  16.8 us (17%)
  other arithmetic  2.38 us (2%)
    ppermute x18, starting transfers between devices, exchange(): received[(b + 3) % BLOCKS] = lax.ppermute(blocks[b], 'sub', route)  28.2 us
    pallas_call x9, Pallas kernels, call(): pl.pallas_call(body, out_shape=[jax.ShapeDtypeStruct(shape, dtype) for sh...  16.9 us
    all_to_all x1, blocking collectives, on_device(): coarse = lax.all_to_all(coarse, 'sub', 0, 0, tiled=True)  16.8 us
    ppermute x18, waiting for transfers between devices, exchange(): received[(b + 3) % BLOCKS] = lax.ppermute(blocks[b], 'sub', route)  8.4 us
    all_to_all x1, waiting for transfers between devices, on_device(): corner_in = lax.all_to_all(corner_in, 'sub', 0, 0, tiled=True)  8.24 us
    ppermute x6, starting transfers between devices, to_groups(): lax.ppermute(block, 'grp', [(i, (i + k) % count) for i in range(count)])  7.02 us
    all_to_all x1, starting transfers between devices, on_device(): corner_in = lax.all_to_all(corner_in, 'sub', 0, 0, tiled=True)  5.1 us
    ppermute x6, waiting for transfers between devices, to_groups(): lax.ppermute(block, 'grp', [(i, (i + k) % count) for i in range(count)])  3.69 us
  transfers between devices with their start and end apart: 25, of which 8 were waited for; matrix products, arithmetic and copies ran while one was open for 0% of the time, Pallas kernels for 12%

profile of v5, /device:TPU:1, one launch (start us, length us, event | category | flops | bytes accessed | tf_op | source)
XLA Modules:
  0.0 97.5 jit_solution(18303632299742482147)
XLA Ops:
  4.0 9.6 %collective-permute-start = (bf16[32,256]{1,0:T(8,128)(2,1)S(1)}, bf16[32,256]{1,0:T(8,128)(2,1)S(1)}, u32[]{:S(2)}, u32[]{:S(2)}) collective-permute-start(bf16[32,256]{1,0:T(8,128)(2,1)S(1)} %get-tuple-element.45), channel_id=1, source_target_pairs={{0,236},{4,240},{8,244},{12,248},{16,252},{20,0},{24,4},{28,8},{32... | collective-permute-start | bytes 49160 | tf_op jit(solution)/shard_map/ppermute | solution.py:313
  14.4 2.0 %collective-permute-start.3 = (bf16[32,256]{1,0:T(8,128)(2,1)S(1)}, bf16[32,256]{1,0:T(8,128)(2,1)S(1)}, u32[]{:S(2)}, u32[]{:S(2)}) collective-permute-start(bf16[32,256]{1,0:T(8,128)(2,1)S(1)} %get-tuple-element.48), channel_id=1, source_target_pairs={{0,20},{4,24},{8,28},{12,32},{16,36},{20,40},{24,44},{28,48},{32,5... | collective-permute-start | bytes 49160 | tf_op jit(solution)/shard_map/ppermute | solution.py:313
  17.1 2.7 %collective-permute-start.13 = (bf16[8,2048]{1,0:T(8,128)(2,1)}, bf16[8,2048]{1,0:T(8,128)(2,1)S(1)}, u32[]{:S(2)}, u32[]{:S(2)}) collective-permute-start(bf16[8,2048]{1,0:T(8,128)(2,1)} %refs_0_), channel_id=1, source_target_pairs={{0,2},{1,3},{2,0},{3,1},{4,6},{5,7},{6,4},{7,5},{8,10},{9,11},{10,... | collective-permute-start | bytes 98312 | tf_op jit(solution)/shard_map/ppermute | solution.py:320
  20.2 1.2 %collective-permute-done.3.refs_3_ = bf16[32,256]{1,0:T(8,128)(2,1)S(1)} collective-permute-done((bf16[32,256]{1,0:T(8,128)(2,1)S(1)}, bf16[32,256]{1,0:T(8,128)(2,1)S(1)}, u32[]{:S(2)}, u32[]{:S(2)}) %collective-permute-start.3) | collective-permute-done | bytes 16416 | tf_op jit(solution)/shard_map/ppermute | solution.py:313
  21.3 2.5 %collective-permute-start.14 = (bf16[8,2048]{1,0:T(8,128)(2,1)}, bf16[8,2048]{1,0:T(8,128)(2,1)S(1)}, u32[]{:S(2)}, u32[]{:S(2)}) collective-permute-start(bf16[8,2048]{1,0:T(8,128)(2,1)} %refs_0_), channel_id=1, source_target_pairs={{0,3},{1,0},{2,1},{3,2},{4,7},{5,4},{6,5},{7,6},{8,11},{9,8},{10,9... | collective-permute-start | bytes 98312 | tf_op jit(solution)/shard_map/ppermute | solution.py:320
  23.8 5.3 %shard_map.105 = (f32[32,1536]{1,0:T(8,128)S(1)}, bf16[32,1536]{1,0:T(8,128)(2,1)S(1)}, f32[8,1536]{1,0:T(8,128)S(1)}, f32[8,32]{1,0:T(8,128)S(1)}, bf16[32,256]...) custom-call(bf16[32,256]{1,0:T(8,128)(2,1)S(1)} %collective-permute-, ...), custom_call_target="tpu_custom_call" | custom-call | flops 16777216 | bytes 16777216 | tf_op jit(solution)/shard_map/pallas_call | solution.py:63
  29.2 4.0 %collective-permute-start.6 = (bf16[32,256]{1,0:T(8,128)(2,1)S(1)}, bf16[32,256]{1,0:T(8,128)(2,1)S(1)}, u32[]{:S(2)}, u32[]{:S(2)}) collective-permute-start(bf16[32,256]{1,0:T(8,128)(2,1)S(1)} %get-tuple-element.52), channel_id=1, source_target_pairs={{0,236},{4,240},{8,244},{12,248},{16,252},{20,0},{24,4},{28,8},{32... | collective-permute-start | bytes 49160 | tf_op jit(solution)/shard_map/ppermute | solution.py:313
  33.1 1.1 %collective-permute-start.7 = (bf16[32,256]{1,0:T(8,128)(2,1)S(1)}, bf16[32,256]{1,0:T(8,128)(2,1)S(1)}, u32[]{:S(2)}, u32[]{:S(2)}) collective-permute-start(bf16[32,256]{1,0:T(8,128)(2,1)S(1)} %get-tuple-element.53), channel_id=1, source_target_pairs={{0,248},{4,252},{8,0},{12,4},{16,8},{20,12},{24,16},{28,20},{32,24... | collective-permute-start | bytes 49160 | tf_op jit(solution)/shard_map/ppermute | solution.py:313
  34.2 2.0 %collective-permute-start.9 = (bf16[32,256]{1,0:T(8,128)(2,1)S(1)}, bf16[32,256]{1,0:T(8,128)(2,1)S(1)}, u32[]{:S(2)}, u32[]{:S(2)}) collective-permute-start(bf16[32,256]{1,0:T(8,128)(2,1)S(1)} %get-tuple-element.55), channel_id=1, source_target_pairs={{0,20},{4,24},{8,28},{12,32},{16,36},{20,40},{24,44},{28,48},{32,5... | collective-permute-start | bytes 49160 | tf_op jit(solution)/shard_map/ppermute | solution.py:313
  36.7 1.0 %shard_map.107 = (bf16[64,8,128]{2,1,0:T(8,128)(2,1)S(1)}, bf16[32,1536]{1,0:T(8,128)(2,1)S(1)}, f32[24,32]{1,0:T(8,128)S(1)}) custom-call(bf16[8,2048]{1,0:T(8,128)(2,1)S(1)} %copy-done, bf16[8,2048]{1,0:T(8,128)(2,1)S(1)} %collective-permute-done.12.refs_1_, bf16[8,2048]{1,0:T(8,128)(2,1)S(1)} %collective-permute-done.13.refs_2_, ...), custom_call_target="tpu_custom_call" | custom-call | flops 2097152 | bytes 2097152 | tf_op jit(solution)/shard_map/pallas_call | solution.py:63
  37.7 3.4 %collective-permute-done.9.refs_3_ = bf16[32,256]{1,0:T(8,128)(2,1)S(1)} collective-permute-done((bf16[32,256]{1,0:T(8,128)(2,1)S(1)}, bf16[32,256]{1,0:T(8,128)(2,1)S(1)}, u32[]{:S(2)}, u32[]{:S(2)}) %collective-permute-start.9) | collective-permute-done | bytes 16416 | tf_op jit(solution)/shard_map/ppermute | solution.py:313
  43.0 5.1 %all-to-all-start = ((bf16[64,8,256]{2,1,0:T(8,128)(2,1)}), bf16[64,8,256]{2,1,0:T(8,128)(2,1)S(1)}, u32[]{:S(2)}, u32[]{:S(2)}) async-start(bf16[64,8,256]{2,1,0:T(8,128)(2,1)} %shard_map.108), calls=%async_computation | async-start | bytes 524288 | tf_op jit(solution)/shard_map/all_to_all | solution.py:395
  48.1 5.0 %shard_map.106 = (f32[32,1536]{1,0:T(8,128)S(1)}, f32[32,1536]{1,0:T(8,128)S(1)}, f32[32,1536]{1,0:T(8,128)S(1)}, f32[8,128]{1,0:T(8,128)S(1)}) custom-call(bf16[32,256]{1,0:T(8,128)(2,1)S(1)} %collective-permute-done.6.refs_0_, bf16[32,256]{1,0:T(8,128)(2,1)S(1)} %collective-permute-done.7.refs_1_, bf16[32,256]{1,0:T(8,128)(2,1)S(1)} %collective-permute-done.8.refs_2_, ...), custom_call_target="tpu_custom_call" | custom-call | flops 8388608 | bytes 8388608 | tf_op jit(solution)/shard_map/pallas_call | solution.py:63
  53.2 8.2 %all-to-all-done.sent_ref = bf16[64,8,256]{2,1,0:T(8,128)(2,1)S(1)} async-done(((bf16[64,8,256]{2,1,0:T(8,128)(2,1)}), bf16[64,8,256]{2,1,0:T(8,128)(2,1)S(1)}, u32[]{:S(2)}, u32[]{:S(2)}) %all-to-all-start) | async-done | bytes 262176 | tf_op jit(solution)/shard_map/all_to_all | solution.py:395
  61.4 1.3 %shard_map.109 = (bf16[512,128]{1,0:T(8,128)(2,1)S(1)}, f32[16,128]{1,0:T(8,128)S(1)}) custom-call(bf16[64,8,256]{2,1,0:T(8,128)(2,1)S(1)} %all-to-all-done.sent_ref, f32[8,128]{1,0:T(8,128)S(1)} %get-tuple-element.70.scalars_ref), custom_call_target="tpu_custom_call" | custom-call | flops 4194304 | bytes 4194304 | tf_op jit(solution)/shard_map/pallas_call | solution.py:63
  64.2 1.0 %collective-permute-done.17.three_ref = f32[16,128]{1,0:T(8,128)S(1)} collective-permute-done((f32[16,128]{1,0:T(8,128)S(1)}, f32[16,128]{1,0:T(8,128)S(1)}, u32[]{:S(2)}, u32[]{:S(2)}) %collective-permute-start.17) | collective-permute-done | bytes 8224 | tf_op jit(solution)/shard_map/ppermute | solution.py:320
  65.3 1.6 %collective-permute-done.16.two_ref = f32[16,128]{1,0:T(8,128)S(1)} collective-permute-done((f32[16,128]{1,0:T(8,128)S(1)}, f32[16,128]{1,0:T(8,128)S(1)}, u32[]{:S(2)}, u32[]{:S(2)}) %collective-permute-start.16) | collective-permute-done | bytes 8224 | tf_op jit(solution)/shard_map/ppermute | solution.py:320
  66.9 1.0 %collective-permute-done.15.one_ref = f32[16,128]{1,0:T(8,128)S(1)} collective-permute-done((f32[16,128]{1,0:T(8,128)S(1)}, f32[16,128]{1,0:T(8,128)S(1)}, u32[]{:S(2)}, u32[]{:S(2)}) %collective-permute-start.15) | collective-permute-done | bytes 8224 | tf_op jit(solution)/shard_map/ppermute | solution.py:320
  68.2 16.8 %all_to_all.10.coarse_ref = bf16[64,8,128]{2,1,0:T(8,128)(2,1)S(1)} all-to-all(bf16[64,8,128]{2,1,0:T(8,128)(2,1)S(1)} %shard_map.110), channel_id=1, replica_groups=mesh['sub'=64,'grp'=4] {'sub'}, dimensions={0} | all-to-all | bytes 262144 | tf_op jit(solution)/shard_map/all_to_all | solution.py:427
  86.3 1.9 %collective-permute-start.19 = (bf16[32,256]{1,0:T(8,128)(2,1)S(1)}, bf16[32,256]{1,0:T(8,128)(2,1)S(1)}, u32[]{:S(2)}, u32[]{:S(2)}) collective-permute-start(bf16[32,256]{1,0:T(8,128)(2,1)S(1)} %get-tuple-element.77), channel_id=1, source_target_pairs={{0,248},{4,252},{8,0},{12,4},{16,8},{20,12},{24,16},{28,20},{32,24... | collective-permute-start | bytes 49160 | tf_op jit(solution)/shard_map/ppermute | solution.py:313
  89.8 1.9 %collective-permute-start.22 = (bf16[32,256]{1,0:T(8,128)(2,1)S(1)}, bf16[32,256]{1,0:T(8,128)(2,1)S(1)}, u32[]{:S(2)}, u32[]{:S(2)}) collective-permute-start(bf16[32,256]{1,0:T(8,128)(2,1)S(1)} %get-tuple-element.80), channel_id=1, source_target_pairs={{0,8},{4,12},{8,16},{12,20},{16,24},{20,28},{24,32},{28,36},{32,40... | collective-permute-start | bytes 49160 | tf_op jit(solution)/shard_map/ppermute | solution.py:313
  91.7 1.3 %collective-permute-start.23 = (bf16[32,256]{1,0:T(8,128)(2,1)S(1)}, bf16[32,256]{1,0:T(8,128)(2,1)S(1)}, u32[]{:S(2)}, u32[]{:S(2)}) collective-permute-start(bf16[32,256]{1,0:T(8,128)(2,1)S(1)} %get-tuple-element.81), channel_id=1, source_target_pairs={{0,4},{4,8},{8,12},{12,16},{16,20},{20,24},{24,28},{28,32},{32,36}... | collective-permute-start | bytes 49160 | tf_op jit(solution)/shard_map/ppermute | solution.py:313
  93.0 2.9 %collective-permute-done.21.refs_3_ = bf16[32,256]{1,0:T(8,128)(2,1)S(1)} collective-permute-done((bf16[32,256]{1,0:T(8,128)(2,1)S(1)}, bf16[32,256]{1,0:T(8,128)(2,1)S(1)}, u32[]{:S(2)}, u32[]{:S(2)}) %collective-permute-start.21) | collective-permute-done | bytes 16416 | tf_op jit(solution)/shard_map/ppermute | solution.py:313
  95.9 1.7 %shard_map.112 = (f32[32,1536]{1,0:T(8,128)}, f32[32,1536]{1,0:T(8,128)}) custom-call(bf16[32,256]{1,0:T(8,128)(2,1)S(1)} %collective-permute-done.18.refs_0_, bf16[32,256]{1,0:T(8,128)(2,1)S(1)} %collective-permute-done.19.refs_1_, bf16[32,256]{1,0:T(8,128)(2,1)S(1)} %collective-permute-done.20.refs_2_, ...), custom_call_target="tpu_custom_call" | custom-call | flops 8388608 | bytes 8388608 | tf_op jit(solution)/shard_map/pallas_call | solution.py:63
  (43 shorter events, 12.2 us)
Async XLA Ops:
  4.0 12.4 %collective-permute-start = (bf16[32,256]{1,0:T(8,128)(2,1)S(1)}, bf16[32,256]{1,0:T(8,128)(2,1)S(1)}, u32[]{:S(2)}, u32[]{:S(2)}) collective-permute-start(bf16[32,256]{1,0:T(8,128)(2,1)S(1)} %get-tuple-element.45), channel_id=1, source_target_pairs={{0,236},{4,240},{8,244},{12,248},{16,252},{20,0},{24,4},{28,8},{32... | collective-permute-start | bytes 49160 | tf_op jit(solution)/shard_map/ppermute | solution.py:313
  13.6 3.5 %collective-permute-start.1 = (bf16[32,256]{1,0:T(8,128)(2,1)S(1)}, bf16[32,256]{1,0:T(8,128)(2,1)S(1)}, u32[]{:S(2)}, u32[]{:S(2)}) collective-permute-start(bf16[32,256]{1,0:T(8,128)(2,1)S(1)} %get-tuple-element.46), channel_id=1, source_target_pairs={{0,248},{4,252},{8,0},{12,4},{16,8},{20,12},{24,16},{28,20},{32,24... | collective-permute-start | bytes 49160 | tf_op jit(solution)/shard_map/ppermute | solution.py:313
  14.4 5.5 %collective-permute-start.2 = (bf16[32,256]{1,0:T(8,128)(2,1)S(1)}, bf16[32,256]{1,0:T(8,128)(2,1)S(1)}, u32[]{:S(2)}, u32[]{:S(2)}) collective-permute-start(bf16[32,256]{1,0:T(8,128)(2,1)S(1)} %get-tuple-element.47), channel_id=1, source_target_pairs={{0,252},{4,0},{8,4},{12,8},{16,12},{20,16},{24,20},{28,24},{32,28}... | collective-permute-start | bytes 49160 | tf_op jit(solution)/shard_map/ppermute | solution.py:313
  14.4 6.9 %collective-permute-start.3 = (bf16[32,256]{1,0:T(8,128)(2,1)S(1)}, bf16[32,256]{1,0:T(8,128)(2,1)S(1)}, u32[]{:S(2)}, u32[]{:S(2)}) collective-permute-start(bf16[32,256]{1,0:T(8,128)(2,1)S(1)} %get-tuple-element.48), channel_id=1, source_target_pairs={{0,20},{4,24},{8,28},{12,32},{16,36},{20,40},{24,44},{28,48},{32,5... | collective-permute-start | bytes 49160 | tf_op jit(solution)/shard_map/ppermute | solution.py:313
  16.3 7.5 %collective-permute-start.4 = (bf16[32,256]{1,0:T(8,128)(2,1)S(1)}, bf16[32,256]{1,0:T(8,128)(2,1)S(1)}, u32[]{:S(2)}, u32[]{:S(2)}) collective-permute-start(bf16[32,256]{1,0:T(8,128)(2,1)S(1)} %get-tuple-element.49), channel_id=1, source_target_pairs={{0,8},{4,12},{8,16},{12,20},{16,24},{20,28},{24,32},{28,36},{32,40... | collective-permute-start | bytes 49160 | tf_op jit(solution)/shard_map/ppermute | solution.py:313
  16.3 7.4 %collective-permute-start.5 = (bf16[32,256]{1,0:T(8,128)(2,1)S(1)}, bf16[32,256]{1,0:T(8,128)(2,1)S(1)}, u32[]{:S(2)}, u32[]{:S(2)}) collective-permute-start(bf16[32,256]{1,0:T(8,128)(2,1)S(1)} %get-tuple-element.50), channel_id=1, source_target_pairs={{0,4},{4,8},{8,12},{12,16},{16,20},{20,24},{24,28},{28,32},{32,36}... | collective-permute-start | bytes 49160 | tf_op jit(solution)/shard_map/ppermute | solution.py:313
  17.1 17.1 %collective-permute-start.13 = (bf16[8,2048]{1,0:T(8,128)(2,1)}, bf16[8,2048]{1,0:T(8,128)(2,1)S(1)}, u32[]{:S(2)}, u32[]{:S(2)}) collective-permute-start(bf16[8,2048]{1,0:T(8,128)(2,1)} %refs_0_), channel_id=1, source_target_pairs={{0,2},{1,3},{2,0},{3,1},{4,6},{5,7},{6,4},{7,5},{8,10},{9,11},{10,... | collective-permute-start | bytes 98312 | tf_op jit(solution)/shard_map/ppermute | solution.py:320
  19.8 14.4 %collective-permute-start.12 = (bf16[8,2048]{1,0:T(8,128)(2,1)}, bf16[8,2048]{1,0:T(8,128)(2,1)S(1)}, u32[]{:S(2)}, u32[]{:S(2)}) collective-permute-start(bf16[8,2048]{1,0:T(8,128)(2,1)} %refs_0_), channel_id=1, source_target_pairs={{0,1},{1,2},{2,3},{3,0},{4,5},{5,6},{6,7},{7,4},{8,9},{9,10},{10,1... | collective-permute-start | bytes 98312 | tf_op jit(solution)/shard_map/ppermute | solution.py:320
  21.3 14.9 %collective-permute-start.14 = (bf16[8,2048]{1,0:T(8,128)(2,1)}, bf16[8,2048]{1,0:T(8,128)(2,1)S(1)}, u32[]{:S(2)}, u32[]{:S(2)}) collective-permute-start(bf16[8,2048]{1,0:T(8,128)(2,1)} %refs_0_), channel_id=1, source_target_pairs={{0,3},{1,0},{2,1},{3,2},{4,7},{5,4},{6,5},{7,6},{8,11},{9,8},{10,9... | collective-permute-start | bytes 98312 | tf_op jit(solution)/shard_map/ppermute | solution.py:320
  29.2 7.0 %collective-permute-start.6 = (bf16[32,256]{1,0:T(8,128)(2,1)S(1)}, bf16[32,256]{1,0:T(8,128)(2,1)S(1)}, u32[]{:S(2)}, u32[]{:S(2)}) collective-permute-start(bf16[32,256]{1,0:T(8,128)(2,1)S(1)} %get-tuple-element.52), channel_id=1, source_target_pairs={{0,236},{4,240},{8,244},{12,248},{16,252},{20,0},{24,4},{28,8},{32... | collective-permute-start | bytes 49160 | tf_op jit(solution)/shard_map/ppermute | solution.py:313
  33.1 4.6 %collective-permute-start.7 = (bf16[32,256]{1,0:T(8,128)(2,1)S(1)}, bf16[32,256]{1,0:T(8,128)(2,1)S(1)}, u32[]{:S(2)}, u32[]{:S(2)}) collective-permute-start(bf16[32,256]{1,0:T(8,128)(2,1)S(1)} %get-tuple-element.53), channel_id=1, source_target_pairs={{0,248},{4,252},{8,0},{12,4},{16,8},{20,12},{24,16},{28,20},{32,24... | collective-permute-start | bytes 49160 | tf_op jit(solution)/shard_map/ppermute | solution.py:313
  34.2 3.5 %collective-permute-start.8 = (bf16[32,256]{1,0:T(8,128)(2,1)S(1)}, bf16[32,256]{1,0:T(8,128)(2,1)S(1)}, u32[]{:S(2)}, u32[]{:S(2)}) collective-permute-start(bf16[32,256]{1,0:T(8,128)(2,1)S(1)} %get-tuple-element.54), channel_id=1, source_target_pairs={{0,252},{4,0},{8,4},{12,8},{16,12},{20,16},{24,20},{28,24},{32,28}... | collective-permute-start | bytes 49160 | tf_op jit(solution)/shard_map/ppermute | solution.py:313
  34.2 6.9 %collective-permute-start.9 = (bf16[32,256]{1,0:T(8,128)(2,1)S(1)}, bf16[32,256]{1,0:T(8,128)(2,1)S(1)}, u32[]{:S(2)}, u32[]{:S(2)}) collective-permute-start(bf16[32,256]{1,0:T(8,128)(2,1)S(1)} %get-tuple-element.55), channel_id=1, source_target_pairs={{0,20},{4,24},{8,28},{12,32},{16,36},{20,40},{24,44},{28,48},{32,5... | collective-permute-start | bytes 49160 | tf_op jit(solution)/shard_map/ppermute | solution.py:313
  36.2 5.9 %collective-permute-start.10 = (bf16[32,256]{1,0:T(8,128)(2,1)S(1)}, bf16[32,256]{1,0:T(8,128)(2,1)S(1)}, u32[]{:S(2)}, u32[]{:S(2)}) collective-permute-start(bf16[32,256]{1,0:T(8,128)(2,1)S(1)} %get-tuple-element.56), channel_id=1, source_target_pairs={{0,8},{4,12},{8,16},{12,20},{16,24},{20,28},{24,32},{28,36},{32,40... | collective-permute-start | bytes 49160 | tf_op jit(solution)/shard_map/ppermute | solution.py:313
  36.2 5.9 %collective-permute-start.11 = (bf16[32,256]{1,0:T(8,128)(2,1)S(1)}, bf16[32,256]{1,0:T(8,128)(2,1)S(1)}, u32[]{:S(2)}, u32[]{:S(2)}) collective-permute-start(bf16[32,256]{1,0:T(8,128)(2,1)S(1)} %get-tuple-element.57), channel_id=1, source_target_pairs={{0,4},{4,8},{8,12},{12,16},{16,20},{20,24},{24,28},{28,32},{32,36}... | collective-permute-start | bytes 49160 | tf_op jit(solution)/shard_map/ppermute | solution.py:313
  43.0 18.4 %all-to-all-start = ((bf16[64,8,256]{2,1,0:T(8,128)(2,1)}), bf16[64,8,256]{2,1,0:T(8,128)(2,1)S(1)}, u32[]{:S(2)}, u32[]{:S(2)}) async-start(bf16[64,8,256]{2,1,0:T(8,128)(2,1)} %shard_map.108), calls=%async_computation | async-start | bytes 524288 | tf_op jit(solution)/shard_map/all_to_all | solution.py:395
  62.8 4.1 %collective-permute-start.16 = (f32[16,128]{1,0:T(8,128)S(1)}, f32[16,128]{1,0:T(8,128)S(1)}, u32[]{:S(2)}, u32[]{:S(2)}) collective-permute-start(f32[16,128]{1,0:T(8,128)S(1)} %get-tuple-element.72.own_ref), channel_id=1, source_target_pairs={{0,2},{1,3},{2,0},{3,1},{4,6},{5,7},{6,4},{7,5},{8,10},{9,11},{10,... | collective-permute-start | bytes 24584 | tf_op jit(solution)/shard_map/ppermute | solution.py:320
  63.7 4.3 %collective-permute-start.15 = (f32[16,128]{1,0:T(8,128)S(1)}, f32[16,128]{1,0:T(8,128)S(1)}, u32[]{:S(2)}, u32[]{:S(2)}) collective-permute-start(f32[16,128]{1,0:T(8,128)S(1)} %get-tuple-element.72.own_ref), channel_id=1, source_target_pairs={{0,1},{1,2},{2,3},{3,0},{4,5},{5,6},{6,7},{7,4},{8,9},{9,10},{10,1... | collective-permute-start | bytes 24584 | tf_op jit(solution)/shard_map/ppermute | solution.py:320
  85.4 6.3 %collective-permute-start.18 = (bf16[32,256]{1,0:T(8,128)(2,1)S(1)}, bf16[32,256]{1,0:T(8,128)(2,1)S(1)}, u32[]{:S(2)}, u32[]{:S(2)}) collective-permute-start(bf16[32,256]{1,0:T(8,128)(2,1)S(1)} %get-tuple-element.76), channel_id=1, source_target_pairs={{0,236},{4,240},{8,244},{12,248},{16,252},{20,0},{24,4},{28,8},{32... | collective-permute-start | bytes 49160 | tf_op jit(solution)/shard_map/ppermute | solution.py:313
  86.3 6.6 %collective-permute-start.19 = (bf16[32,256]{1,0:T(8,128)(2,1)S(1)}, bf16[32,256]{1,0:T(8,128)(2,1)S(1)}, u32[]{:S(2)}, u32[]{:S(2)}) collective-permute-start(bf16[32,256]{1,0:T(8,128)(2,1)S(1)} %get-tuple-element.77), channel_id=1, source_target_pairs={{0,248},{4,252},{8,0},{12,4},{16,8},{20,12},{24,16},{28,20},{32,24... | collective-permute-start | bytes 49160 | tf_op jit(solution)/shard_map/ppermute | solution.py:313
  88.3 4.7 %collective-permute-start.20 = (bf16[32,256]{1,0:T(8,128)(2,1)S(1)}, bf16[32,256]{1,0:T(8,128)(2,1)S(1)}, u32[]{:S(2)}, u32[]{:S(2)}) collective-permute-start(bf16[32,256]{1,0:T(8,128)(2,1)S(1)} %get-tuple-element.78), channel_id=1, source_target_pairs={{0,252},{4,0},{8,4},{12,8},{16,12},{20,16},{24,20},{28,24},{32,28}... | collective-permute-start | bytes 49160 | tf_op jit(solution)/shard_map/ppermute | solution.py:313
  89.0 6.8 %collective-permute-start.21 = (bf16[32,256]{1,0:T(8,128)(2,1)S(1)}, bf16[32,256]{1,0:T(8,128)(2,1)S(1)}, u32[]{:S(2)}, u32[]{:S(2)}) collective-permute-start(bf16[32,256]{1,0:T(8,128)(2,1)S(1)} %get-tuple-element.79), channel_id=1, source_target_pairs={{0,20},{4,24},{8,28},{12,32},{16,36},{20,40},{24,44},{28,48},{32,5... | collective-permute-start | bytes 49160 | tf_op jit(solution)/shard_map/ppermute | solution.py:313
  89.8 6.1 %collective-permute-start.22 = (bf16[32,256]{1,0:T(8,128)(2,1)S(1)}, bf16[32,256]{1,0:T(8,128)(2,1)S(1)}, u32[]{:S(2)}, u32[]{:S(2)}) collective-permute-start(bf16[32,256]{1,0:T(8,128)(2,1)S(1)} %get-tuple-element.80), channel_id=1, source_target_pairs={{0,8},{4,12},{8,16},{12,20},{16,24},{20,28},{24,32},{28,36},{32,40... | collective-permute-start | bytes 49160 | tf_op jit(solution)/shard_map/ppermute | solution.py:313
  91.7 4.2 %collective-permute-start.23 = (bf16[32,256]{1,0:T(8,128)(2,1)S(1)}, bf16[32,256]{1,0:T(8,128)(2,1)S(1)}, u32[]{:S(2)}, u32[]{:S(2)}) collective-permute-start(bf16[32,256]{1,0:T(8,128)(2,1)S(1)} %get-tuple-element.81), channel_id=1, source_target_pairs={{0,4},{4,8},{8,12},{12,16},{16,20},{20,24},{24,28},{28,32},{32,36}... | collective-permute-start | bytes 49160 | tf_op jit(solution)/shard_map/ppermute | solution.py:313
  (3 other events, 80.1 us)
